TPU v7x, 32 devices: a whole 2x2x4 slice. The times are simulated.
32 devices in a mesh: wide: 8 (over z, y), narrow: 4 (over x, core).
Axes of the slice: x: 2, y: 2, z: 4, core: 2. Of those that a mesh axis runs over, the one named last changes fastest.
Arguments:
- layer_in: bfloat16 [128, 2048, 768], P(('wide', 'narrow')), may hold values from -6 to 6
- lengths: int32 [128], P(('wide', 'narrow')), may hold values from 1024 to 2048, as said below
- padding: int32 [128, 2048], P(('wide', 'narrow')), may hold values from 0 to 1, as said below
- picked: int32 [128, 256], P(('wide', 'narrow')), may hold values from 0 to 2047, as said below
- first_gain: bfloat16 [768], P(('wide', 'narrow')), may hold values from 0.5 to 1.5
- project_in: bfloat16 [768, 2304], P(('wide', 'narrow')), may hold values from -0.21875 to 0.21875
- project_out: bfloat16 [768, 768], P(None, ('wide', 'narrow')), may hold values from -0.875 to 0.875
- second_gain: bfloat16 [768], P(('wide', 'narrow')), may hold values from 0.5 to 1.5
- up_weight: bfloat16 [768, 3072], P(('wide', 'narrow')), may hold values from -0.21875 to 0.21875
- up_bias: bfloat16 [3072], P(('wide', 'narrow')), may hold values from -3 to 3
- down_weight: bfloat16 [3072, 768], P(None, ('wide', 'narrow')), may hold values from -0.109375 to 0.109375
- down_bias: bfloat16 [768], P(('wide', 'narrow')), may hold values from -3 to 3
- router: bfloat16 [768], P(('wide', 'narrow')), may hold values from -0.21875 to 0.21875
- cotangent: bfloat16 [128, 2048, 768], P(('wide', 'narrow')), may hold values from -6 to 6
Outputs:
- layer_out: bfloat16 [128, 2048, 768], P(('wide', 'narrow'))
- input_grad: bfloat16 [128, 2048, 768], P(('wide', 'narrow'))
- first_gain_grad: float32 [768], P(('wide', 'narrow'))
- project_in_grad: float32 [768, 2304], P(('wide', 'narrow'))
- project_out_grad: float32 [768, 768], P(None, ('wide', 'narrow'))
- second_gain_grad: float32 [768], P(('wide', 'narrow'))
- up_weight_grad: float32 [768, 3072], P(('wide', 'narrow'))
- up_bias_grad: float32 [3072], P(('wide', 'narrow'))
- down_weight_grad: float32 [3072, 768], P(None, ('wide', 'narrow'))
- down_bias_grad: float32 [768], P(('wide', 'narrow'))
- router_grad: float32 [768], P(('wide', 'narrow'))
Inputs may be any that keep to these rules, and one draw needn't show every extreme that they name: `lengths`: each sequence's true token count; one sequence has exactly 2048, one exactly 1024. `padding`: row b is 1 on one contiguous run of lengths[b] positions and 0 elsewhere. `picked`: the first lengths[b] // 8 entries of row b are strictly increasing positions at which padding is 1; the other entries are 0.
All inputs are finite; a program needn't handle non-finite values.
Results may differ from a plain program's by a relative error of at most 0.01.
Values may be sent and summed in bfloat16 or wider, within the bound.
No kernel may reach another device: no remote copies, remote signals or barrier semaphores. Data moves between devices by JAX's collectives and lax.ppermute only.
A program may use at most 256 MiB of HBM per device.

v0:
```python
from functools import partial

import jax
import jax.numpy as jnp
import numpy as np
from jax import lax
from jax.experimental import pallas as pl
from jax.experimental.pallas import tpu as pltpu
from jax.sharding import PartitionSpec as P

HEAD_DIM = 64
EPSILON = 1e-06
NEG_FILL = -1e30
F32 = jnp.float32
BF16 = jnp.bfloat16
AXES = ("wide", "narrow")
SCALE = HEAD_DIM**-0.5
GELU_A = 0.7978845608028654
GELU_B = 0.044715
LSE_LANE = 16
MLP_CHUNKS = 4
PAIRS = 3
PLACE_ROWS = 512
ANY = pl.BlockSpec(memory_space=pl.ANY)
VMEM_LIMIT = 67043328


def dot(left, right, left_dim=1, right_dim=0):
    return lax.dot_general(
        left, right, (((left_dim,), (right_dim,)), ((), ())), preferred_element_type=F32
    )


def params(*semantics):
    return pltpu.CompilerParams(
        dimension_semantics=semantics or None, vmem_limit_bytes=VMEM_LIMIT
    )


def whole(shape):
    return pl.BlockSpec(shape, lambda *_: (0,) * len(shape))


def cost(flops, bytes_accessed):
    return pl.CostEstimate(
        flops=int(flops), bytes_accessed=int(bytes_accessed), transcendentals=0
    )


class Layout:
    def __init__(self, height, plane, blocks):
        self.height, self.plane, self.blocks = height, plane, tuple(blocks)
        self.pieces = 1 + max(piece for piece, *_ in blocks)
        self.depth = len(blocks) // plane

    def natural(self, here, step, line):
        return pl.multiple_of((line * self.plane + (here ^ step)) * self.height, 8)


def load_rows(layout, here, pieces, target, sems, source, columns):
    height = layout.height
    return [
        pltpu.make_async_copy(
            pieces[piece].at[pl.ds(at * height, height), source],
            target.at[pl.ds(layout.natural(here, step, line), height), columns],
            sems.at[j],
        )
        for j, (piece, at, step, line) in enumerate(layout.blocks)
    ]


def both_halves(layout, here, own, oth, target, sems, start, count):
    source = pl.ds(start, count)
    return load_rows(layout, here, own, target, sems.at[0], source, pl.ds(0, count)) + load_rows(
        layout, here, oth, target, sems.at[1], source, pl.ds(count, count)
    )


def store_rows(layout, here, target, value):
    height = layout.height
    for line in range(layout.depth):
        for owner in range(layout.plane):
            start = pl.multiple_of(((owner ^ here) * layout.depth + line) * height, 8)
            c = line * layout.plane + owner
            target[pl.ds(start, height), :] = value[c * height : (c + 1) * height, :]


def gather_kernel(target, x, cot, sel, grad):
    length = x.shape[1]
    places = lax.broadcasted_iota(jnp.int32, (target.shape[1], length), 1)
    chosen = jnp.where(target[0] == places, 1.0, 0.0).astype(BF16)
    sel[...] = dot(chosen, x[0]).astype(BF16)
    grad[...] = dot(chosen, cot[0]).astype(BF16)


def gather_rows(target, layer_in, cotangent):
    seqs, length, width = layer_in.shape
    slots = target.shape[1]
    big = pl.BlockSpec((1, length, width), lambda b: (b, 0, 0))
    out = pl.BlockSpec((slots, width), lambda b: (b, 0))
    return pl.pallas_call(
        gather_kernel,
        grid=(seqs,),
        in_specs=[pl.BlockSpec((1, slots, 1), lambda b: (b, 0, 0)), big, big],
        out_specs=[out, out],
        out_shape=[jax.ShapeDtypeStruct((seqs * slots, width), BF16)] * 2,
        compiler_params=params("arbitrary"),
        cost_estimate=cost(
            4 * seqs * slots * length * width, 4 * seqs * length * width
        ),
        name="gather_rows",
    )(target, layer_in, cotangent)


def allowed_keys(slots, valid):
    rows = lax.broadcasted_iota(jnp.int32, (2 * slots, slots), 0)
    rows = jnp.where(rows >= slots, rows - slots, rows)
    keys = lax.broadcasted_iota(jnp.int32, (2 * slots, slots), 1)
    return (keys <= rows) & (keys < valid)


def split_pair(pair):
    lane = lax.broadcasted_iota(jnp.int32, pair.shape, 1)
    zero = jnp.zeros_like(pair)
    first = lane < HEAD_DIM
    return jnp.concatenate(
        [jnp.where(first, pair, zero), jnp.where(first, zero, pair)], axis=0
    )


def join_pair(stacked):
    half = stacked.shape[0] // 2
    lane = lax.broadcasted_iota(jnp.int32, (half, stacked.shape[1]), 1)
    return jnp.where(lane < HEAD_DIM, stacked[:half], stacked[half:])


def pair_loop(pairs, body, carry):
    def step(k, carry):
        for p in range(PAIRS):
            carry = body(k * PAIRS + p, carry)
        return carry

    return lax.fori_loop(0, pairs // PAIRS, step, carry)


def pair_columns(pair, half_width):
    per_half = half_width // (2 * HEAD_DIM)
    base = (pair // per_half) * 3 * half_width + (pair % per_half) * 2 * HEAD_DIM
    return tuple(
        pl.ds(pl.multiple_of(base + k * half_width, 128), 2 * HEAD_DIM) for k in range(3)
    )


def forward_kernel(
    where, counts, sel, grad, *rest, layout, half, third
):
    own, oth = rest[: layout.pieces], rest[layout.pieces : 2 * layout.pieces]
    (
    qkv, att, mid, n2, n2t, g, gt, n1t, stats, vec, bias, gsum,
    w_in, w_out, w_ext, sem_in, sem_out, sem_ext,
    ) = rest[2 * layout.pieces :]
    b = pl.program_id(0)
    slots, width = sel.shape
    here = where[0]

    def in_copies():
        return both_halves(layout, here, own, oth, w_in, sem_in, 0, half)

    def out_copies():
        return both_halves(layout, here, own, oth, w_out, sem_out, half, third)

    @pl.when(b == 0)
    def _():
        small = both_halves(layout, here, own, oth, w_ext, sem_ext, half + third, 128)
        first = in_copies()
        for c in small + first + out_copies():
            c.start()
        for c in small:
            c.wait()
        per = width // 128
        high = 4 * per
        total = sum(w_ext[k * high : (k + 1) * high, :].astype(F32) for k in range(width // high))
        mine, others = total[:, :128], total[:, 128:]
        vectors = jnp.where(where[1] == 0, mine, others)
        biases = jnp.where(where[1] == 0, others, mine)
        vec[...] = jnp.zeros_like(vec)
        for v in range(4):
            for k in range(per):
                vec[v : v + 1, k * 128 : (k + 1) * 128] = vectors[v * per + k : v * per + k + 1, :]
        for k in range(bias.shape[1] // 128):
            bias[0:1, k * 128 : (k + 1) * 128] = biases[k : k + 1, :]
        for c in first:
            c.wait()

    x = sel[...].astype(F32)
    r1 = lax.rsqrt(jnp.mean(x * x, axis=-1, keepdims=True) + EPSILON)
    n1 = (x * r1 * vec[0:1, :]).astype(BF16)
    logit = jnp.sum(x * vec[3:4, :], axis=-1, keepdims=True)
    rate = jax.nn.sigmoid(logit)
    d_mlp = (rate * grad[...].astype(F32)).astype(BF16)
    g[...] = d_mlp
    gsum_now = jnp.sum(d_mlp.astype(F32), axis=0, keepdims=True)

    @pl.when(b == 0)
    def _():
        gsum[...] = gsum_now

    @pl.when(b > 0)
    def _():
        gsum[...] += gsum_now

    store_rows(layout, here, gt, d_mlp.T)
    store_rows(layout, here, n1t, n1.T)
    qkv[...] = dot(n1, w_in[...]).astype(BF16)

    allowed = allowed_keys(slots, counts[b])
    lane = lax.broadcasted_iota(jnp.int32, (slots, 128), 1)
    kept = jnp.where(lane == 0, r1, jnp.where(lane == 1, rate, 0.0))

    def attend(pair, kept):
        qc, kc, vc = pair_columns(pair, width // 2)
        scores = dot(split_pair(qkv[:, qc] * SCALE), qkv[:, kc], 1, 1)
        scores = jnp.where(allowed, scores, NEG_FILL)
        top = jnp.max(scores, axis=-1, keepdims=True)
        exps = jnp.exp(scores - top)
        total = jnp.sum(exps, axis=-1, keepdims=True)
        lse = top + jnp.log(total)
        probs = (exps * (1.0 / total)).astype(BF16)
        here_now = pl.ds(pl.multiple_of(pair * 128, 128), 128)
        att[:, here_now] = join_pair(dot(probs, qkv[:, vc])).astype(BF16)
        kept = jnp.where(lane == LSE_LANE + 2 * pair, lse[:slots], kept)
        return jnp.where(lane == LSE_LANE + 2 * pair + 1, lse[slots:], kept)

    kept = pair_loop(width // (2 * HEAD_DIM), attend, kept)

    @pl.when(b == 0)
    def _():
        for c in out_copies():
            c.wait()

    stream = x + dot(att[...], w_out[...], 1, 1)
    mid[...] = stream
    r2 = lax.rsqrt(jnp.mean(stream * stream, axis=-1, keepdims=True) + EPSILON)
    normed = (stream * r2 * vec[1:2, :]).astype(BF16)
    n2[...] = normed
    store_rows(layout, here, n2t, normed.T)
    stats[...] = jnp.where(lane == 2, r2, kept)


def forward_block(layout, hidden, where, counts, sel, grad, own, oth):
    rows, width = sel.shape
    seqs = counts.shape[0]
    slots = rows // seqs
    blocks = len(layout.blocks)
    row = lambda w: pl.BlockSpec((slots, w), lambda b, *_: (b, 0))
    col = pl.BlockSpec((width, slots), lambda b, *_: (0, b))
    shape = jax.ShapeDtypeStruct
    return pl.pallas_call(
        partial(forward_kernel, layout=layout, half=3 * width // 2, third=width // 2),
        grid_spec=pltpu.PrefetchScalarGridSpec(
            num_scalar_prefetch=2,
            grid=(seqs,),
            in_specs=[row(width), row(width)] + [ANY] * (2 * layout.pieces),
            out_specs=[
                row(3 * width), row(width), row(width), row(width), col, row(width), col, col, row(128),
                whole((8, width)), whole((1, hidden)), whole((1, width)),
            ],
            scratch_shapes=[
                pltpu.VMEM((width, 3 * width), BF16),
                pltpu.VMEM((width, width), BF16),
                pltpu.VMEM((width, 256), BF16),
                pltpu.SemaphoreType.DMA((2, blocks)),
                pltpu.SemaphoreType.DMA((2, blocks)),
                pltpu.SemaphoreType.DMA((2, blocks)),
            ],
        ),
        out_shape=[
            shape((rows, 3 * width), BF16),
            shape((rows, width), BF16),
            shape((rows, width), F32),
            shape((rows, width), BF16),
            shape((width, rows), BF16),
            shape((rows, width), BF16),
            shape((width, rows), BF16),
            shape((width, rows), BF16),
            shape((rows, 128), F32),
            shape((8, width), F32),
            shape((1, hidden), F32),
            shape((1, width), F32),
        ],
        compiler_params=params("arbitrary"),
        cost_estimate=cost(10 * rows * width * width, 30 * rows * width),
        name="forward_block",
    )(where, counts, sel, grad, *own, *oth)


def mlp_kernel(where, bias, *rest, layout, tile):
    rows_in = rest[:4]
    own, oth = rest[4 : 4 + layout.pieces], rest[4 + layout.pieces : 4 + 2 * layout.pieces]
    mlp, dn2, d_own, d_oth, dbias, *held, w_up, w_down, d_first, act, d_pre, sem_rows, sems, sem_out = rest[
        4 + 2 * layout.pieces :
    ]
    n2, n2t, g, gt = held
    i = pl.program_id(0)
    here = where[0]
    row_copies = [
        pltpu.make_async_copy(rows_in[k], held[k], sem_rows.at[k]) for k in range(4)
    ]
    out_copy = pltpu.make_async_copy(d_first, d_own, sem_out)

    def copies(side, kind):
        source, target = (own, oth)[side], (w_up, w_down)[kind].at[side]
        return load_rows(
            layout, here, source, target, sems.at[side, kind], pl.ds(kind * tile, tile), pl.ds(0, tile)
        )

    def wait_first(*waited):
        @pl.when(i == 0)
        def _():
            for c in waited:
                c.wait()

    @pl.when(i == 0)
    def _():
        started = copies(0, 0) + row_copies[:1] + copies(0, 1) + row_copies[2:3]
        started = started + row_copies[1:2] + row_copies[3:] + copies(1, 0) + copies(1, 1)
        for c in started:
            c.start()

    wait_first(*copies(0, 0), row_copies[0])

    @pl.when(i == 1)
    def _():
        out_copy.start()
        for c in copies(1, 0) + copies(1, 1):
            c.wait()

    wait_first(*copies(0, 1), row_copies[2])
    up_now = w_up.at[i]
    down_now = w_down.at[i]
    rows = n2.shape[0] // MLP_CHUNKS

    def chunk(c, total):
        here = pl.ds(pl.multiple_of(c * rows, rows), rows)
        pre = dot(n2[here, :], up_now[...]) + bias[...]
        square = pre * pre
        th = jnp.tanh(pre * (GELU_A + GELU_A * GELU_B * square))
        half = 0.5 * (1.0 + th)
        act_now = (pre * half).astype(BF16)
        act[here, :] = act_now
        slope = half + 0.5 * pre * (1.0 - th * th) * (GELU_A + 3 * GELU_A * GELU_B * square)
        d_pre_now = (slope * dot(g[here, :], down_now[...])).astype(BF16)
        d_pre[here, :] = d_pre_now
        mlp[here, :] = jnp.where(i == 0, 0.0, mlp[here, :]) + dot(act_now, down_now[...], 1, 1)
        dn2[here, :] = jnp.where(i == 0, 0.0, dn2[here, :]) + dot(d_pre_now, up_now[...], 1, 1)
        return total + jnp.sum(d_pre_now.astype(F32), axis=0, keepdims=True)

    dbias[...] = lax.fori_loop(0, MLP_CHUNKS, chunk, jnp.zeros_like(dbias))
    wait_first(row_copies[1], row_copies[3])
    dup = dot(n2t[...], d_pre[...]).astype(BF16)
    ddown = dot(gt[...], act[...]).astype(BF16)

    @pl.when(i == 0)
    def _():
        d_first[:, :tile] = dup
        d_first[:, tile:] = ddown

    @pl.when(i == 1)
    def _():
        d_oth[:, :tile] = dup
        d_oth[:, tile:] = ddown
        out_copy.wait()


def mlp_part(layout, where, part, tile, n2, n2t, g, gt, own, oth, bias):
    rows, width = n2.shape
    parts = bias.shape[1] // (2 * tile)
    blocks = len(layout.blocks)
    shape = jax.ShapeDtypeStruct
    return pl.pallas_call(
        partial(mlp_kernel, layout=layout, tile=tile),
        grid_spec=pltpu.PrefetchScalarGridSpec(
            num_scalar_prefetch=1,
            grid=(2,),
            in_specs=[
                pl.BlockSpec((1, tile), lambda i, where: (0, (where[1] ^ i) * parts + part)),
            ] + [ANY] * (4 + 2 * layout.pieces),
            out_specs=[
                whole((rows, width)), whole((rows, width)), ANY, whole((width, 2 * tile)),
                pl.BlockSpec((1, tile), lambda i, where: (0, i)),
            ],
            scratch_shapes=[
                pltpu.VMEM((rows, width), BF16),
                pltpu.VMEM((width, rows), BF16),
                pltpu.VMEM((rows, width), BF16),
                pltpu.VMEM((width, rows), BF16),
                pltpu.VMEM((2, width, tile), BF16),
                pltpu.VMEM((2, width, tile), BF16),
                pltpu.VMEM((width, 2 * tile), BF16),
                pltpu.VMEM((rows, tile), BF16),
                pltpu.VMEM((rows, tile), BF16),
                pltpu.SemaphoreType.DMA((4,)),
                pltpu.SemaphoreType.DMA((2, 2, blocks)),
                pltpu.SemaphoreType.DMA,
            ],
        ),
        out_shape=[
            shape((rows, width), F32),
            shape((rows, width), F32),
            shape((width, 2 * tile), BF16),
            shape((width, 2 * tile), BF16),
            shape((1, 2 * tile), F32),
        ],
        compiler_params=params("arbitrary"),
        cost_estimate=cost(24 * rows * width * tile, 8 * rows * width),
        name="mlp_part",
    )(where, bias, n2, n2t, g, gt, *own, *oth)


def norm_pull(values, inverse, scaled):
    return inverse * scaled - values * (
        inverse * inverse * inverse * jnp.mean(scaled * values, axis=-1, keepdims=True)
    )


def backward_kernel(
    where, counts, sel, grad, vec, qkv, mid, stats, mlp, mlp_two, dn2, dn2_two, *rest, layout, half, third
):
    own, oth = rest[: layout.pieces], rest[layout.pieces : 2 * layout.pieces]
    dqkv, dattnt, dmid, new_rows, drouter, w_out, d_att, sem_out = rest[2 * layout.pieces :]
    b = pl.program_id(0)
    slots, width = sel.shape
    here = where[0]

    @pl.when(b == 0)
    def _():
        copies = both_halves(layout, here, own, oth, w_out, sem_out, half, third)
        for c in copies:
            c.start()
        for c in copies:
            c.wait()

    x = sel[...].astype(F32)
    stream = mid[...]
    rate = stats[:, 1:2]
    r2 = stats[:, 2:3]
    slot_grad = grad[...].astype(F32)
    branch = (stream - x) + ((mlp[...] + mlp_two[...]) + vec[2:3, :])
    new_rows[...] = (x + rate * branch).astype(BF16)
    d_logit = jnp.sum(slot_grad * branch, axis=-1, keepdims=True) * (rate * (1.0 - rate))
    router_now = jnp.sum(d_logit * x, axis=0, keepdims=True)

    @pl.when(b == 0)
    def _():
        drouter[...] = router_now

    @pl.when(b > 0)
    def _():
        drouter[...] += router_now

    d_mid = norm_pull(stream, r2, vec[1:2, :] * (dn2[...] + dn2_two[...]))
    dmid[...] = d_mid + d_logit * vec[3:4, :]
    d_attn = (rate * slot_grad + d_mid).astype(BF16)
    store_rows(layout, here, dattnt, d_attn.T)
    d_att[...] = dot(d_attn, w_out[...]).astype(BF16)

    allowed = allowed_keys(slots, counts[b])
    lane = lax.broadcasted_iota(jnp.int32, (slots, 128), 1)

    def pull(pair, carry):
        qc, kc, vc = pair_columns(pair, width // 2)
        queries = split_pair(qkv[:, qc] * SCALE)
        keys = qkv[:, kc]
        lse = jnp.concatenate(
            [
                jnp.sum(jnp.where(lane == LSE_LANE + 2 * pair + k, stats[...], 0.0), axis=-1, keepdims=True)
                for k in (0, 1)
            ],
            axis=0,
        )
        upstream = split_pair(d_att[:, pl.ds(pl.multiple_of(pair * 128, 128), 128)])
        scores = dot(queries, keys, 1, 1)
        probs = jnp.exp(jnp.where(allowed, scores - lse, NEG_FILL))
        d_probs = dot(upstream, qkv[:, vc], 1, 1)
        d_scores = (probs * (d_probs - jnp.sum(probs * d_probs, axis=-1, keepdims=True))).astype(BF16)
        dqkv[:, qc] = (join_pair(dot(d_scores, keys)) * SCALE).astype(BF16)
        dqkv[:, kc] = dot(d_scores, queries, 0, 0).astype(BF16)
        dqkv[:, vc] = dot(probs.astype(BF16), upstream, 0, 0).astype(BF16)
        return carry

    pair_loop(width // (2 * HEAD_DIM), pull, 0)


def backward_block(layout, where, counts, sel, grad, vec, qkv, mid, stats, sums, own, oth):
    rows, width = sel.shape
    seqs = counts.shape[0]
    slots = rows // seqs
    blocks = len(layout.blocks)
    row = lambda w: pl.BlockSpec((slots, w), lambda b, *_: (b, 0))
    col = pl.BlockSpec((width, slots), lambda b, *_: (0, b))
    shape = jax.ShapeDtypeStruct
    return pl.pallas_call(
        partial(backward_kernel, layout=layout, half=3 * width // 2, third=width // 2),
        grid_spec=pltpu.PrefetchScalarGridSpec(
            num_scalar_prefetch=2,
            grid=(seqs,),
            in_specs=[
                row(width), row(width), whole(vec.shape), row(3 * width), row(width), row(128),
            ] + [row(width)] * 4 + [ANY] * (2 * layout.pieces),
            out_specs=[row(3 * width), col, row(width), row(width), whole((1, width))],
            scratch_shapes=[
                pltpu.VMEM((width, width), BF16),
                pltpu.VMEM((slots, width), BF16),
                pltpu.SemaphoreType.DMA((2, blocks)),
            ],
        ),
        out_shape=[
            shape((rows, 3 * width), BF16),
            shape((width, rows), BF16),
            shape((rows, width), F32),
            shape((rows, width), BF16),
            shape((1, width), F32),
        ],
        compiler_params=params("arbitrary"),
        cost_estimate=cost(20 * rows * width * width, 30 * rows * width),
        name="backward_block",
    )(where, counts, sel, grad, vec, qkv, mid, stats, *sums, *own, *oth)


def project_kernel(where, n1t, dattnt, dqkv, att, dbias_one, dbias_two, ddown, drouter, oth, own):
    half = dqkv.shape[1]
    third = att.shape[1]
    width = n1t.shape[0]
    high, tile = 4 * width // 128, dbias_one.shape[1] // 2
    in_now = dot(n1t[...], dqkv[...]).astype(BF16)
    out_now = dot(dattnt[...], att[...]).astype(BF16)
    first_core = where[1] == 0

    def bias_rows():
        rows = []
        for side in (0, 1):
            for part in (dbias_one, dbias_two):
                for k in range(tile // 128):
                    a, b = side * tile + k * 128, (1 - side) * tile + k * 128
                    rows.append(jnp.where(first_core, part[:, a : a + 128], part[:, b : b + 128]))
        return rows

    def vector_rows():
        rows = [v[:, k * 128 : (k + 1) * 128] for v in (ddown, drouter) for k in range(width // 128)]
        return rows + [jnp.zeros((1, 128), F32)] * (high - len(rows))

    def store(out, is_first):
        out[:, :half] = in_now
        out[:, half : half + third] = out_now
        small = jnp.where(
            is_first, jnp.concatenate(bias_rows(), axis=0), jnp.concatenate(vector_rows(), axis=0)
        )
        small = jnp.concatenate([small] * 2, axis=0).astype(BF16)
        for k in range(width // (2 * high)):
            out[2 * k * high : 2 * (k + 1) * high, half + third :] = small

    pl.when(pl.program_id(0) == 0)(lambda: store(oth, where[1] == 1))
    pl.when(pl.program_id(0) == 1)(lambda: store(own, where[1] == 0))


def project_grads(where, n1t, dattnt, dqkv, att, *vectors):
    width, rows = n1t.shape
    half, third = dqkv.shape[1] // 2, att.shape[1] // 2
    total = half + third + 128
    return pl.pallas_call(
        project_kernel,
        grid_spec=pltpu.PrefetchScalarGridSpec(
            num_scalar_prefetch=1,
            grid=(2,),
            in_specs=[
                whole((width, rows)), whole((width, rows)),
                pl.BlockSpec((rows, half), lambda i, where: (0, 1 - i)),
                pl.BlockSpec((rows, third), lambda i, where: (0, 1 - i)),
            ] + [whole(v.shape) for v in vectors],
            out_specs=[whole((width, total))] * 2,
        ),
        out_shape=[jax.ShapeDtypeStruct((width, total), BF16)] * 2,
        compiler_params=params("arbitrary"),
        cost_estimate=cost(4 * width * rows * total, 2 * (2 * width * rows + rows * total + width * total)),
        name="project_grads",
    )(where, n1t, dattnt, dqkv, att, *vectors)


def place(out, rows, target, x, start, count):
    chunk = min(PLACE_ROWS, x.shape[1])

    def one(c, carry):
        here = pl.ds(pl.multiple_of(c * chunk, chunk), chunk)
        places = lax.broadcasted_iota(jnp.int32, (chunk, target.shape[2]), 0) + c * chunk
        hits = target[0] == places
        moved = dot(jnp.where(hits, 1.0, 0.0).astype(BF16), rows[...])
        hit = jnp.max(jnp.where(hits, 1.0, 0.0), axis=-1, keepdims=True)
        at = lax.broadcasted_iota(jnp.int32, (chunk, 1), 0) + c * chunk
        kept = (at >= start) & (at < start + count) & (hit < 0.5)
        out[0, here, :] = jnp.where(kept, x[0, here, :].astype(F32), moved).astype(BF16)
        return carry

    lax.fori_loop(0, x.shape[1] // chunk, one, 0)


def out_kernel(runs, rows, target, x, out):
    b = pl.program_id(0)
    place(out, rows, target, x, runs[0, b], runs[1, b])


def place_rows(runs, rows, target, x):
    seqs, length, width = x.shape
    slots = target.shape[2]
    big = pl.BlockSpec((1, length, width), lambda b, *_: (b, 0, 0))
    return pl.pallas_call(
        out_kernel,
        grid_spec=pltpu.PrefetchScalarGridSpec(
            num_scalar_prefetch=1,
            grid=(seqs,),
            in_specs=[
                pl.BlockSpec((slots, width), lambda b, *_: (b, 0)),
                pl.BlockSpec((1, 1, slots), lambda b, *_: (b, 0, 0)),
                big,
            ],
            out_specs=big,
        ),
        out_shape=jax.ShapeDtypeStruct(x.shape, BF16),
        compiler_params=params("arbitrary"),
        cost_estimate=cost(2 * seqs * slots * length * width, 4 * seqs * length * width),
        name="place_rows",
    )(runs, rows, target, x)


def input_kernel(
    where, runs, sel, grad, vec, stats, dmid, dqkv, target, x, *rest, layout, first
):
    own, oth = rest[: layout.pieces], rest[layout.pieces : 2 * layout.pieces]
    *_, out, w_in, moved, sem_in = rest[2 * layout.pieces :]
    b = pl.program_id(0)

    @pl.when(b == 0)
    def _():
        copies = both_halves(layout, where[0], own, oth, w_in, sem_in, 0, w_in.shape[1] // 2)
        for c in copies:
            c.start()
        for c in copies:
            c.wait()

    d_normed = dot(dqkv[...], w_in[...], 1, 1)
    d_sel = norm_pull(sel[...].astype(F32), stats[:, 0:1], vec[0:1, :] * d_normed) + dmid[...]
    moved[...] = (grad[...].astype(F32) + d_sel).astype(BF16)
    place(out, moved, target, x, runs[0, first + b], runs[1, first + b])


def input_rows(layout, where, runs, sel, grad, vec, stats, dmid, dqkv, target, x, own, oth, first, count, begun=()):
    seqs, length, width = x.shape
    slots = target.shape[2]
    blocks = len(layout.blocks)
    row = lambda w: pl.BlockSpec((slots, w), lambda b, *_: (first + b, 0))
    big = pl.BlockSpec((1, length, width), lambda b, *_: (first + b, 0, 0))
    return pl.pallas_call(
        partial(input_kernel, layout=layout, first=first),
        grid_spec=pltpu.PrefetchScalarGridSpec(
            num_scalar_prefetch=2,
            grid=(count,),
            in_specs=[
                row(width), row(width), whole(vec.shape), row(128), row(width), row(3 * width),
                pl.BlockSpec((1, 1, slots), lambda b, *_: (first + b, 0, 0)),
                big,
            ] + [ANY] * (2 * layout.pieces + len(begun)),
            out_specs=big,
            scratch_shapes=[
                pltpu.VMEM((width, 3 * width), BF16),
                pltpu.VMEM((slots, width), BF16),
                pltpu.SemaphoreType.DMA((2, blocks)),
            ],
        ),
        out_shape=jax.ShapeDtypeStruct(x.shape, BF16),
        compiler_params=params("arbitrary"),
        cost_estimate=cost(8 * seqs * slots * length * width, 4 * seqs * length * width),
        input_output_aliases={10 + 2 * layout.pieces: 0} if begun else {},
        name="input_rows",
    )(where, runs, sel, grad, vec, stats, dmid, dqkv, target, x, *own, *oth, *begun)


class Paths:
    def __init__(self, wide, narrow):
        self.wide, self.narrow, self.depth = wide, narrow, wide // 2
        ids = np.arange(wide * narrow).reshape(self.depth, 4, 2)
        self.lines = ids.transpose(1, 0, 2).reshape(4, -1).tolist()

    def swap(self, value):
        return lax.ppermute(value, "narrow", [(i, i ^ 1) for i in range(self.narrow)])

    def over(self, value, step):
        if step == 1:
            return lax.ppermute(value, "narrow", [(i, i ^ 2) for i in range(self.narrow)])
        if step == 2:
            return lax.ppermute(value, "wide", [(i, i ^ 1) for i in range(self.wide)])
        mask = self.narrow ^ 2
        return lax.ppermute(value, AXES, [(i, i ^ mask) for i in range(self.wide * self.narrow)])

    def along(self, value):
        return lax.all_to_all(value, AXES, 0, 0, axis_index_groups=self.lines, tiled=True)

    def to_line(self, halves):
        shard, cols = halves[0].shape
        sent = jnp.broadcast_to(jnp.stack(halves)[None], (self.depth, 2, shard, cols))
        return sent.reshape(self.depth * 2 * shard, cols)

    def gather_halved(self, held):
        near_x, near_y = self.over(held, 1), self.over(held, 2)
        mid = held.shape[0] // 2
        return [held, near_x, near_y, self.over(near_y[:mid], 1), self.over(near_x[mid:], 2)]

    def gather_direct(self, held):
        return [held] + [self.over(held, step) for step in (1, 2, 3)]

    def swap_all(self, pieces):
        return [self.swap(p) for p in pieces]

    def chip_sums(self, own, got):
        rows = own.shape[0] // 4
        return [
            add_halves(own[step * rows : (step + 1) * rows], got[step * rows : (step + 1) * rows])
            for step in range(4)
        ]

    def send_plane(self, sums):
        return [self.over(sums[step], step) for step in (1, 2, 3)]

    def sum_plane(self, mine, got):
        total = mine.astype(F32)
        for v in got:
            total = total + v.astype(F32)
        return total.astype(BF16)

    def sum_line(self, got):
        return jnp.sum(got.reshape(self.depth, 2, -1, got.shape[1]).astype(F32), axis=0)


def halved(depth):
    return [(piece, z, piece, z) for piece in range(3) for z in range(depth)] + [
        (3 + (z >= depth // 2), z % (depth // 2), 3, z) for z in range(depth)
    ]


def direct(depth):
    return [(piece, z, piece, z) for piece in range(4) for z in range(depth)]


def add_halves(own, got):
    return (own.astype(F32) + got.astype(F32)).astype(BF16)


def tie(*values):
    return lax.optimization_barrier(values)


def per_device(
    layer_in,
    lengths,
    padding,
    picked,
    first_gain,
    project_in,
    project_out,
    second_gain,
    up_weight,
    up_bias,
    down_weight,
    down_bias,
    router,
    cotangent,
    *,
    wide,
    narrow,
):
    seqs, slots = picked.shape
    shard, in_width = project_in.shape
    width = in_width // 3
    hidden = up_weight.shape[1]
    devices = wide * narrow
    half = 3 * width // 2
    third = width // 2
    tile = hidden // 4
    fast = shard == 24 and wide % 4 == 0 and narrow == 4
    core = lax.axis_index("narrow") & 1 if fast else jnp.int32(0)
    device = lax.axis_index("wide") * narrow + lax.axis_index("narrow")

    in_split = project_in.reshape(shard, 3, 2, third)
    in_halves = [in_split[:, :, side].reshape(shard, half) for side in (0, 1)]
    out_t = project_out.T
    down_t = down_weight.T
    vectors = jnp.stack([first_gain, second_gain, down_bias, router])

    first = [
        jnp.concatenate([in_halves[side], out_t[:, side * third : (side + 1) * third]], axis=1)
        for side in (0, 1)
    ]

    def rest_of(side, part):
        at = (2 * side + part) * tile
        return jnp.concatenate([up_weight[:, at : at + tile], down_t[:, at : at + tile]], axis=1)

    def places(lengths):
        counts = lengths // 8
        valid = jnp.arange(slots)[None, :] < counts[:, None]
        target = jnp.where(valid, picked, -1)
        runs = jnp.stack([jnp.argmax(padding, axis=1).astype(jnp.int32), lengths])
        return counts, runs, target[:, :, None], target[:, None, :]

    if fast:
        paths = Paths(wide, narrow)
        here = (lax.axis_index("wide") & 1) * 2 + (lax.axis_index("narrow") >> 1)
        lay_one = Layout(2 * shard, 4, halved(paths.depth))
        lay_two = Layout(2 * shard, 4, direct(paths.depth))
        placed = lax.dynamic_update_slice(
            jnp.zeros((4, width), BF16), vectors, (0, device * shard)
        ).reshape(shard, 128)
        biases = lax.dynamic_update_slice(
            jnp.zeros((hidden,), BF16), up_bias, (device * 4 * shard,)
        ).reshape(shard, 128)
        sent = paths.to_line(
            [
                jnp.concatenate([first[0], placed], axis=1),
                jnp.concatenate([first[1], biases], axis=1),
            ]
        )
        sent, lengths = tie(sent, lengths)
        line = paths.along(sent)
        counts, runs, columns, target_row = places(lengths)
        sel, slot_grad = gather_rows(columns, layer_in, cotangent)
        rest = paths.to_line(
            [jnp.concatenate([rest_of(side, 0), rest_of(side, 1)], axis=1) for side in (0, 1)]
        )
        line, rest, sel, slot_grad, runs, target_row = tie(line, rest, sel, slot_grad, runs, target_row)
        own = paths.gather_halved(line)
        oth = paths.swap_all(own)
        rest = paths.along(rest)
        own, oth, rest, sel = tie(own, oth, rest, sel)
        one_own = paths.gather_direct(rest[:, : 2 * tile])
        two_own = paths.gather_direct(rest[:, 2 * tile :])
    else:
        counts, runs, columns, target_row = places(lengths)
        here = jnp.int32(0)
        lay_one = lay_two = Layout(width, 1, [(0, 0, 0, 0)])
        packed = jnp.concatenate(
            first + [rest_of(side, part) for part in (0, 1) for side in (0, 1)], axis=1
        )
        full = lax.all_gather(packed, AXES, axis=0, tiled=True)
        cuts = [0]
        for n in (half + third,) * 2 + (2 * tile,) * 4:
            cuts.append(cuts[-1] + n)
        own, oth, one_own, one_oth, two_own, two_oth = (
            [full[:, a:b]] for a, b in zip(cuts, cuts[1:])
        )
        every = lax.all_gather(vectors, AXES, axis=1, tiled=True).reshape(-1, 128)
        biases = lax.all_gather(up_bias, AXES, axis=0, tiled=True).reshape(-1, 128)
        own, oth = (
            [jnp.concatenate([p[0], jnp.pad(v, ((0, width - v.shape[0]), (0, 0)))], axis=1)]
            for p, v in ((own, every), (oth, biases))
        )
        sel, slot_grad = gather_rows(columns, layer_in, cotangent)

    where = jnp.stack([here, core]).astype(jnp.int32)
    qkv, att, mid, n2, n2t, g, gt, n1t, stats, vec, bias, ddown_bias = forward_block(
        lay_one, hidden, where, counts, sel, slot_grad, own, oth
    )
    if fast:
        one_own, n2 = tie(one_own, n2)
        one_oth = paths.swap_all(one_own)
    mlp, dn2, d_one_own, d_one_oth, dbias_one = mlp_part(
        lay_two, where, 0, tile, n2, n2t, g, gt, one_own, one_oth, bias
    )
    if fast:
        two_own, mlp, n2 = tie(two_own, mlp, n2)
        two_oth = paths.swap_all(two_own)
        d_one_got = paths.swap(d_one_oth)
    mlp_two, dn2_two, d_two_own, d_two_oth, dbias_two = mlp_part(
        lay_two, where, 1, tile, n2, n2t, g, gt, two_own, two_oth, bias
    )
    if fast:
        d_two_got = paths.swap(d_two_oth)
        d_one_got, mlp_two = tie(d_one_got, mlp_two)
        d_one = paths.chip_sums(d_one_own, d_one_got)
        d_one_plane = paths.send_plane(d_one)
        d_two = paths.chip_sums(d_two_own, d_two_got)
        _, d_two, mlp_two = tie(d_one, d_two, mlp_two)
        d_two_plane = paths.send_plane(d_two)
    dqkv, dattnt, dmid, new_rows, drouter = backward_block(
        lay_one, where, counts, sel, slot_grad, vec, qkv, mid, stats, (mlp, mlp_two, dn2, dn2_two), own, oth
    )
    if fast:
        d_one_plane, dqkv = tie(d_one_plane, dqkv)

    if fast:
        one = paths.sum_plane(d_one[0], d_one_plane)
        one, new_rows = tie(one, new_rows)
        one = paths.along(one)
    layer_out = place_rows(runs, new_rows, target_row, layer_in)
    if fast:
        dqkv, layer_out = tie(dqkv, layer_out)
    proj_oth, proj_own = project_grads(
        where, n1t, dattnt, dqkv, att, dbias_one, dbias_two, ddown_bias, drouter
    )
    if fast:
        one, d_two_plane, proj_oth = tie(one, d_two_plane, proj_oth)
        proj = paths.chip_sums(proj_own, paths.swap(proj_oth))
        two = paths.sum_plane(d_two[0], d_two_plane)
        two, proj, dmid = tie(two, proj, dmid)
        proj_plane = paths.send_plane(proj)
        two = paths.along(two)
    part = seqs // 2
    input_grad = input_rows(
        lay_one, where, runs, sel, slot_grad, vec, stats, dmid, dqkv, target_row, cotangent, own, oth, 0, part
    )
    if fast:
        proj = paths.sum_plane(proj[0], proj_plane)
        two, proj, dmid, input_grad = tie(two, proj, dmid, input_grad)
    input_grad = input_rows(
        lay_one, where, runs, sel, slot_grad, vec, stats, dmid, dqkv, target_row, cotangent, own, oth,
        part, seqs - part, (input_grad,),
    )

    if fast:
        one, two = paths.sum_line(one), paths.sum_line(two)
        proj = paths.sum_line(paths.along(proj))
    else:
        flat = jnp.concatenate(
            [d_one_own, d_one_oth, d_two_own, d_two_oth, proj_own, proj_oth], axis=1
        )
        total = lax.psum_scatter(flat.astype(F32), AXES, scatter_dimension=0, tiled=True)
        p = proj_own.shape[1]
        one = total[:, : 4 * tile].reshape(shard, 2, 2 * tile).transpose(1, 0, 2)
        two = total[:, 4 * tile : 8 * tile].reshape(shard, 2, 2 * tile).transpose(1, 0, 2)
        proj = total[:, 8 * tile :].reshape(shard, 2, p).transpose(1, 0, 2)

    up_grad = jnp.concatenate(
        [v[side, :, :tile] for side in (0, 1) for v in (one, two)], axis=1
    )
    down_grad = jnp.concatenate(
        [v[side, :, tile:] for side in (0, 1) for v in (one, two)], axis=1
    ).T
    in_grad = jnp.stack(
        [proj[side, :, :half].reshape(shard, 3, third) for side in (0, 1)], axis=2
    ).reshape(shard, in_width)
    out_grad = jnp.concatenate([proj[side, :, half : half + third] for side in (0, 1)], axis=1).T
    if fast:
        every, vectors = proj[0, :, half + third :], proj[1, :, half + third :]
    else:
        high = 4 * width // 128
        mine = proj_own[:high, half + third :], proj_oth[:high, half + third :]
        every, vectors = lax.psum(tuple(v.astype(F32) for v in mine), AXES)
    d_up_bias = lax.dynamic_slice(every.reshape(-1), (device * 4 * shard,), (4 * shard,))
    vectors = vectors.reshape(4, width)
    d_down_bias, d_router = (
        lax.dynamic_slice(vectors[k], (device * shard,), (shard,)) for k in (0, 1)
    )
    gain_one = jnp.sum(project_in.astype(F32) * in_grad, axis=1) / first_gain.astype(F32)
    gain_two = jnp.sum(up_weight.astype(F32) * up_grad, axis=1) / second_gain.astype(F32)
    return (
        layer_out,
        input_grad,
        gain_one,
        in_grad,
        out_grad,
        gain_two,
        up_grad,
        d_up_bias,
        down_grad,
        d_down_bias,
        d_router,
    )


def solution(mesh):
    both = ("wide", "narrow")
    rows3, rows2, rows1, cols = P(both, None, None), P(both, None), P(both), P(None, both)
    in_specs = (
        rows3, rows1, rows2, rows2, rows1, rows2, cols, rows1, rows2, rows1, cols, rows1, rows1, rows3,
    )
    out_specs = (rows3, rows3, rows1, rows2, cols, rows1, rows2, rows1, cols, rows1, rows1)
    return jax.shard_map(
        partial(per_device, wide=mesh.shape["wide"], narrow=mesh.shape["narrow"]),
        mesh=mesh,
        in_specs=in_specs,
        out_specs=out_specs,
        check_vma=False,
    )
```

profile of v0, /device:TPU:0, one launch (start us, length us, event | category | flops | bytes accessed | tf_op | source)
XLA Modules:
  0.0 307.1 jit_solution(9348774387392093540)
XLA Ops:
  5.7 6.4 %all-to-all-start = ((bf16[8,24,1664]{2,1,0:T(8,128)(2,1)}), bf16[8,24,1664]{2,1,0:T(8,128)(2,1)}, u32[]{:S(2)}, u32[]{:S(2)}) async-start(bf16[8,24,1664]{2,1,0:T(8,128)(2,1)} %bitcast.11), calls=%async_computation | async-start | bytes 1277952 | tf_op jit(solution)/shard_map/all_to_all | solution.py:704
  16.1 12.6 %gather_rows.1 = (bf16[1024,768]{1,0:T(8,128)(2,1)}, bf16[1024,768]{1,0:T(8,128)(2,1)}) custom-call(s32[4,256,1]{2,1,0:T(8,128)} %copy.33.target, bf16[4,2048,768]{2,1,0:T(8,128)(2,1)} %x.5, bf16[4,2048,768]{2,1,0:T(8,128)(2,1)} %x.7), custom_call_target="tpu_custom_call" | custom-call | flops 6442450944 | bytes 25165824 | tf_op jit(solution)/shard_map/gather_rows/pallas_call | solution.py:101
  28.7 1.4 all-to-all-done
  30.1 2.1 broadcast_in_dim.33
  32.2 3.7 %all-to-all-start.1 = ((bf16[8,24,3072]{2,1,0:T(8,128)(2,1)}), bf16[8,24,3072]{2,1,0:T(8,128)(2,1)S(1)}, u32[]{:S(2)}, u32[]{:S(2)}) async-start(bf16[8,24,3072]{2,1,0:T(8,128)(2,1)} %bitcast.20), calls=%async_computation.1 | async-start | bytes 2359296 | tf_op jit(solution)/shard_map/all_to_all | solution.py:704
  35.9 1.6 collective-permute-start.1
  37.5 1.5 collective-permute-start
  39.0 13.9 %collective-permute-done.1.rest_2_ = bf16[192,1664]{1,0:T(8,128)(2,1)S(1)} collective-permute-done((bf16[192,1664]{1,0:T(8,128)(2,1)}, bf16[192,1664]{1,0:T(8,128)(2,1)S(1)}, u32[]{:S(2)}, u32[]{:S(2)}) %collective-permute-start.1) | collective-permute-done | bytes 639008 | tf_op jit(solution)/shard_map/ppermute | solution.py:699
  52.9 1.6 collective-permute-start.2
  54.5 1.6 collective-permute-start.3
  56.6 5.3 %collective-permute-done.2.rest_3_ = bf16[96,1664]{1,0:T(8,128)(2,1)S(1)} collective-permute-done((bf16[96,1664]{1,0:T(8,128)(2,1)S(1)}, bf16[96,1664]{1,0:T(8,128)(2,1)S(1)}, u32[]{:S(2)}, u32[]{:S(2)}) %collective-permute-start.2) | collective-permute-done | bytes 319520 | tf_op jit(solution)/shard_map/ppermute | solution.py:697
  61.9 1.4 collective-permute-done.3.rest_4_
  63.7 1.6 collective-permute-done.8.rest_9_
  65.3 1.1 fusion.1
  66.5 1.6 collective-permute-start.10
  68.0 1.4 collective-permute-start.11
  70.6 25.4 %forward_block.1 = (bf16[1024,2304]{1,0:T(8,128)(2,1)}, bf16[1024,768]{1,0:T(8,128)(2,1)}, f32[1024,768]{1,0:T(8,128)}, bf16[1024,768]{1,0:T(8,128)(2,1)}, bf16[...) custom-call(s32[2]{0:T(128)} %pad_add_fusion.1.where, ...), custom_call_target="tpu_custom_call" | custom-call | flops 6039797760 | bytes 23592960 | tf_op jit(solution)/shard_map/forward_block/pallas_call | solution.py:258
  97.1 1.4 collective-permute-start.17
  98.5 1.5 collective-permute-start.18
  100.1 1.6 collective-permute-start.19
  101.7 26.9 %mlp_part.2 = (f32[1024,768]{1,0:T(8,128)}, f32[1024,768]{1,0:T(8,128)}, bf16[768,1536]{1,0:T(8,128)(2,1)}, bf16[768,1536]{1,0:T(8,128)(2,1)}, f32[1,1536]{1,0:T(1,128)}) custom-call(s32[2]{0:T(128)} %pad_add_fusion.1.where, f32[1,3072]{1,0:T(1,128)} %get-tuple-element.124.bias, bf16[1024,768]{1,0:T(8,128)(2,1)} %get-tuple-element.138.rest_0_, ...), custom_call_target="tpu_custom_call" | custom-call | flops 14495514624 | bytes 6291456 | tf_op jit(solution)/shard_map/mlp_part/pallas_call | solution.py:380
  129.8 1.2 collective-permute-done.20.rest_8_
  133.5 27.0 %mlp_part.3 = (f32[1024,768]{1,0:T(8,128)}, f32[1024,768]{1,0:T(8,128)}, bf16[768,1536]{1,0:T(8,128)(2,1)}, bf16[768,1536]{1,0:T(8,128)(2,1)}, f32[1,1536]{1,0:T(1,128)}) custom-call(s32[2]{0:T(128)} %pad_add_fusion.1.where, f32[1,3072]{1,0:T(1,128)} %get-tuple-element.124.bias, bf16[1024,768]{1,0:T(8,128)(2,1)} %get-tuple-element.138.rest_0_, ...), custom_call_target="tpu_custom_call" | custom-call | flops 14495514624 | bytes 6291456 | tf_op jit(solution)/shard_map/mlp_part/pallas_call | solution.py:380
  160.8 4.3 %add_convert_fusion.11 = (bf16[192,1536]{1,0:T(8,128)(2,1)}, bf16[192,1536]{1,0:T(8,128)(2,1)}, bf16[192,1536]{1,0:T(8,128)(2,1)}, bf16[192,1536]{1,0:T(8,128)(2,1)}) fusion(bf16[768,1536]{1,0:T(8,128)(2,1)} %collective-permute-done.16, bf16[768,1536]{1,0:T(8,128)(2,1)} %get-tuple-element.135), kind=kLoop, calls=%fused_computation.14 | loop fusion | flops 4718592 | bytes 7077888 | tf_op jit(solution)/shard_map/convert_element_type | solution.py:753
  165.8 1.5 collective-permute-start.25
  167.3 1.2 collective-permute-start.26
  168.5 1.8 add_convert_fusion.7
  170.4 28.6 %backward_block.1 = (bf16[1024,2304]{1,0:T(8,128)(2,1)}, bf16[768,1024]{1,0:T(8,128)(2,1)}, f32[1024,768]{1,0:T(8,128)}, bf16[1024,768]{1,0:T(8,128)(2,1)}, f32[1,768]{1,0:T(1,128)}) custom-call(s32[2]{0:T(128)} %pad_add_fusion.1.where, s32[4]{0:T(128)} %copy-done.18, bf16[1024,768]{1,0:T(8,128)(2,1)} %get-tuple-element.112.sel, ...), custom_call_target="tpu_custom_call" | custom-call | flops 12079595520 | bytes 23592960 | tf_op jit(solution)/shard_map/backward_block/pallas_call | solution.py:502
  198.9 2.7 add_convert_fusion.6
  201.7 4.5 %all-to-all-start.2 = ((bf16[8,24,1536]{2,1,0:T(8,128)(2,1)}), bf16[8,24,1536]{2,1,0:T(8,128)(2,1)}, u32[]{:S(2)}, u32[]{:S(2)}) async-start(bf16[8,24,1536]{2,1,0:T(8,128)(2,1)} %bitcast.22), calls=%async_computation.2 | async-start | bytes 1179648 | tf_op jit(solution)/shard_map/all_to_all | solution.py:704
  206.9 1.5 collective-permute-start.29
  208.4 1.2 collective-permute-start.30
  209.7 13.5 %place_rows.1 = bf16[4,2048,768]{2,1,0:T(8,128)(2,1)} custom-call(s32[2,4]{1,0:T(2,128)} %pad_add_fusion.runs, bf16[1024,768]{1,0:T(8,128)(2,1)} %get-tuple-element.163.rows, s32[4,1,256]{2,1,0:T(1,128)} %broadcast_in_dim.36.target, bf16[4,2048,768]{2,1,0:T(8,128)(2,1)} %x.5), custom_call_target="tpu_custom_call" | custom-call | flops 3221225472 | bytes 25165824 | tf_op jit(solution)/shard_map/place_rows/pallas_call | solution.py:615
  223.2 12.5 %project_grads.1 = (bf16[768,1664]{1,0:T(8,128)(2,1)}, bf16[768,1664]{1,0:T(8,128)(2,1)}) custom-call(s32[2]{0:T(128)} %pad_add_fusion.1.where, bf16[768,1024]{1,0:T(8,128)(2,1)} %get-tuple-element.171.n1t, bf16[768,1024]{1,0:T(8,128)(2,1)} %get-tuple-element.172.dattnt, bf16[1024,2304]{1,0:T(8,128)(2,1)} %get-tuple-element.173.dqkv, ...), custom_call_target="tpu_custom_call" | custom-call | flops 5234491392 | bytes 9109504 | tf_op jit(solution)/shard_map/project_grads/pallas_call | solution.py:570
  235.9 1.2 convert_reduce_fusion.2
  237.8 2.7 add_convert_fusion.5
  240.9 1.9 add_convert_fusion.1
  243.5 1.5 collective-permute-start.33
  245.0 1.3 collective-permute-start.34
  246.3 4.7 %all-to-all-start.3 = ((bf16[8,24,1536]{2,1,0:T(8,128)(2,1)}), bf16[8,24,1536]{2,1,0:T(8,128)(2,1)}, u32[]{:S(2)}, u32[]{:S(2)}) async-start(bf16[8,24,1536]{2,1,0:T(8,128)(2,1)} %bitcast.24), calls=%async_computation.3 | async-start | bytes 1179648 | tf_op jit(solution)/shard_map/all_to_all | solution.py:704
  250.9 14.3 %input_rows.2.rest_10_ = bf16[4,2048,768]{2,1,0:T(8,128)(2,1)} custom-call(s32[2]{0:T(128)} %pad_add_fusion.1.where, s32[2,4]{1,0:T(2,128)} %pad_add_fusion.runs, bf16[1024,768]{1,0:T(8,128)(2,1)} %get-tuple-element.112.sel, bf16[1024,768]{1,0:T(8,128)(2,1)} %get-tuple-element.113.grad, f32[8,768]{1,0:T(8,128)} %get-tuple-element.145.vec, ...), custom_call_target="tpu_custom_call" | custom-call | flops 12884901888 | bytes 25165824 | tf_op jit(solution)/shard_map/input_rows/pallas_call | solution.py:661
  265.3 7.4 %collective-permute-done.33 = bf16[192,1664]{1,0:T(8,128)(2,1)} collective-permute-done((bf16[192,1664]{1,0:T(8,128)(2,1)}, bf16[192,1664]{1,0:T(8,128)(2,1)}, u32[]{:S(2)}, u32[]{:S(2)}) %collective-permute-start.33) | collective-permute-done | bytes 639008 | tf_op jit(solution)/shard_map/ppermute | solution.py:699
  273.8 2.8 add_convert_fusion
  276.7 1.2 convert_reduce_fusion.1
  279.4 4.7 %all-to-all-start.4 = ((bf16[8,24,1664]{2,1,0:T(8,128)(2,1)}), bf16[8,24,1664]{2,1,0:T(8,128)(2,1)}, u32[]{:S(2)}, u32[]{:S(2)}) async-start(bf16[8,24,1664]{2,1,0:T(8,128)(2,1)} %bitcast.26), calls=%async_computation.4 | async-start | bytes 1277952 | tf_op jit(solution)/shard_map/all_to_all | solution.py:704
  284.8 14.4 %input_rows.3 = bf16[4,2048,768]{2,1,0:T(8,128)(2,1)} custom-call(s32[2]{0:T(128)} %pad_add_fusion.1.where, s32[2,4]{1,0:T(2,128)} %pad_add_fusion.runs, bf16[1024,768]{1,0:T(8,128)(2,1)} %get-tuple-element.112.sel, bf16[1024,768]{1,0:T(8,128)(2,1)} %get-tuple-element.113.grad, f32[8,768]{1,0:T(8,128)} %get-tuple-element.145.vec, ...), custom_call_target="tpu_custom_call", output_to_operand_aliasing={{}: (20, {})} | custom-call | flops 12884901888 | bytes 25165824 | tf_op jit(solution)/shard_map/input_rows/pallas_call | solution.py:661
  299.2 2.8 all-to-all-done.4
  302.0 1.2 convert_reduce_fusion
  (144 shorter events, 26.6 us)
Async XLA Ops:
  4.8 7.4 %copy-start.19 = (s32[4]{0:T(128)S(1)}, s32[4]{0:T(128)}, u32[]{:S(2)}) copy-start(s32[4]{0:T(128)} %param.15) | copy-start | bytes 52
  4.8 7.4 %copy-start.16 = (s32[4,2048]{1,0:T(4,128)S(1)}, s32[4,2048]{1,0:T(4,128)}, u32[]{:S(2)}) copy-start(s32[4,2048]{1,0:T(4,128)} %param.16) | copy-start | bytes 98308
  4.8 8.1 %copy-start.7 = (bf16[24,3072]{1,0:T(8,128)(2,1)S(1)}, bf16[24,3072]{1,0:T(8,128)(2,1)}, u32[]{:S(2)}) copy-start(bf16[24,3072]{1,0:T(8,128)(2,1)} %param.22) | copy-start | bytes 442372
  4.8 8.1 %copy-start.15 = (bf16[3072,24]{0,1:T(8,128)(2,1)S(1)}, bf16[3072,24]{0,1:T(8,128)(2,1)}, u32[]{:S(2)}) copy-start(bf16[3072,24]{0,1:T(8,128)(2,1)} %param.24) | copy-start | bytes 442372
  4.8 8.1 %copy-start.17 = (s32[4,256]{1,0:T(4,128)S(1)}, s32[4,256]{1,0:T(4,128)}, u32[]{:S(2)}) copy-start(s32[4,256]{1,0:T(4,128)} %param.17) | copy-start | bytes 12292
  5.7 24.3 %all-to-all-start = ((bf16[8,24,1664]{2,1,0:T(8,128)(2,1)}), bf16[8,24,1664]{2,1,0:T(8,128)(2,1)}, u32[]{:S(2)}, u32[]{:S(2)}) async-start(bf16[8,24,1664]{2,1,0:T(8,128)(2,1)} %bitcast.11), calls=%async_computation | async-start | bytes 1277952 | tf_op jit(solution)/shard_map/all_to_all | solution.py:704
  32.2 33.1 %all-to-all-start.1 = ((bf16[8,24,3072]{2,1,0:T(8,128)(2,1)}), bf16[8,24,3072]{2,1,0:T(8,128)(2,1)S(1)}, u32[]{:S(2)}, u32[]{:S(2)}) async-start(bf16[8,24,3072]{2,1,0:T(8,128)(2,1)} %bitcast.20), calls=%async_computation.1 | async-start | bytes 2359296 | tf_op jit(solution)/shard_map/all_to_all | solution.py:704
  35.9 16.9 %collective-permute-start.1 = (bf16[192,1664]{1,0:T(8,128)(2,1)}, bf16[192,1664]{1,0:T(8,128)(2,1)S(1)}, u32[]{:S(2)}, u32[]{:S(2)}) collective-permute-start(bf16[192,1664]{1,0:T(8,128)(2,1)} %bitcast.12.rest_0_), channel_id=1, source_target_pairs={{0,4},{4,0},{8,12},{12,8},{16,20},{20,16},{24,28},{28,24},{1,5},{5... | collective-permute-start | bytes 1916936 | tf_op jit(solution)/shard_map/ppermute | solution.py:699
  37.5 17.0 %collective-permute-start = (bf16[192,1664]{1,0:T(8,128)(2,1)}, bf16[192,1664]{1,0:T(8,128)(2,1)S(1)}, u32[]{:S(2)}, u32[]{:S(2)}) collective-permute-start(bf16[192,1664]{1,0:T(8,128)(2,1)} %bitcast.12.rest_0_), channel_id=1, source_target_pairs={{0,2},{1,3},{2,0},{3,1},{4,6},{5,7},{6,4},{7,5},{8,10},{9,11},{10,... | collective-permute-start | bytes 1916936 | tf_op jit(solution)/shard_map/ppermute | solution.py:697
  39.0 24.3 %collective-permute-start.4 = (bf16[192,1664]{1,0:T(8,128)(2,1)}, bf16[192,1664]{1,0:T(8,128)(2,1)S(1)}, u32[]{:S(2)}, u32[]{:S(2)}) collective-permute-start(bf16[192,1664]{1,0:T(8,128)(2,1)} %bitcast.12.rest_0_), channel_id=1, source_target_pairs={{0,1},{1,0},{2,3},{3,2},{4,5},{5,4},{6,7},{7,6},{8,9},{9,8},{10,11... | collective-permute-start | bytes 1916936 | tf_op jit(solution)/shard_map/ppermute | solution.py:693
  52.9 13.6 %copy-start.3 = (bf16[192,1664]{1,0:T(8,128)(2,1)}, bf16[192,1664]{1,0:T(8,128)(2,1)S(1)}, u32[]{:S(2)}) copy-start(bf16[192,1664]{1,0:T(8,128)(2,1)S(1)} %collective-permute-done.1.rest_2_) | copy-start | bytes 1916932
  52.9 9.0 %collective-permute-start.2 = (bf16[96,1664]{1,0:T(8,128)(2,1)S(1)}, bf16[96,1664]{1,0:T(8,128)(2,1)S(1)}, u32[]{:S(2)}, u32[]{:S(2)}) collective-permute-start(bf16[96,1664]{1,0:T(8,128)(2,1)S(1)} %slice.233), channel_id=1, source_target_pairs={{0,2},{1,3},{2,0},{3,1},{4,6},{5,7},{6,4},{7,5},{8,10},{9,11},{10,... | collective-permute-start | bytes 958472 | tf_op jit(solution)/shard_map/ppermute | solution.py:697
  54.5 12.0 %copy-start.4 = (bf16[192,1664]{1,0:T(8,128)(2,1)}, bf16[192,1664]{1,0:T(8,128)(2,1)S(1)}, u32[]{:S(2)}) copy-start(bf16[192,1664]{1,0:T(8,128)(2,1)S(1)} %collective-permute-done.rest_1_) | copy-start | bytes 1916932
  54.5 8.8 %collective-permute-start.3 = (bf16[96,1664]{1,0:T(8,128)(2,1)S(1)}, bf16[96,1664]{1,0:T(8,128)(2,1)}, u32[]{:S(2)}, u32[]{:S(2)}) collective-permute-start(bf16[96,1664]{1,0:T(8,128)(2,1)S(1)} %slice.234), channel_id=1, source_target_pairs={{0,4},{4,0},{8,12},{12,8},{16,20},{20,16},{24,28},{28,24},{1,5},{5... | collective-permute-start | bytes 958472 | tf_op jit(solution)/shard_map/ppermute | solution.py:699
  56.1 9.2 %collective-permute-start.5 = (bf16[192,1664]{1,0:T(8,128)(2,1)S(1)}, bf16[192,1664]{1,0:T(8,128)(2,1)}, u32[]{:S(2)}, u32[]{:S(2)}) collective-permute-start(bf16[192,1664]{1,0:T(8,128)(2,1)S(1)} %collective-permute-done.rest_1_), channel_id=1, source_target_pairs={{0,1},{1,0},{2,3},{3,2},{4,5},{5,4},{6,7},{7,6},{8,9},{9,8},{10,11... | collective-permute-start | bytes 1916936 | tf_op jit(solution)/shard_map/ppermute | solution.py:693
  56.1 9.2 %collective-permute-start.6 = (bf16[192,1664]{1,0:T(8,128)(2,1)S(1)}, bf16[192,1664]{1,0:T(8,128)(2,1)}, u32[]{:S(2)}, u32[]{:S(2)}) collective-permute-start(bf16[192,1664]{1,0:T(8,128)(2,1)S(1)} %collective-permute-done.1.rest_2_), channel_id=1, source_target_pairs={{0,1},{1,0},{2,3},{3,2},{4,5},{5,4},{6,7},{7,6},{8,9},{9,8},{10,11... | collective-permute-start | bytes 1916936 | tf_op jit(solution)/shard_map/ppermute | solution.py:693
  61.9 1.7 collective-permute-start.7
  63.3 2.0 collective-permute-start.8
  66.5 29.5 %collective-permute-start.10 = (bf16[192,1536]{1,0:T(8,128)(2,1)}, bf16[192,1536]{1,0:T(8,128)(2,1)}, u32[]{:S(2)}, u32[]{:S(2)}) collective-permute-start(bf16[192,1536]{1,0:T(8,128)(2,1)} %get-tuple-element.131.rest_4_), channel_id=1, source_target_pairs={{0,4},{4,0},{8,12},{12,8},{16,20},{20,16},{24,28},{28,24},{1,5},{5... | collective-permute-start | bytes 1769480 | tf_op jit(solution)/shard_map/ppermute | solution.py:699
  68.0 28.0 %collective-permute-start.11 = (bf16[192,1536]{1,0:T(8,128)(2,1)}, bf16[192,1536]{1,0:T(8,128)(2,1)}, u32[]{:S(2)}, u32[]{:S(2)}) collective-permute-start(bf16[192,1536]{1,0:T(8,128)(2,1)} %get-tuple-element.131.rest_4_), channel_id=1, source_target_pairs={{0,6},{1,7},{2,4},{3,5},{4,2},{5,3},{6,0},{7,1},{8,14},{9,15},{10,... | collective-permute-start | bytes 1769480 | tf_op jit(solution)/shard_map/ppermute | solution.py:701
  69.4 26.7 %collective-permute-start.9 = (bf16[192,1536]{1,0:T(8,128)(2,1)}, bf16[192,1536]{1,0:T(8,128)(2,1)}, u32[]{:S(2)}, u32[]{:S(2)}) collective-permute-start(bf16[192,1536]{1,0:T(8,128)(2,1)} %get-tuple-element.131.rest_4_), channel_id=1, source_target_pairs={{0,2},{1,3},{2,0},{3,1},{4,6},{5,7},{6,4},{7,5},{8,10},{9,11},{10,... | collective-permute-start | bytes 1769480 | tf_op jit(solution)/shard_map/ppermute | solution.py:697
  96.1 2.5 collective-permute-start.12
  96.1 3.9 %collective-permute-start.13 = (bf16[192,1536]{1,0:T(8,128)(2,1)}, bf16[192,1536]{1,0:T(8,128)(2,1)}, u32[]{:S(2)}, u32[]{:S(2)}) collective-permute-start(bf16[192,1536]{1,0:T(8,128)(2,1)} %collective-permute-done.9.rest_5_), channel_id=1, source_target_pairs={{0,1},{1,0},{2,3},{3,2},{4,5},{5,4},{6,7},{7,6},{8,9},{9,8},{10,11... | collective-permute-start | bytes 1769480 | tf_op jit(solution)/shard_map/ppermute | solution.py:693
  96.6 5.0 %collective-permute-start.14 = (bf16[192,1536]{1,0:T(8,128)(2,1)}, bf16[192,1536]{1,0:T(8,128)(2,1)}, u32[]{:S(2)}, u32[]{:S(2)}) collective-permute-start(bf16[192,1536]{1,0:T(8,128)(2,1)} %collective-permute-done.10.rest_6_), channel_id=1, source_target_pairs={{0,1},{1,0},{2,3},{3,2},{4,5},{5,4},{6,7},{7,6},{8,9},{9,8},{10,11... | collective-permute-start | bytes 1769480 | tf_op jit(solution)/shard_map/ppermute | solution.py:693
  96.7 5.0 %collective-permute-start.15 = (bf16[192,1536]{1,0:T(8,128)(2,1)}, bf16[192,1536]{1,0:T(8,128)(2,1)}, u32[]{:S(2)}, u32[]{:S(2)}) collective-permute-start(bf16[192,1536]{1,0:T(8,128)(2,1)} %collective-permute-done.11.rest_7_), channel_id=1, source_target_pairs={{0,1},{1,0},{2,3},{3,2},{4,5},{5,4},{6,7},{7,6},{8,9},{9,8},{10,11... | collective-permute-start | bytes 1769480 | tf_op jit(solution)/shard_map/ppermute | solution.py:693
  97.1 31.4 %collective-permute-start.17 = (bf16[192,1536]{1,0:T(8,128)(2,1)}, bf16[192,1536]{1,0:T(8,128)(2,1)}, u32[]{:S(2)}, u32[]{:S(2)}) collective-permute-start(bf16[192,1536]{1,0:T(8,128)(2,1)} %get-tuple-element.139.rest_4_), channel_id=1, source_target_pairs={{0,2},{1,3},{2,0},{3,1},{4,6},{5,7},{6,4},{7,5},{8,10},{9,11},{10,... | collective-permute-start | bytes 1769480 | tf_op jit(solution)/shard_map/ppermute | solution.py:697
  98.5 30.0 %collective-permute-start.18 = (bf16[192,1536]{1,0:T(8,128)(2,1)}, bf16[192,1536]{1,0:T(8,128)(2,1)}, u32[]{:S(2)}, u32[]{:S(2)}) collective-permute-start(bf16[192,1536]{1,0:T(8,128)(2,1)} %get-tuple-element.139.rest_4_), channel_id=1, source_target_pairs={{0,4},{4,0},{8,12},{12,8},{16,20},{20,16},{24,28},{28,24},{1,5},{5... | collective-permute-start | bytes 1769480 | tf_op jit(solution)/shard_map/ppermute | solution.py:699
  100.1 28.5 %collective-permute-start.19 = (bf16[192,1536]{1,0:T(8,128)(2,1)}, bf16[192,1536]{1,0:T(8,128)(2,1)}, u32[]{:S(2)}, u32[]{:S(2)}) collective-permute-start(bf16[192,1536]{1,0:T(8,128)(2,1)} %get-tuple-element.139.rest_4_), channel_id=1, source_target_pairs={{0,6},{1,7},{2,4},{3,5},{4,2},{5,3},{6,0},{7,1},{8,14},{9,15},{10,... | collective-permute-start | bytes 1769480 | tf_op jit(solution)/shard_map/ppermute | solution.py:701
  128.6 2.4 collective-permute-start.20
  128.7 3.2 %collective-permute-start.21 = (bf16[192,1536]{1,0:T(8,128)(2,1)}, bf16[192,1536]{1,0:T(8,128)(2,1)}, u32[]{:S(2)}, u32[]{:S(2)}) collective-permute-start(bf16[192,1536]{1,0:T(8,128)(2,1)} %collective-permute-done.17.rest_5_), channel_id=1, source_target_pairs={{0,1},{1,0},{2,3},{3,2},{4,5},{5,4},{6,7},{7,6},{8,9},{9,8},{10,11... | collective-permute-start | bytes 1769480 | tf_op jit(solution)/shard_map/ppermute | solution.py:693
  129.2 3.5 %collective-permute-start.22 = (bf16[192,1536]{1,0:T(8,128)(2,1)}, bf16[192,1536]{1,0:T(8,128)(2,1)}, u32[]{:S(2)}, u32[]{:S(2)}) collective-permute-start(bf16[192,1536]{1,0:T(8,128)(2,1)} %collective-permute-done.18.rest_6_), channel_id=1, source_target_pairs={{0,1},{1,0},{2,3},{3,2},{4,5},{5,4},{6,7},{7,6},{8,9},{9,8},{10,11... | collective-permute-start | bytes 1769480 | tf_op jit(solution)/shard_map/ppermute | solution.py:693
  129.3 4.3 %collective-permute-start.23 = (bf16[192,1536]{1,0:T(8,128)(2,1)}, bf16[192,1536]{1,0:T(8,128)(2,1)}, u32[]{:S(2)}, u32[]{:S(2)}) collective-permute-start(bf16[192,1536]{1,0:T(8,128)(2,1)} %collective-permute-done.19.rest_7_), channel_id=1, source_target_pairs={{0,1},{1,0},{2,3},{3,2},{4,5},{5,4},{6,7},{7,6},{8,9},{9,8},{10,11... | collective-permute-start | bytes 1769480 | tf_op jit(solution)/shard_map/ppermute | solution.py:693
  129.7 31.1 %collective-permute-start.16 = (bf16[768,1536]{1,0:T(8,128)(2,1)}, bf16[768,1536]{1,0:T(8,128)(2,1)}, u32[]{:S(2)}, u32[]{:S(2)}) collective-permute-start(bf16[768,1536]{1,0:T(8,128)(2,1)} %get-tuple-element.136), channel_id=1, source_target_pairs={{0,1},{1,0},{2,3},{3,2},{4,5},{5,4},{6,7},{7,6},{8,9},{9,8},{10,11... | collective-permute-start | bytes 7077896 | tf_op jit(solution)/shard_map/ppermute | solution.py:693
  160.5 8.0 %collective-permute-start.27 = (bf16[768,1536]{1,0:T(8,128)(2,1)}, bf16[768,1536]{1,0:T(8,128)(2,1)S(1)}, u32[]{:S(2)}, u32[]{:S(2)}) collective-permute-start(bf16[768,1536]{1,0:T(8,128)(2,1)} %get-tuple-element.151), channel_id=1, source_target_pairs={{0,1},{1,0},{2,3},{3,2},{4,5},{5,4},{6,7},{7,6},{8,9},{9,8},{10,11... | collective-permute-start | bytes 7077896 | tf_op jit(solution)/shard_map/ppermute | solution.py:693
  160.8 7.8 %copy-start.1 = (bf16[768,1536]{1,0:T(8,128)(2,1)S(1)}, bf16[768,1536]{1,0:T(8,128)(2,1)}, u32[]{:S(2)}) copy-start(bf16[768,1536]{1,0:T(8,128)(2,1)} %get-tuple-element.150) | copy-start | bytes 7077892
  165.0 33.9 %collective-permute-start.24 = (bf16[192,1536]{1,0:T(8,128)(2,1)}, bf16[192,1536]{1,0:T(8,128)(2,1)}, u32[]{:S(2)}, u32[]{:S(2)}) collective-permute-start(bf16[192,1536]{1,0:T(8,128)(2,1)} %get-tuple-element.212), channel_id=1, source_target_pairs={{0,2},{1,3},{2,0},{3,1},{4,6},{5,7},{6,4},{7,5},{8,10},{9,11},{10,... | collective-permute-start | bytes 1769480 | tf_op jit(solution)/shard_map/ppermute | solution.py:697
  165.8 33.2 %collective-permute-start.25 = (bf16[192,1536]{1,0:T(8,128)(2,1)}, bf16[192,1536]{1,0:T(8,128)(2,1)}, u32[]{:S(2)}, u32[]{:S(2)}) collective-permute-start(bf16[192,1536]{1,0:T(8,128)(2,1)} %get-tuple-element.211), channel_id=1, source_target_pairs={{0,4},{4,0},{8,12},{12,8},{16,20},{20,16},{24,28},{28,24},{1,5},{5... | collective-permute-start | bytes 1769480 | tf_op jit(solution)/shard_map/ppermute | solution.py:699
  167.3 31.7 %collective-permute-start.26 = (bf16[192,1536]{1,0:T(8,128)(2,1)}, bf16[192,1536]{1,0:T(8,128)(2,1)}, u32[]{:S(2)}, u32[]{:S(2)}) collective-permute-start(bf16[192,1536]{1,0:T(8,128)(2,1)} %get-tuple-element.210), channel_id=1, source_target_pairs={{0,6},{1,7},{2,4},{3,5},{4,2},{5,3},{6,0},{7,1},{8,14},{9,15},{10,... | collective-permute-start | bytes 1769480 | tf_op jit(solution)/shard_map/ppermute | solution.py:701
  201.7 34.1 %all-to-all-start.2 = ((bf16[8,24,1536]{2,1,0:T(8,128)(2,1)}), bf16[8,24,1536]{2,1,0:T(8,128)(2,1)}, u32[]{:S(2)}, u32[]{:S(2)}) async-start(bf16[8,24,1536]{2,1,0:T(8,128)(2,1)} %bitcast.22), calls=%async_computation.2 | async-start | bytes 1179648 | tf_op jit(solution)/shard_map/all_to_all | solution.py:704
  206.1 29.6 %collective-permute-start.28 = (bf16[192,1536]{1,0:T(8,128)(2,1)}, bf16[192,1536]{1,0:T(8,128)(2,1)}, u32[]{:S(2)}, u32[]{:S(2)}) collective-permute-start(bf16[192,1536]{1,0:T(8,128)(2,1)} %get-tuple-element.168), channel_id=1, source_target_pairs={{0,2},{1,3},{2,0},{3,1},{4,6},{5,7},{6,4},{7,5},{8,10},{9,11},{10,... | collective-permute-start | bytes 1769480 | tf_op jit(solution)/shard_map/ppermute | solution.py:697
  206.9 28.8 %collective-permute-start.29 = (bf16[192,1536]{1,0:T(8,128)(2,1)}, bf16[192,1536]{1,0:T(8,128)(2,1)}, u32[]{:S(2)}, u32[]{:S(2)}) collective-permute-start(bf16[192,1536]{1,0:T(8,128)(2,1)} %get-tuple-element.169), channel_id=1, source_target_pairs={{0,4},{4,0},{8,12},{12,8},{16,20},{20,16},{24,28},{28,24},{1,5},{5... | collective-permute-start | bytes 1769480 | tf_op jit(solution)/shard_map/ppermute | solution.py:699
  208.4 27.3 %collective-permute-start.30 = (bf16[192,1536]{1,0:T(8,128)(2,1)}, bf16[192,1536]{1,0:T(8,128)(2,1)}, u32[]{:S(2)}, u32[]{:S(2)}) collective-permute-start(bf16[192,1536]{1,0:T(8,128)(2,1)} %get-tuple-element.170), channel_id=1, source_target_pairs={{0,6},{1,7},{2,4},{3,5},{4,2},{5,3},{6,0},{7,1},{8,14},{9,15},{10,... | collective-permute-start | bytes 1769480 | tf_op jit(solution)/shard_map/ppermute | solution.py:701
  235.8 5.1 %collective-permute-start.31 = (bf16[768,1664]{1,0:T(8,128)(2,1)}, bf16[768,1664]{1,0:T(8,128)(2,1)S(1)}, u32[]{:S(2)}, u32[]{:S(2)}) collective-permute-start(bf16[768,1664]{1,0:T(8,128)(2,1)} %get-tuple-element.184), channel_id=1, source_target_pairs={{0,1},{1,0},{2,3},{3,2},{4,5},{5,4},{6,7},{7,6},{8,9},{9,8},{10,11... | collective-permute-start | bytes 7667720 | tf_op jit(solution)/shard_map/ppermute | solution.py:693
  242.8 22.5 %collective-permute-start.32 = (bf16[192,1664]{1,0:T(8,128)(2,1)}, bf16[192,1664]{1,0:T(8,128)(2,1)}, u32[]{:S(2)}, u32[]{:S(2)}) collective-permute-start(bf16[192,1664]{1,0:T(8,128)(2,1)} %get-tuple-element.188), channel_id=1, source_target_pairs={{0,2},{1,3},{2,0},{3,1},{4,6},{5,7},{6,4},{7,5},{8,10},{9,11},{10,... | collective-permute-start | bytes 1916936 | tf_op jit(solution)/shard_map/ppermute | solution.py:697
  243.5 29.2 %collective-permute-start.33 = (bf16[192,1664]{1,0:T(8,128)(2,1)}, bf16[192,1664]{1,0:T(8,128)(2,1)}, u32[]{:S(2)}, u32[]{:S(2)}) collective-permute-start(bf16[192,1664]{1,0:T(8,128)(2,1)} %get-tuple-element.189), channel_id=1, source_target_pairs={{0,4},{4,0},{8,12},{12,8},{16,20},{20,16},{24,28},{28,24},{1,5},{5... | collective-permute-start | bytes 1916936 | tf_op jit(solution)/shard_map/ppermute | solution.py:699
  245.0 28.8 %collective-permute-start.34 = (bf16[192,1664]{1,0:T(8,128)(2,1)}, bf16[192,1664]{1,0:T(8,128)(2,1)}, u32[]{:S(2)}, u32[]{:S(2)}) collective-permute-start(bf16[192,1664]{1,0:T(8,128)(2,1)} %get-tuple-element.190), channel_id=1, source_target_pairs={{0,6},{1,7},{2,4},{3,5},{4,2},{5,3},{6,0},{7,1},{8,14},{9,15},{10,... | collective-permute-start | bytes 1916936 | tf_op jit(solution)/shard_map/ppermute | solution.py:701
  246.3 30.4 %all-to-all-start.3 = ((bf16[8,24,1536]{2,1,0:T(8,128)(2,1)}), bf16[8,24,1536]{2,1,0:T(8,128)(2,1)}, u32[]{:S(2)}, u32[]{:S(2)}) async-start(bf16[8,24,1536]{2,1,0:T(8,128)(2,1)} %bitcast.24), calls=%async_computation.3 | async-start | bytes 1179648 | tf_op jit(solution)/shard_map/all_to_all | solution.py:704
  279.4 22.6 %all-to-all-start.4 = ((bf16[8,24,1664]{2,1,0:T(8,128)(2,1)}), bf16[8,24,1664]{2,1,0:T(8,128)(2,1)}, u32[]{:S(2)}, u32[]{:S(2)}) async-start(bf16[8,24,1664]{2,1,0:T(8,128)(2,1)} %bitcast.26), calls=%async_computation.4 | async-start | bytes 1277952 | tf_op jit(solution)/shard_map/all_to_all | solution.py:704
  (14 other events, 38.6 us)
where the time goes:
time: 308 us; the launch traced here: 307 us
  Pallas kernels  175 us (57%)
  starting transfers between devices  51.8 us (17%)
  waiting for transfers between devices  39.6 us (13%)
  other arithmetic  26.9 us (9%)
  local copies, waits for them, and re-layouts  12.5 us (4%)
    pallas_call x2, Pallas kernels, mlp_part(): pl.pallas_call(partial(mlp_kernel, layout=layout, tile=tile), grid_spec=p...  53.9 us
    pallas_call x2, Pallas kernels, input_rows(): pl.pallas_call(partial(input_kernel, layout=layout, first=first), grid_sp...  28.7 us
    pallas_call x1, Pallas kernels, backward_block(): pl.pallas_call(partial(backward_kernel, layout=layout, half=3 * width //...  28.6 us
    pallas_call x1, Pallas kernels, forward_block(): pl.pallas_call(partial(forward_kernel, layout=layout, half=3 * width // 2...  25.4 us
    all_to_all x5, starting transfers between devices, along(): lax.all_to_all(value, AXES, 0, 0, axis_index_groups=self.lines, tiled=True)  24 us
    ppermute x7, waiting for transfers between devices, over(): return lax.ppermute(value, 'wide', [(i, i ^ 1) for i in range(self.wide)])  22.7 us
    pallas_call x1, Pallas kernels, place_rows(): pl.pallas_call(out_kernel, grid_spec=pltpu.PrefetchScalarGridSpec(num_sca...  13.5 us
    pallas_call x1, Pallas kernels, gather_rows(): pl.pallas_call(gather_kernel, grid=(seqs,), in_specs=[pl.BlockSpec((1, sl...  12.6 us
  transfers between devices with their start and end apart: 40, of which 15 were waited for; matrix products, arithmetic and copies ran while one was open for 6% of the time, Pallas kernels for 57%

commit v1 on v0

--- a/solution.py
+++ b/solution.py
@@ -76,13 +76,13 @@
     )
 
 
-def store_rows(layout, here, target, value):
+def store_rows(layout, target, value):
     height = layout.height
     for line in range(layout.depth):
         for owner in range(layout.plane):
-            start = pl.multiple_of(((owner ^ here) * layout.depth + line) * height, 8)
+            start = (owner * layout.depth + line) * height
             c = line * layout.plane + owner
-            target[pl.ds(start, height), :] = value[c * height : (c + 1) * height, :]
+            target[start : start + height, :] = value[c * height : (c + 1) * height, :]
 
 
 def gather_kernel(target, x, cot, sel, grad):
@@ -209,8 +209,8 @@
     def _():
         gsum[...] += gsum_now
 
-    store_rows(layout, here, gt, d_mlp.T)
-    store_rows(layout, here, n1t, n1.T)
+    store_rows(layout, gt, d_mlp.T)
+    store_rows(layout, n1t, n1.T)
     qkv[...] = dot(n1, w_in[...]).astype(BF16)
 
     allowed = allowed_keys(slots, counts[b])
@@ -243,7 +243,7 @@
     r2 = lax.rsqrt(jnp.mean(stream * stream, axis=-1, keepdims=True) + EPSILON)
     normed = (stream * r2 * vec[1:2, :]).astype(BF16)
     n2[...] = normed
-    store_rows(layout, here, n2t, normed.T)
+    store_rows(layout, n2t, normed.T)
     stats[...] = jnp.where(lane == 2, r2, kept)
 
 
@@ -300,7 +300,7 @@
     mlp, dn2, d_own, d_oth, dbias, *held, w_up, w_down, d_first, act, d_pre, sem_rows, sems, sem_out = rest[
         4 + 2 * layout.pieces :
     ]
-    n2, n2t, g, gt = held
+    n2, n2t, g, gt, mlp_sum, dn2_sum = held
     i = pl.program_id(0)
     here = where[0]
     row_copies = [
@@ -351,8 +351,12 @@
         slope = half + 0.5 * pre * (1.0 - th * th) * (GELU_A + 3 * GELU_A * GELU_B * square)
         d_pre_now = (slope * dot(g[here, :], down_now[...])).astype(BF16)
         d_pre[here, :] = d_pre_now
-        mlp[here, :] = jnp.where(i == 0, 0.0, mlp[here, :]) + dot(act_now, down_now[...], 1, 1)
-        dn2[here, :] = jnp.where(i == 0, 0.0, dn2[here, :]) + dot(d_pre_now, up_now[...], 1, 1)
+        mlp_now = jnp.where(i == 0, 0.0, mlp_sum[here, :]) + dot(act_now, down_now[...], 1, 1)
+        mlp_sum[here, :] = mlp_now
+        mlp[here, :] = mlp_now.astype(BF16)
+        dn2_now = jnp.where(i == 0, 0.0, dn2_sum[here, :]) + dot(d_pre_now, up_now[...], 1, 1)
+        dn2_sum[here, :] = dn2_now
+        dn2[here, :] = dn2_now.astype(BF16)
         return total + jnp.sum(d_pre_now.astype(F32), axis=0, keepdims=True)
 
     dbias[...] = lax.fori_loop(0, MLP_CHUNKS, chunk, jnp.zeros_like(dbias))
@@ -394,6 +398,8 @@
                 pltpu.VMEM((width, rows), BF16),
                 pltpu.VMEM((rows, width), BF16),
                 pltpu.VMEM((width, rows), BF16),
+                pltpu.VMEM((rows, width), F32),
+                pltpu.VMEM((rows, width), F32),
                 pltpu.VMEM((2, width, tile), BF16),
                 pltpu.VMEM((2, width, tile), BF16),
                 pltpu.VMEM((width, 2 * tile), BF16),
@@ -405,8 +411,8 @@
             ],
         ),
         out_shape=[
-            shape((rows, width), F32),
-            shape((rows, width), F32),
+            shape((rows, width), BF16),
+            shape((rows, width), BF16),
             shape((width, 2 * tile), BF16),
             shape((width, 2 * tile), BF16),
             shape((1, 2 * tile), F32),
@@ -445,7 +451,7 @@
     rate = stats[:, 1:2]
     r2 = stats[:, 2:3]
     slot_grad = grad[...].astype(F32)
-    branch = (stream - x) + ((mlp[...] + mlp_two[...]) + vec[2:3, :])
+    branch = (stream - x) + (mlp[...].astype(F32) + mlp_two[...].astype(F32) + vec[2:3, :])
     new_rows[...] = (x + rate * branch).astype(BF16)
     d_logit = jnp.sum(slot_grad * branch, axis=-1, keepdims=True) * (rate * (1.0 - rate))
     router_now = jnp.sum(d_logit * x, axis=0, keepdims=True)
@@ -458,10 +464,10 @@
     def _():
         drouter[...] += router_now
 
-    d_mid = norm_pull(stream, r2, vec[1:2, :] * (dn2[...] + dn2_two[...]))
+    d_mid = norm_pull(stream, r2, vec[1:2, :] * (dn2[...].astype(F32) + dn2_two[...].astype(F32)))
     dmid[...] = d_mid + d_logit * vec[3:4, :]
     d_attn = (rate * slot_grad + d_mid).astype(BF16)
-    store_rows(layout, here, dattnt, d_attn.T)
+    store_rows(layout, dattnt, d_attn.T)
     d_att[...] = dot(d_attn, w_out[...]).astype(BF16)
 
     allowed = allowed_keys(slots, counts[b])
@@ -522,7 +528,7 @@
             shape((1, width), F32),
         ],
         compiler_params=params("arbitrary"),
-        cost_estimate=cost(20 * rows * width * width, 30 * rows * width),
+        cost_estimate=cost(2 * 20 * rows * width * width, 2 * 30 * rows * width),
         name="backward_block",
     )(where, counts, sel, grad, vec, qkv, mid, stats, *sums, *own, *oth)
 
@@ -581,7 +587,7 @@
         ),
         out_shape=[jax.ShapeDtypeStruct((width, total), BF16)] * 2,
         compiler_params=params("arbitrary"),
-        cost_estimate=cost(4 * width * rows * total, 2 * (2 * width * rows + rows * total + width * total)),
+        cost_estimate=cost(2 * 4 * width * rows * total, 2 * 4 * width * rows),
         name="project_grads",
     )(where, n1t, dattnt, dqkv, att, *vectors)
 
@@ -677,17 +683,18 @@
         ),
         out_shape=jax.ShapeDtypeStruct(x.shape, BF16),
         compiler_params=params("arbitrary"),
-        cost_estimate=cost(8 * seqs * slots * length * width, 4 * seqs * length * width),
+        cost_estimate=cost(1, 1),
         input_output_aliases={10 + 2 * layout.pieces: 0} if begun else {},
         name="input_rows",
     )(where, runs, sel, grad, vec, stats, dmid, dqkv, target, x, *own, *oth, *begun)
 
 
 class Paths:
-    def __init__(self, wide, narrow):
-        self.wide, self.narrow, self.depth = wide, narrow, wide // 2
+    def __init__(self, wide, narrow, here):
+        self.wide, self.narrow, self.depth, self.here = wide, narrow, wide // 2, here
         ids = np.arange(wide * narrow).reshape(self.depth, 4, 2)
         self.lines = ids.transpose(1, 0, 2).reshape(4, -1).tolist()
+        self.planes = ids.transpose(0, 2, 1).reshape(-1, 4).tolist()
 
     def swap(self, value):
         return lax.ppermute(value, "narrow", [(i, i ^ 1) for i in range(self.narrow)])
@@ -721,10 +728,17 @@
 
     def chip_sums(self, own, got):
         rows = own.shape[0] // 4
+        starts = [(self.here ^ step) * rows for step in range(4)]
         return [
-            add_halves(own[step * rows : (step + 1) * rows], got[step * rows : (step + 1) * rows])
-            for step in range(4)
+            add_halves(
+                lax.dynamic_slice(own, (start, 0), (rows, own.shape[1])),
+                lax.dynamic_slice(got, (start, 0), (rows, own.shape[1])),
+            )
+            for start in starts
         ]
+
+    def exchange_plane(self, both):
+        return lax.all_to_all(both, AXES, 0, 0, axis_index_groups=self.planes, tiled=True)
 
     def send_plane(self, sums):
         return [self.over(sums[step], step) for step in (1, 2, 3)]
@@ -811,8 +825,8 @@
         return counts, runs, target[:, :, None], target[:, None, :]
 
     if fast:
-        paths = Paths(wide, narrow)
         here = (lax.axis_index("wide") & 1) * 2 + (lax.axis_index("narrow") >> 1)
+        paths = Paths(wide, narrow, here)
         lay_one = Layout(2 * shard, 4, halved(paths.depth))
         lay_two = Layout(2 * shard, 4, direct(paths.depth))
         placed = lax.dynamic_update_slice(
@@ -830,10 +844,11 @@
         sent, lengths = tie(sent, lengths)
         line = paths.along(sent)
         counts, runs, columns, target_row = places(lengths)
-        sel, slot_grad = gather_rows(columns, layer_in, cotangent)
         rest = paths.to_line(
             [jnp.concatenate([rest_of(side, 0), rest_of(side, 1)], axis=1) for side in (0, 1)]
         )
+        rest, columns = tie(rest, columns)
+        sel, slot_grad = gather_rows(columns, layer_in, cotangent)
         line, rest, sel, slot_grad, runs, target_row = tie(line, rest, sel, slot_grad, runs, target_row)
         own = paths.gather_halved(line)
         oth = paths.swap_all(own)
@@ -881,50 +896,48 @@
         lay_two, where, 1, tile, n2, n2t, g, gt, two_own, two_oth, bias
     )
     if fast:
-        d_two_got = paths.swap(d_two_oth)
         d_one_got, mlp_two = tie(d_one_got, mlp_two)
         d_one = paths.chip_sums(d_one_own, d_one_got)
         d_one_plane = paths.send_plane(d_one)
-        d_two = paths.chip_sums(d_two_own, d_two_got)
-        _, d_two, mlp_two = tie(d_one, d_two, mlp_two)
-        d_two_plane = paths.send_plane(d_two)
+        d_two = add_halves(d_two_own, paths.swap(d_two_oth))
+        d_two, mlp_two = tie(d_two, mlp_two)
+        d_two = paths.exchange_plane(d_two)
     dqkv, dattnt, dmid, new_rows, drouter = backward_block(
         lay_one, where, counts, sel, slot_grad, vec, qkv, mid, stats, (mlp, mlp_two, dn2, dn2_two), own, oth
     )
+
+    proj_oth, proj_own = project_grads(
+        where, n1t, dattnt, dqkv, att, dbias_one, dbias_two, ddown_bias, drouter
+    )
     if fast:
-        d_one_plane, dqkv = tie(d_one_plane, dqkv)
-
-    if fast:
-        one = paths.sum_plane(d_one[0], d_one_plane)
-        one, new_rows = tie(one, new_rows)
-        one = paths.along(one)
+        d_one_plane, d_two, proj_oth = tie(d_one_plane, d_two, proj_oth)
+        proj_got = paths.swap(proj_oth)
+        proj = paths.chip_sums(proj_own, proj_got)
+        d_two = d_two.reshape(4, -1, 2 * tile)
+        sums = jnp.concatenate(
+            [paths.sum_plane(d_one[0], d_one_plane), paths.sum_plane(d_two[0], list(d_two[1:]))], axis=1
+        )
+        sums, proj, new_rows = tie(sums, proj, new_rows)
+        proj_plane = paths.send_plane(proj)
+        sums = paths.along(sums)
     layer_out = place_rows(runs, new_rows, target_row, layer_in)
     if fast:
-        dqkv, layer_out = tie(dqkv, layer_out)
-    proj_oth, proj_own = project_grads(
-        where, n1t, dattnt, dqkv, att, dbias_one, dbias_two, ddown_bias, drouter
-    )
-    if fast:
-        one, d_two_plane, proj_oth = tie(one, d_two_plane, proj_oth)
-        proj = paths.chip_sums(proj_own, paths.swap(proj_oth))
-        two = paths.sum_plane(d_two[0], d_two_plane)
-        two, proj, dmid = tie(two, proj, dmid)
-        proj_plane = paths.send_plane(proj)
-        two = paths.along(two)
+        dmid, layer_out = tie(dmid, layer_out)
     part = seqs // 2
     input_grad = input_rows(
         lay_one, where, runs, sel, slot_grad, vec, stats, dmid, dqkv, target_row, cotangent, own, oth, 0, part
     )
     if fast:
         proj = paths.sum_plane(proj[0], proj_plane)
-        two, proj, dmid, input_grad = tie(two, proj, dmid, input_grad)
+        sums, proj, dmid, input_grad = tie(sums, proj, dmid, input_grad)
     input_grad = input_rows(
         lay_one, where, runs, sel, slot_grad, vec, stats, dmid, dqkv, target_row, cotangent, own, oth,
         part, seqs - part, (input_grad,),
     )
 
     if fast:
-        one, two = paths.sum_line(one), paths.sum_line(two)
+        sums = paths.sum_line(sums)
+        one, two = sums[:, :, : 2 * tile], sums[:, :, 2 * tile :]
         proj = paths.sum_line(paths.along(proj))
     else:
         flat = jnp.concatenate(
@@ -954,9 +967,7 @@
         every, vectors = lax.psum(tuple(v.astype(F32) for v in mine), AXES)
     d_up_bias = lax.dynamic_slice(every.reshape(-1), (device * 4 * shard,), (4 * shard,))
     vectors = vectors.reshape(4, width)
-    d_down_bias, d_router = (
-        lax.dynamic_slice(vectors[k], (device * shard,), (shard,)) for k in (0, 1)
-    )
+    vectors = lax.dynamic_slice(vectors, (0, device * shard), (2, shard))
     gain_one = jnp.sum(project_in.astype(F32) * in_grad, axis=1) / first_gain.astype(F32)
     gain_two = jnp.sum(up_weight.astype(F32) * up_grad, axis=1) / second_gain.astype(F32)
     return (
@@ -969,8 +980,8 @@
         up_grad,
         d_up_bias,
         down_grad,
-        d_down_bias,
-        d_router,
+        vectors[0],
+        vectors[1],
     )
 
 

time: 308 us -> 293 us (0.951)
  waiting for transfers between devices: 39.6 us -> 32.1 us
  starting transfers between devices: 51.8 us -> 48.4 us
    ppermute x7 -> x6, waiting for transfers between devices: 22.7 us -> 15.4 us  [over(): return lax.ppermute(value, 'wide', [(i, i ^ 1) for i in range(self.wide)])]
    all_to_all x0 -> x1, starting transfers between devices: none -> 4.5 us  [exchange_plane(): lax.all_to_all(both, AXES, 0, 0, axis_index_groups=self.planes, tiled=True)]
    all_to_all x0 -> x1, waiting for transfers between devices: none -> 4.15 us  [exchange_plane(): lax.all_to_all(both, AXES, 0, 0, axis_index_groups=self.planes, tiled=True)]
    all_to_all x5 -> x4, starting transfers between devices: 24 us -> 20.1 us  [along(): lax.all_to_all(value, AXES, 0, 0, axis_index_groups=self.lines, tiled=True)]
    all_to_all x5 -> x4, waiting for transfers between devices: 4.19 us -> 0.65 us  [along(): lax.all_to_all(value, AXES, 0, 0, axis_index_groups=self.lines, tiled=True)]
    ppermute x7 -> x6, starting transfers between devices: 10.7 us -> 7.64 us  [over(): return lax.ppermute(value, 'wide', [(i, i ^ 1) for i in range(self.wide)])]
    ppermute x5 -> x4, starting transfers between devices: 6.74 us -> 6.03 us  [over(): lax.ppermute(value, AXES, [(i, i ^ mask) for i in range(self.wide * self....]
    ppermute x7 -> x6, starting transfers between devices: 7.34 us -> 7.32 us  [over(): lax.ppermute(value, 'narrow', [(i, i ^ 2) for i in range(self.narrow)])]
  transfers between devices with their start and end apart: 40 -> 37, of which waited for: 15 -> 12; matrix products, arithmetic and copies ran while one was open for 6% -> 8% of each run, Pallas kernels for 57% -> 59%
where the time goes in v1:
time: 293 us; the launch traced here: 292 us
  Pallas kernels  173 us (59%)
  starting transfers between devices  48.4 us (17%)
  waiting for transfers between devices  32.1 us (11%)
  other arithmetic  25.5 us (9%)
  local copies, waits for them, and re-layouts  11.8 us (4%)
    pallas_call x2, Pallas kernels, mlp_part(): pl.pallas_call(partial(mlp_kernel, layout=layout, tile=tile), grid_spec=p...  51.8 us
    pallas_call x2, Pallas kernels, input_rows(): pl.pallas_call(partial(input_kernel, layout=layout, first=first), grid_sp...  28.7 us
    pallas_call x1, Pallas kernels, backward_block(): pl.pallas_call(partial(backward_kernel, layout=layout, half=3 * width //...  28.2 us
    pallas_call x1, Pallas kernels, forward_block(): pl.pallas_call(partial(forward_kernel, layout=layout, half=3 * width // 2...  25.4 us
    all_to_all x4, starting transfers between devices, along(): lax.all_to_all(value, AXES, 0, 0, axis_index_groups=self.lines, tiled=True)  20.1 us
    ppermute x6, waiting for transfers between devices, over(): return lax.ppermute(value, 'wide', [(i, i ^ 1) for i in range(self.wide)])  15.4 us
    pallas_call x1, Pallas kernels, place_rows(): pl.pallas_call(out_kernel, grid_spec=pltpu.PrefetchScalarGridSpec(num_sca...  13.5 us
    pallas_call x1, Pallas kernels, gather_rows(): pl.pallas_call(gather_kernel, grid=(seqs,), in_specs=[pl.BlockSpec((1, sl...  12.6 us
  transfers between devices with their start and end apart: 37, of which 12 were waited for; matrix products, arithmetic and copies ran while one was open for 8% of the time, Pallas kernels for 59%

profile of v1, /device:TPU:0, one launch (start us, length us, event | category | flops | bytes accessed | tf_op | source)
XLA Modules:
  0.0 291.5 jit_solution(5218292978026540058)
XLA Ops:
  1.6 0.9 reshape.70
  4.8 0.9 broadcast_in_dim.32
  5.7 6.4 %all-to-all-start = ((bf16[8,24,1664]{2,1,0:T(8,128)(2,1)}), bf16[8,24,1664]{2,1,0:T(8,128)(2,1)}, u32[]{:S(2)}, u32[]{:S(2)}) async-start(bf16[8,24,1664]{2,1,0:T(8,128)(2,1)} %bitcast.11), calls=%async_computation | async-start | bytes 1277952 | tf_op jit(solution)/shard_map/all_to_all | solution.py:711
  12.8 1.1 broadcast_in_dim.33
  14.0 1.0 copy.33.target
  16.8 12.6 %gather_rows.1 = (bf16[1024,768]{1,0:T(8,128)(2,1)}, bf16[1024,768]{1,0:T(8,128)(2,1)}) custom-call(s32[4,256,1]{2,1,0:T(8,128)} %copy.33.target, bf16[4,2048,768]{2,1,0:T(8,128)(2,1)} %x.5, bf16[4,2048,768]{2,1,0:T(8,128)(2,1)} %x.7), custom_call_target="tpu_custom_call" | custom-call | flops 6442450944 | bytes 25165824 | tf_op jit(solution)/shard_map/gather_rows/pallas_call | solution.py:101
  30.1 4.4 %all-to-all-start.1 = ((bf16[8,24,3072]{2,1,0:T(8,128)(2,1)}), bf16[8,24,3072]{2,1,0:T(8,128)(2,1)S(1)}, u32[]{:S(2)}, u32[]{:S(2)}) async-start(bf16[8,24,3072]{2,1,0:T(8,128)(2,1)} %bitcast.70), calls=%async_computation.1 | async-start | bytes 2359296 | tf_op jit(solution)/shard_map/all_to_all | solution.py:711
  34.5 1.5 collective-permute-start.1
  36.0 1.5 collective-permute-start
  37.5 14.0 %collective-permute-done.1.rest_2_ = bf16[192,1664]{1,0:T(8,128)(2,1)S(1)} collective-permute-done((bf16[192,1664]{1,0:T(8,128)(2,1)}, bf16[192,1664]{1,0:T(8,128)(2,1)S(1)}, u32[]{:S(2)}, u32[]{:S(2)}) %collective-permute-start.1) | collective-permute-done | bytes 639008 | tf_op jit(solution)/shard_map/ppermute | solution.py:706
  51.5 1.6 collective-permute-start.2
  53.1 1.6 collective-permute-start.3
  55.2 5.5 %collective-permute-done.2.rest_3_ = bf16[96,1664]{1,0:T(8,128)(2,1)S(1)} collective-permute-done((bf16[96,1664]{1,0:T(8,128)(2,1)S(1)}, bf16[96,1664]{1,0:T(8,128)(2,1)S(1)}, u32[]{:S(2)}, u32[]{:S(2)}) %collective-permute-start.2) | collective-permute-done | bytes 319520 | tf_op jit(solution)/shard_map/ppermute | solution.py:704
  60.7 1.4 collective-permute-done.3.rest_4_
  62.4 1.6 collective-permute-done.8.rest_9_
  64.1 1.1 fusion.1
  65.2 1.4 collective-permute-start.12
  66.6 1.5 collective-permute-start.13
  69.4 25.4 %forward_block.1 = (bf16[1024,2304]{1,0:T(8,128)(2,1)}, bf16[1024,768]{1,0:T(8,128)(2,1)}, f32[1024,768]{1,0:T(8,128)}, bf16[1024,768]{1,0:T(8,128)(2,1)}, bf16[...) custom-call(s32[2]{0:T(128)} %pad_add_fusion.1.where, ...), custom_call_target="tpu_custom_call" | custom-call | flops 6039797760 | bytes 23592960 | tf_op jit(solution)/shard_map/forward_block/pallas_call | solution.py:258
  95.9 1.5 collective-permute-start.10
  97.4 2.0 collective-permute-start.11
  100.2 25.8 %mlp_part.2 = (bf16[1024,768]{1,0:T(8,128)(2,1)}, bf16[1024,768]{1,0:T(8,128)(2,1)}, bf16[768,1536]{1,0:T(8,128)(2,1)}, bf16[768,1536]{1,0:T(8,128)(2,1)}, f32[1,1536]{1,0:T(1,128)}) custom-call(s32[2]{0:T(128)} %pad_add_fusion.1.where, f32[1,3072]{1,0:T(1,128)} %get-tuple-element.124.bias, bf16[1024,768]{1,0:T(8,128)(2,1)} %get-tuple-element.136.rest_0_, ...), custom_call_target="tpu_custom_call" | custom-call | flops 14495514624 | bytes 6291456 | tf_op jit(solution)/shard_map/mlp_part/pallas_call | solution.py:384
  127.6 1.3 collective-permute-done.19.rest_8_
  131.4 26.0 %mlp_part.3 = (bf16[1024,768]{1,0:T(8,128)(2,1)}, bf16[1024,768]{1,0:T(8,128)(2,1)}, bf16[768,1536]{1,0:T(8,128)(2,1)}, bf16[768,1536]{1,0:T(8,128)(2,1)}, f32[1,1536]{1,0:T(1,128)}) custom-call(s32[2]{0:T(128)} %pad_add_fusion.1.where, f32[1,3072]{1,0:T(1,128)} %get-tuple-element.124.bias, bf16[1024,768]{1,0:T(8,128)(2,1)} %get-tuple-element.136.rest_0_, ...), custom_call_target="tpu_custom_call" | custom-call | flops 14495514624 | bytes 6291456 | tf_op jit(solution)/shard_map/mlp_part/pallas_call | solution.py:384
  157.6 3.5 %add_convert_fusion.8 = (bf16[192,1536]{1,0:T(8,128)(2,1)}, bf16[192,1536]{1,0:T(8,128)(2,1)}, bf16[192,1536]{1,0:T(8,128)(2,1)}) fusion(bf16[768,1536]{1,0:T(8,128)(2,1)} %collective-permute-done.24, s32[]{:T(128)S(6)} %select_n.52, bf16[768,1536]{1,0:T(8,128)(2,1)} %get-tuple-element.151, s32[]{:T(128)S(6)} %select_n.51, s32[]{:T(128)S(6)} %select_n.50), kind=kLoop, calls=%fused_computation.11 | loop fusion | flops 3538944 | bytes 5308428 | tf_op jit(solution)/shard_map/convert_element_type | solution.py:767
  161.1 1.3 collective-permute-start.25
  163.0 1.6 collective-permute-start.27
  164.6 2.0 add_convert_fusion
  166.6 4.5 %all-to-all-start.2 = ((bf16[4,192,1536]{2,1,0:T(8,128)(2,1)}), bf16[4,192,1536]{2,1,0:T(8,128)(2,1)}, u32[]{:S(2)}, u32[]{:S(2)}) async-start(bf16[4,192,1536]{2,1,0:T(8,128)(2,1)} %bitcast.22), calls=%async_computation.2 | async-start | bytes 4718592 | tf_op jit(solution)/shard_map/all_to_all | solution.py:741
  171.1 28.2 %backward_block.1 = (bf16[1024,2304]{1,0:T(8,128)(2,1)}, bf16[768,1024]{1,0:T(8,128)(2,1)}, f32[1024,768]{1,0:T(8,128)}, bf16[1024,768]{1,0:T(8,128)(2,1)}, f32[1,768]{1,0:T(1,128)}) custom-call(s32[2]{0:T(128)} %pad_add_fusion.1.where, s32[4]{0:T(128)} %copy-done.13, bf16[1024,768]{1,0:T(8,128)(2,1)} %get-tuple-element.107.sel, ...), custom_call_target="tpu_custom_call" | custom-call | flops 24159191040 | bytes 47185920 | tf_op jit(solution)/shard_map/backward_block/pallas_call | solution.py:508
  199.4 12.5 %project_grads.1 = (bf16[768,1664]{1,0:T(8,128)(2,1)}, bf16[768,1664]{1,0:T(8,128)(2,1)}) custom-call(s32[2]{0:T(128)} %pad_add_fusion.1.where, bf16[768,1024]{1,0:T(8,128)(2,1)} %get-tuple-element.154.n1t, bf16[768,1024]{1,0:T(8,128)(2,1)} %get-tuple-element.155.dattnt, bf16[1024,2304]{1,0:T(8,128)(2,1)} %get-tuple-element.156.dqkv, ...), custom_call_target="tpu_custom_call" | custom-call | flops 10468982784 | bytes 6291456 | tf_op jit(solution)/shard_map/project_grads/pallas_call | solution.py:576
  211.8 4.2 %all-to-all-done.2 = bf16[4,192,1536]{2,1,0:T(8,128)(2,1)} async-done(((bf16[4,192,1536]{2,1,0:T(8,128)(2,1)}), bf16[4,192,1536]{2,1,0:T(8,128)(2,1)}, u32[]{:S(2)}, u32[]{:S(2)}) %all-to-all-start.2) | async-done | bytes 2359328 | tf_op jit(solution)/shard_map/all_to_all | solution.py:741
  216.0 1.9 add_convert_fusion.6
  217.9 2.3 add_convert_fusion.7
  220.2 1.2 pad_maximum_fusion
  221.4 2.0 add_convert_fusion.2
  223.3 4.3 %all-to-all-start.3 = ((bf16[8,24,3072]{2,1,0:T(8,128)(2,1)}), bf16[8,24,3072]{2,1,0:T(8,128)(2,1)}, u32[]{:S(2)}, u32[]{:S(2)}) async-start(bf16[8,24,3072]{2,1,0:T(8,128)(2,1)} %bitcast.24), calls=%async_computation.3 | async-start | bytes 2359296 | tf_op jit(solution)/shard_map/all_to_all | solution.py:711
  227.6 0.9 collective-permute-start.29
  228.5 1.0 collective-permute-start.30
  229.5 1.7 collective-permute-start.31
  231.2 13.5 %place_rows.1 = bf16[4,2048,768]{2,1,0:T(8,128)(2,1)} custom-call(s32[2,4]{1,0:T(2,128)} %pad_add_fusion.runs, bf16[1024,768]{1,0:T(8,128)(2,1)} %get-tuple-element.170.rows, s32[4,1,256]{2,1,0:T(1,128)} %broadcast_in_dim.36.target, bf16[4,2048,768]{2,1,0:T(8,128)(2,1)} %x.5), custom_call_target="tpu_custom_call" | custom-call | flops 3221225472 | bytes 25165824 | tf_op jit(solution)/shard_map/place_rows/pallas_call | solution.py:621
  244.7 14.3 %input_rows.2.rest_10_ = bf16[4,2048,768]{2,1,0:T(8,128)(2,1)} custom-call(s32[2]{0:T(128)} %pad_add_fusion.1.where, s32[2,4]{1,0:T(2,128)} %pad_add_fusion.runs, bf16[1024,768]{1,0:T(8,128)(2,1)} %get-tuple-element.107.sel, bf16[1024,768]{1,0:T(8,128)(2,1)} %get-tuple-element.108.grad, f32[8,768]{1,0:T(8,128)} %get-tuple-element.119.vec, ...), custom_call_target="tpu_custom_call" | custom-call | flops 1 | bytes 1 | tf_op jit(solution)/shard_map/input_rows/pallas_call | solution.py:667
  259.0 2.9 add_convert_fusion.1
  261.9 4.9 %all-to-all-start.4 = ((bf16[8,24,1664]{2,1,0:T(8,128)(2,1)}), bf16[8,24,1664]{2,1,0:T(8,128)(2,1)}, u32[]{:S(2)}, u32[]{:S(2)}) async-start(bf16[8,24,1664]{2,1,0:T(8,128)(2,1)} %bitcast.26), calls=%async_computation.4 | async-start | bytes 1277952 | tf_op jit(solution)/shard_map/all_to_all | solution.py:711
  266.9 2.3 convert_reduce_fusion
  269.2 14.3 %input_rows.3 = bf16[4,2048,768]{2,1,0:T(8,128)(2,1)} custom-call(s32[2]{0:T(128)} %pad_add_fusion.1.where, s32[2,4]{1,0:T(2,128)} %pad_add_fusion.runs, bf16[1024,768]{1,0:T(8,128)(2,1)} %get-tuple-element.107.sel, bf16[1024,768]{1,0:T(8,128)(2,1)} %get-tuple-element.108.grad, f32[8,768]{1,0:T(8,128)} %get-tuple-element.119.vec, ...), custom_call_target="tpu_custom_call", output_to_operand_aliasing={{}: (20, {})} | custom-call | flops 1 | bytes 1 | tf_op jit(solution)/shard_map/input_rows/pallas_call | solution.py:667
  283.6 1.2 slice_bitcast_fusion.3
  286.9 1.2 convert_reduce_fusion.1
  (127 shorter events, 20.7 us)
Async XLA Ops:
  4.8 7.4 %copy-start.14 = (s32[4]{0:T(128)S(1)}, s32[4]{0:T(128)}, u32[]{:S(2)}) copy-start(s32[4]{0:T(128)} %param.15) | copy-start | bytes 52
  4.8 7.4 %copy-start.12 = (s32[4,256]{1,0:T(4,128)S(1)}, s32[4,256]{1,0:T(4,128)}, u32[]{:S(2)}) copy-start(s32[4,256]{1,0:T(4,128)} %param.17) | copy-start | bytes 12292
  4.8 7.6 %copy-start.7 = (bf16[24,3072]{1,0:T(8,128)(2,1)S(1)}, bf16[24,3072]{1,0:T(8,128)(2,1)}, u32[]{:S(2)}) copy-start(bf16[24,3072]{1,0:T(8,128)(2,1)} %param.22) | copy-start | bytes 442372
  4.8 7.5 %copy-start.10 = (bf16[3072,24]{0,1:T(8,128)(2,1)S(1)}, bf16[3072,24]{0,1:T(8,128)(2,1)}, u32[]{:S(2)}) copy-start(bf16[3072,24]{0,1:T(8,128)(2,1)} %param.24) | copy-start | bytes 442372
  5.7 24.3 %all-to-all-start = ((bf16[8,24,1664]{2,1,0:T(8,128)(2,1)}), bf16[8,24,1664]{2,1,0:T(8,128)(2,1)}, u32[]{:S(2)}, u32[]{:S(2)}) async-start(bf16[8,24,1664]{2,1,0:T(8,128)(2,1)} %bitcast.11), calls=%async_computation | async-start | bytes 1277952 | tf_op jit(solution)/shard_map/all_to_all | solution.py:711
  12.8 2.8 copy-start.11
  30.1 34.0 %all-to-all-start.1 = ((bf16[8,24,3072]{2,1,0:T(8,128)(2,1)}), bf16[8,24,3072]{2,1,0:T(8,128)(2,1)S(1)}, u32[]{:S(2)}, u32[]{:S(2)}) async-start(bf16[8,24,3072]{2,1,0:T(8,128)(2,1)} %bitcast.70), calls=%async_computation.1 | async-start | bytes 2359296 | tf_op jit(solution)/shard_map/all_to_all | solution.py:711
  34.5 17.0 %collective-permute-start.1 = (bf16[192,1664]{1,0:T(8,128)(2,1)}, bf16[192,1664]{1,0:T(8,128)(2,1)S(1)}, u32[]{:S(2)}, u32[]{:S(2)}) collective-permute-start(bf16[192,1664]{1,0:T(8,128)(2,1)} %bitcast.12.rest_0_), channel_id=1, source_target_pairs={{0,4},{4,0},{8,12},{12,8},{16,20},{20,16},{24,28},{28,24},{1,5},{5... | collective-permute-start | bytes 1916936 | tf_op jit(solution)/shard_map/ppermute | solution.py:706
  36.0 17.1 %collective-permute-start = (bf16[192,1664]{1,0:T(8,128)(2,1)}, bf16[192,1664]{1,0:T(8,128)(2,1)S(1)}, u32[]{:S(2)}, u32[]{:S(2)}) collective-permute-start(bf16[192,1664]{1,0:T(8,128)(2,1)} %bitcast.12.rest_0_), channel_id=1, source_target_pairs={{0,2},{1,3},{2,0},{3,1},{4,6},{5,7},{6,4},{7,5},{8,10},{9,11},{10,... | collective-permute-start | bytes 1916936 | tf_op jit(solution)/shard_map/ppermute | solution.py:704
  37.5 24.6 %collective-permute-start.4 = (bf16[192,1664]{1,0:T(8,128)(2,1)}, bf16[192,1664]{1,0:T(8,128)(2,1)S(1)}, u32[]{:S(2)}, u32[]{:S(2)}) collective-permute-start(bf16[192,1664]{1,0:T(8,128)(2,1)} %bitcast.12.rest_0_), channel_id=1, source_target_pairs={{0,1},{1,0},{2,3},{3,2},{4,5},{5,4},{6,7},{7,6},{8,9},{9,8},{10,11... | collective-permute-start | bytes 1916936 | tf_op jit(solution)/shard_map/ppermute | solution.py:700
  51.5 13.7 %copy-start = (bf16[192,1664]{1,0:T(8,128)(2,1)}, bf16[192,1664]{1,0:T(8,128)(2,1)S(1)}, u32[]{:S(2)}) copy-start(bf16[192,1664]{1,0:T(8,128)(2,1)S(1)} %collective-permute-done.1.rest_2_) | copy-start | bytes 1916932
  51.5 9.2 %collective-permute-start.2 = (bf16[96,1664]{1,0:T(8,128)(2,1)S(1)}, bf16[96,1664]{1,0:T(8,128)(2,1)S(1)}, u32[]{:S(2)}, u32[]{:S(2)}) collective-permute-start(bf16[96,1664]{1,0:T(8,128)(2,1)S(1)} %slice.159), channel_id=1, source_target_pairs={{0,2},{1,3},{2,0},{3,1},{4,6},{5,7},{6,4},{7,5},{8,10},{9,11},{10,... | collective-permute-start | bytes 958472 | tf_op jit(solution)/shard_map/ppermute | solution.py:704
  53.1 12.1 %copy-start.1 = (bf16[192,1664]{1,0:T(8,128)(2,1)}, bf16[192,1664]{1,0:T(8,128)(2,1)S(1)}, u32[]{:S(2)}) copy-start(bf16[192,1664]{1,0:T(8,128)(2,1)S(1)} %collective-permute-done.rest_1_) | copy-start | bytes 1916932
  53.1 9.0 %collective-permute-start.3 = (bf16[96,1664]{1,0:T(8,128)(2,1)S(1)}, bf16[96,1664]{1,0:T(8,128)(2,1)}, u32[]{:S(2)}, u32[]{:S(2)}) collective-permute-start(bf16[96,1664]{1,0:T(8,128)(2,1)S(1)} %slice.160), channel_id=1, source_target_pairs={{0,4},{4,0},{8,12},{12,8},{16,20},{20,16},{24,28},{28,24},{1,5},{5... | collective-permute-start | bytes 958472 | tf_op jit(solution)/shard_map/ppermute | solution.py:706
  54.7 9.4 %collective-permute-start.5 = (bf16[192,1664]{1,0:T(8,128)(2,1)S(1)}, bf16[192,1664]{1,0:T(8,128)(2,1)}, u32[]{:S(2)}, u32[]{:S(2)}) collective-permute-start(bf16[192,1664]{1,0:T(8,128)(2,1)S(1)} %collective-permute-done.rest_1_), channel_id=1, source_target_pairs={{0,1},{1,0},{2,3},{3,2},{4,5},{5,4},{6,7},{7,6},{8,9},{9,8},{10,11... | collective-permute-start | bytes 1916936 | tf_op jit(solution)/shard_map/ppermute | solution.py:700
  54.7 9.4 %collective-permute-start.6 = (bf16[192,1664]{1,0:T(8,128)(2,1)S(1)}, bf16[192,1664]{1,0:T(8,128)(2,1)}, u32[]{:S(2)}, u32[]{:S(2)}) collective-permute-start(bf16[192,1664]{1,0:T(8,128)(2,1)S(1)} %collective-permute-done.1.rest_2_), channel_id=1, source_target_pairs={{0,1},{1,0},{2,3},{3,2},{4,5},{5,4},{6,7},{7,6},{8,9},{9,8},{10,11... | collective-permute-start | bytes 1916936 | tf_op jit(solution)/shard_map/ppermute | solution.py:700
  60.7 5.9 %copy-start.5 = (bf16[96,1664]{1,0:T(8,128)(2,1)}, bf16[96,1664]{1,0:T(8,128)(2,1)S(1)}, u32[]{:S(2)}) copy-start(bf16[96,1664]{1,0:T(8,128)(2,1)S(1)} %collective-permute-done.2.rest_3_) | copy-start | bytes 958468
  60.7 1.7 collective-permute-start.7
  62.1 2.0 collective-permute-start.8
  62.1 3.1 %copy-start.3 = (bf16[192,1664]{1,0:T(8,128)(2,1)}, bf16[192,1664]{1,0:T(8,128)(2,1)S(1)}, u32[]{:S(2)}) copy-start(bf16[192,1664]{1,0:T(8,128)(2,1)S(1)} %collective-permute-done.4.rest_5_) | copy-start | bytes 1916932
  65.2 29.6 %collective-permute-start.12 = (bf16[192,1536]{1,0:T(8,128)(2,1)}, bf16[192,1536]{1,0:T(8,128)(2,1)}, u32[]{:S(2)}, u32[]{:S(2)}) collective-permute-start(bf16[192,1536]{1,0:T(8,128)(2,1)} %get-tuple-element.130.rest_4_), channel_id=1, source_target_pairs={{0,2},{1,3},{2,0},{3,1},{4,6},{5,7},{6,4},{7,5},{8,10},{9,11},{10,... | collective-permute-start | bytes 1769480 | tf_op jit(solution)/shard_map/ppermute | solution.py:704
  66.6 28.2 %collective-permute-start.13 = (bf16[192,1536]{1,0:T(8,128)(2,1)}, bf16[192,1536]{1,0:T(8,128)(2,1)}, u32[]{:S(2)}, u32[]{:S(2)}) collective-permute-start(bf16[192,1536]{1,0:T(8,128)(2,1)} %get-tuple-element.130.rest_4_), channel_id=1, source_target_pairs={{0,4},{4,0},{8,12},{12,8},{16,20},{20,16},{24,28},{28,24},{1,5},{5... | collective-permute-start | bytes 1769480 | tf_op jit(solution)/shard_map/ppermute | solution.py:706
  68.1 26.7 %collective-permute-start.14 = (bf16[192,1536]{1,0:T(8,128)(2,1)}, bf16[192,1536]{1,0:T(8,128)(2,1)}, u32[]{:S(2)}, u32[]{:S(2)}) collective-permute-start(bf16[192,1536]{1,0:T(8,128)(2,1)} %get-tuple-element.130.rest_4_), channel_id=1, source_target_pairs={{0,6},{1,7},{2,4},{3,5},{4,2},{5,3},{6,0},{7,1},{8,14},{9,15},{10,... | collective-permute-start | bytes 1769480 | tf_op jit(solution)/shard_map/ppermute | solution.py:708
  94.8 2.6 collective-permute-start.15
  94.9 4.6 %collective-permute-start.16 = (bf16[192,1536]{1,0:T(8,128)(2,1)}, bf16[192,1536]{1,0:T(8,128)(2,1)}, u32[]{:S(2)}, u32[]{:S(2)}) collective-permute-start(bf16[192,1536]{1,0:T(8,128)(2,1)} %collective-permute-done.12.rest_5_), channel_id=1, source_target_pairs={{0,1},{1,0},{2,3},{3,2},{4,5},{5,4},{6,7},{7,6},{8,9},{9,8},{10,11... | collective-permute-start | bytes 1769480 | tf_op jit(solution)/shard_map/ppermute | solution.py:700
  95.4 4.8 %collective-permute-start.17 = (bf16[192,1536]{1,0:T(8,128)(2,1)}, bf16[192,1536]{1,0:T(8,128)(2,1)}, u32[]{:S(2)}, u32[]{:S(2)}) collective-permute-start(bf16[192,1536]{1,0:T(8,128)(2,1)} %collective-permute-done.13.rest_6_), channel_id=1, source_target_pairs={{0,1},{1,0},{2,3},{3,2},{4,5},{5,4},{6,7},{7,6},{8,9},{9,8},{10,11... | collective-permute-start | bytes 1769480 | tf_op jit(solution)/shard_map/ppermute | solution.py:700
  95.5 4.7 %collective-permute-start.18 = (bf16[192,1536]{1,0:T(8,128)(2,1)}, bf16[192,1536]{1,0:T(8,128)(2,1)}, u32[]{:S(2)}, u32[]{:S(2)}) collective-permute-start(bf16[192,1536]{1,0:T(8,128)(2,1)} %collective-permute-done.14.rest_7_), channel_id=1, source_target_pairs={{0,1},{1,0},{2,3},{3,2},{4,5},{5,4},{6,7},{7,6},{8,9},{9,8},{10,11... | collective-permute-start | bytes 1769480 | tf_op jit(solution)/shard_map/ppermute | solution.py:700
  95.9 30.1 %collective-permute-start.10 = (bf16[192,1536]{1,0:T(8,128)(2,1)}, bf16[192,1536]{1,0:T(8,128)(2,1)}, u32[]{:S(2)}, u32[]{:S(2)}) collective-permute-start(bf16[192,1536]{1,0:T(8,128)(2,1)} %get-tuple-element.137.rest_4_), channel_id=1, source_target_pairs={{0,4},{4,0},{8,12},{12,8},{16,20},{20,16},{24,28},{28,24},{1,5},{5... | collective-permute-start | bytes 1769480 | tf_op jit(solution)/shard_map/ppermute | solution.py:706
  97.4 28.6 %collective-permute-start.11 = (bf16[192,1536]{1,0:T(8,128)(2,1)}, bf16[192,1536]{1,0:T(8,128)(2,1)}, u32[]{:S(2)}, u32[]{:S(2)}) collective-permute-start(bf16[192,1536]{1,0:T(8,128)(2,1)} %get-tuple-element.137.rest_4_), channel_id=1, source_target_pairs={{0,6},{1,7},{2,4},{3,5},{4,2},{5,3},{6,0},{7,1},{8,14},{9,15},{10,... | collective-permute-start | bytes 1769480 | tf_op jit(solution)/shard_map/ppermute | solution.py:708
  99.4 27.1 %collective-permute-start.9 = (bf16[192,1536]{1,0:T(8,128)(2,1)}, bf16[192,1536]{1,0:T(8,128)(2,1)}, u32[]{:S(2)}, u32[]{:S(2)}) collective-permute-start(bf16[192,1536]{1,0:T(8,128)(2,1)} %get-tuple-element.137.rest_4_), channel_id=1, source_target_pairs={{0,2},{1,3},{2,0},{3,1},{4,6},{5,7},{6,4},{7,5},{8,10},{9,11},{10,... | collective-permute-start | bytes 1769480 | tf_op jit(solution)/shard_map/ppermute | solution.py:704
  126.5 2.3 collective-permute-start.19
  126.5 3.2 %collective-permute-start.20 = (bf16[192,1536]{1,0:T(8,128)(2,1)}, bf16[192,1536]{1,0:T(8,128)(2,1)}, u32[]{:S(2)}, u32[]{:S(2)}) collective-permute-start(bf16[192,1536]{1,0:T(8,128)(2,1)} %collective-permute-done.9.rest_5_), channel_id=1, source_target_pairs={{0,1},{1,0},{2,3},{3,2},{4,5},{5,4},{6,7},{7,6},{8,9},{9,8},{10,11... | collective-permute-start | bytes 1769480 | tf_op jit(solution)/shard_map/ppermute | solution.py:700
  127.0 3.5 %collective-permute-start.21 = (bf16[192,1536]{1,0:T(8,128)(2,1)}, bf16[192,1536]{1,0:T(8,128)(2,1)}, u32[]{:S(2)}, u32[]{:S(2)}) collective-permute-start(bf16[192,1536]{1,0:T(8,128)(2,1)} %collective-permute-done.10.rest_6_), channel_id=1, source_target_pairs={{0,1},{1,0},{2,3},{3,2},{4,5},{5,4},{6,7},{7,6},{8,9},{9,8},{10,11... | collective-permute-start | bytes 1769480 | tf_op jit(solution)/shard_map/ppermute | solution.py:700
  127.0 4.4 %collective-permute-start.22 = (bf16[192,1536]{1,0:T(8,128)(2,1)}, bf16[192,1536]{1,0:T(8,128)(2,1)}, u32[]{:S(2)}, u32[]{:S(2)}) collective-permute-start(bf16[192,1536]{1,0:T(8,128)(2,1)} %collective-permute-done.11.rest_7_), channel_id=1, source_target_pairs={{0,1},{1,0},{2,3},{3,2},{4,5},{5,4},{6,7},{7,6},{8,9},{9,8},{10,11... | collective-permute-start | bytes 1769480 | tf_op jit(solution)/shard_map/ppermute | solution.py:700
  127.6 30.1 %collective-permute-start.24 = (bf16[768,1536]{1,0:T(8,128)(2,1)}, bf16[768,1536]{1,0:T(8,128)(2,1)}, u32[]{:S(2)}, u32[]{:S(2)}) collective-permute-start(bf16[768,1536]{1,0:T(8,128)(2,1)} %get-tuple-element.143), channel_id=1, source_target_pairs={{0,1},{1,0},{2,3},{3,2},{4,5},{5,4},{6,7},{7,6},{8,9},{9,8},{10,11... | collective-permute-start | bytes 7077896 | tf_op jit(solution)/shard_map/ppermute | solution.py:700
  157.4 7.2 %collective-permute-start.23 = (bf16[768,1536]{1,0:T(8,128)(2,1)}, bf16[768,1536]{1,0:T(8,128)(2,1)S(1)}, u32[]{:S(2)}, u32[]{:S(2)}) collective-permute-start(bf16[768,1536]{1,0:T(8,128)(2,1)} %get-tuple-element.142), channel_id=1, source_target_pairs={{0,1},{1,0},{2,3},{3,2},{4,5},{5,4},{6,7},{7,6},{8,9},{9,8},{10,11... | collective-permute-start | bytes 7077896 | tf_op jit(solution)/shard_map/ppermute | solution.py:700
  157.6 7.0 %copy-start.4 = (bf16[768,1536]{1,0:T(8,128)(2,1)S(1)}, bf16[768,1536]{1,0:T(8,128)(2,1)}, u32[]{:S(2)}) copy-start(bf16[768,1536]{1,0:T(8,128)(2,1)} %get-tuple-element.141) | copy-start | bytes 7077892
  161.1 50.7 %collective-permute-start.25 = (bf16[192,1536]{1,0:T(8,128)(2,1)}, bf16[192,1536]{1,0:T(8,128)(2,1)}, u32[]{:S(2)}, u32[]{:S(2)}) collective-permute-start(bf16[192,1536]{1,0:T(8,128)(2,1)} %get-tuple-element.193), channel_id=1, source_target_pairs={{0,2},{1,3},{2,0},{3,1},{4,6},{5,7},{6,4},{7,5},{8,10},{9,11},{10,... | collective-permute-start | bytes 1769480 | tf_op jit(solution)/shard_map/ppermute | solution.py:704
  162.4 49.4 %collective-permute-start.26 = (bf16[192,1536]{1,0:T(8,128)(2,1)}, bf16[192,1536]{1,0:T(8,128)(2,1)}, u32[]{:S(2)}, u32[]{:S(2)}) collective-permute-start(bf16[192,1536]{1,0:T(8,128)(2,1)} %get-tuple-element.192), channel_id=1, source_target_pairs={{0,4},{4,0},{8,12},{12,8},{16,20},{20,16},{24,28},{28,24},{1,5},{5... | collective-permute-start | bytes 1769480 | tf_op jit(solution)/shard_map/ppermute | solution.py:706
  163.0 48.8 %collective-permute-start.27 = (bf16[192,1536]{1,0:T(8,128)(2,1)}, bf16[192,1536]{1,0:T(8,128)(2,1)}, u32[]{:S(2)}, u32[]{:S(2)}) collective-permute-start(bf16[192,1536]{1,0:T(8,128)(2,1)} %get-tuple-element.191), channel_id=1, source_target_pairs={{0,6},{1,7},{2,4},{3,5},{4,2},{5,3},{6,0},{7,1},{8,14},{9,15},{10,... | collective-permute-start | bytes 1769480 | tf_op jit(solution)/shard_map/ppermute | solution.py:708
  166.6 49.4 %all-to-all-start.2 = ((bf16[4,192,1536]{2,1,0:T(8,128)(2,1)}), bf16[4,192,1536]{2,1,0:T(8,128)(2,1)}, u32[]{:S(2)}, u32[]{:S(2)}) async-start(bf16[4,192,1536]{2,1,0:T(8,128)(2,1)} %bitcast.22), calls=%async_computation.2 | async-start | bytes 4718592 | tf_op jit(solution)/shard_map/all_to_all | solution.py:741
  216.0 5.4 %collective-permute-start.28 = (bf16[768,1664]{1,0:T(8,128)(2,1)}, bf16[768,1664]{1,0:T(8,128)(2,1)S(1)}, u32[]{:S(2)}, u32[]{:S(2)}) collective-permute-start(bf16[768,1664]{1,0:T(8,128)(2,1)} %get-tuple-element.168), channel_id=1, source_target_pairs={{0,1},{1,0},{2,3},{3,2},{4,5},{5,4},{6,7},{7,6},{8,9},{9,8},{10,11... | collective-permute-start | bytes 7667720 | tf_op jit(solution)/shard_map/ppermute | solution.py:700
  217.9 3.5 %copy-start.2 = (bf16[768,1664]{1,0:T(8,128)(2,1)S(1)}, bf16[768,1664]{1,0:T(8,128)(2,1)}, u32[]{:S(2)}) copy-start(bf16[768,1664]{1,0:T(8,128)(2,1)} %get-tuple-element.167) | copy-start | bytes 7667716
  223.3 38.6 %all-to-all-start.3 = ((bf16[8,24,3072]{2,1,0:T(8,128)(2,1)}), bf16[8,24,3072]{2,1,0:T(8,128)(2,1)}, u32[]{:S(2)}, u32[]{:S(2)}) async-start(bf16[8,24,3072]{2,1,0:T(8,128)(2,1)} %bitcast.24), calls=%async_computation.3 | async-start | bytes 2359296 | tf_op jit(solution)/shard_map/all_to_all | solution.py:711
  227.6 31.4 %collective-permute-start.29 = (bf16[192,1664]{1,0:T(8,128)(2,1)}, bf16[192,1664]{1,0:T(8,128)(2,1)}, u32[]{:S(2)}, u32[]{:S(2)}) collective-permute-start(bf16[192,1664]{1,0:T(8,128)(2,1)} %get-tuple-element.175), channel_id=1, source_target_pairs={{0,2},{1,3},{2,0},{3,1},{4,6},{5,7},{6,4},{7,5},{8,10},{9,11},{10,... | collective-permute-start | bytes 1916936 | tf_op jit(solution)/shard_map/ppermute | solution.py:704
  228.5 30.5 %collective-permute-start.30 = (bf16[192,1664]{1,0:T(8,128)(2,1)}, bf16[192,1664]{1,0:T(8,128)(2,1)}, u32[]{:S(2)}, u32[]{:S(2)}) collective-permute-start(bf16[192,1664]{1,0:T(8,128)(2,1)} %get-tuple-element.176), channel_id=1, source_target_pairs={{0,4},{4,0},{8,12},{12,8},{16,20},{20,16},{24,28},{28,24},{1,5},{5... | collective-permute-start | bytes 1916936 | tf_op jit(solution)/shard_map/ppermute | solution.py:706
  229.5 29.6 %collective-permute-start.31 = (bf16[192,1664]{1,0:T(8,128)(2,1)}, bf16[192,1664]{1,0:T(8,128)(2,1)}, u32[]{:S(2)}, u32[]{:S(2)}) collective-permute-start(bf16[192,1664]{1,0:T(8,128)(2,1)} %get-tuple-element.177), channel_id=1, source_target_pairs={{0,6},{1,7},{2,4},{3,5},{4,2},{5,3},{6,0},{7,1},{8,14},{9,15},{10,... | collective-permute-start | bytes 1916936 | tf_op jit(solution)/shard_map/ppermute | solution.py:708
  261.9 25.0 %all-to-all-start.4 = ((bf16[8,24,1664]{2,1,0:T(8,128)(2,1)}), bf16[8,24,1664]{2,1,0:T(8,128)(2,1)}, u32[]{:S(2)}, u32[]{:S(2)}) async-start(bf16[8,24,1664]{2,1,0:T(8,128)(2,1)} %bitcast.26), calls=%async_computation.4 | async-start | bytes 1277952 | tf_op jit(solution)/shard_map/all_to_all | solution.py:711
  (6 other events, 8.3 us)

commit v2 on v1

--- a/solution.py
+++ b/solution.py
@@ -134,13 +134,13 @@
     return jnp.where(lane < HEAD_DIM, stacked[:half], stacked[half:])
 
 
-def pair_loop(pairs, body, carry):
+def pair_loop(pairs, body, carry, at_once=PAIRS):
     def step(k, carry):
-        for p in range(PAIRS):
-            carry = body(k * PAIRS + p, carry)
+        for p in range(at_once):
+            carry = body(k * at_once + p, carry)
         return carry
 
-    return lax.fori_loop(0, pairs // PAIRS, step, carry)
+    return lax.fori_loop(0, pairs // at_once, step, carry)
 
 
 def pair_columns(pair, half_width):
@@ -231,7 +231,7 @@
         kept = jnp.where(lane == LSE_LANE + 2 * pair, lse[:slots], kept)
         return jnp.where(lane == LSE_LANE + 2 * pair + 1, lse[slots:], kept)
 
-    kept = pair_loop(width // (2 * HEAD_DIM), attend, kept)
+    kept = pair_loop(width // (2 * HEAD_DIM), attend, kept, 2 * PAIRS)
 
     @pl.when(b == 0)
     def _():
@@ -955,9 +955,9 @@
     down_grad = jnp.concatenate(
         [v[side, :, tile:] for side in (0, 1) for v in (one, two)], axis=1
     ).T
-    in_grad = jnp.stack(
-        [proj[side, :, :half].reshape(shard, 3, third) for side in (0, 1)], axis=2
-    ).reshape(shard, in_width)
+    in_grad = jnp.concatenate(
+        [proj[side, :, k * third : (k + 1) * third] for k in range(3) for side in (0, 1)], axis=1
+    )
     out_grad = jnp.concatenate([proj[side, :, half : half + third] for side in (0, 1)], axis=1).T
     if fast:
         every, vectors = proj[0, :, half + third :], proj[1, :, half + third :]

time: 293 us -> 291 us (level)
  transfers between devices with their start and end apart: 37 -> 37, of which waited for: 12 -> 15; matrix products, arithmetic and copies ran while one was open for 8% -> 8% of each run, Pallas kernels for 59% -> 59%
where the time goes in v2:
time: 291 us; the launch traced here: 290 us
  Pallas kernels  171 us (59%)
  starting transfers between devices  47.9 us (16%)
  waiting for transfers between devices  33.6 us (12%)
  other arithmetic  25.4 us (9%)
  local copies, waits for them, and re-layouts  11.1 us (4%)
    pallas_call x2, Pallas kernels, mlp_part(): pl.pallas_call(partial(mlp_kernel, layout=layout, tile=tile), grid_spec=p...  51.8 us
    pallas_call x2, Pallas kernels, input_rows(): pl.pallas_call(partial(input_kernel, layout=layout, first=first), grid_sp...  28.7 us
    pallas_call x1, Pallas kernels, backward_block(): pl.pallas_call(partial(backward_kernel, layout=layout, half=3 * width //...  28.2 us
    pallas_call x1, Pallas kernels, forward_block(): pl.pallas_call(partial(forward_kernel, layout=layout, half=3 * width // 2...  23.9 us
    all_to_all x4, starting transfers between devices, along(): lax.all_to_all(value, AXES, 0, 0, axis_index_groups=self.lines, tiled=True)  20.5 us
    ppermute x6, waiting for transfers between devices, over(): return lax.ppermute(value, 'wide', [(i, i ^ 1) for i in range(self.wide)])  15.4 us
    pallas_call x1, Pallas kernels, place_rows(): pl.pallas_call(out_kernel, grid_spec=pltpu.PrefetchScalarGridSpec(num_sca...  13.5 us
    pallas_call x1, Pallas kernels, gather_rows(): pl.pallas_call(gather_kernel, grid=(seqs,), in_specs=[pl.BlockSpec((1, sl...  12.6 us
  transfers between devices with their start and end apart: 37, of which 15 were waited for; matrix products, arithmetic and copies ran while one was open for 8% of the time, Pallas kernels for 59%

profile of v2, /device:TPU:0, one launch (start us, length us, event | category | flops | bytes accessed | tf_op | source)
XLA Modules:
  0.0 290.3 jit_solution(2706156276839675177)
XLA Ops:
  1.6 0.9 reshape.67
  4.8 0.9 broadcast_in_dim.32
  5.7 6.4 %all-to-all-start = ((bf16[8,24,1664]{2,1,0:T(8,128)(2,1)}), bf16[8,24,1664]{2,1,0:T(8,128)(2,1)}, u32[]{:S(2)}, u32[]{:S(2)}) async-start(bf16[8,24,1664]{2,1,0:T(8,128)(2,1)} %bitcast.11), calls=%async_computation | async-start | bytes 1277952 | tf_op jit(solution)/shard_map/all_to_all | solution.py:711
  12.8 1.1 broadcast_in_dim.33
  14.0 1.0 copy.29.target
  16.8 12.6 %gather_rows.1 = (bf16[1024,768]{1,0:T(8,128)(2,1)}, bf16[1024,768]{1,0:T(8,128)(2,1)}) custom-call(s32[4,256,1]{2,1,0:T(8,128)} %copy.29.target, bf16[4,2048,768]{2,1,0:T(8,128)(2,1)} %x.5, bf16[4,2048,768]{2,1,0:T(8,128)(2,1)} %x.7), custom_call_target="tpu_custom_call" | custom-call | flops 6442450944 | bytes 25165824 | tf_op jit(solution)/shard_map/gather_rows/pallas_call | solution.py:101
  30.1 4.5 %all-to-all-start.1 = ((bf16[8,24,3072]{2,1,0:T(8,128)(2,1)}), bf16[8,24,3072]{2,1,0:T(8,128)(2,1)S(1)}, u32[]{:S(2)}, u32[]{:S(2)}) async-start(bf16[8,24,3072]{2,1,0:T(8,128)(2,1)} %bitcast.94), calls=%async_computation.1 | async-start | bytes 2359296 | tf_op jit(solution)/shard_map/all_to_all | solution.py:711
  34.6 1.5 collective-permute-start.1
  36.1 1.5 collective-permute-start
  37.6 14.0 %collective-permute-done.1.rest_2_ = bf16[192,1664]{1,0:T(8,128)(2,1)S(1)} collective-permute-done((bf16[192,1664]{1,0:T(8,128)(2,1)}, bf16[192,1664]{1,0:T(8,128)(2,1)S(1)}, u32[]{:S(2)}, u32[]{:S(2)}) %collective-permute-start.1) | collective-permute-done | bytes 639008 | tf_op jit(solution)/shard_map/ppermute | solution.py:706
  51.6 1.5 collective-permute-start.2
  53.2 1.6 collective-permute-start.3
  55.3 5.5 %collective-permute-done.2.rest_3_ = bf16[96,1664]{1,0:T(8,128)(2,1)S(1)} collective-permute-done((bf16[96,1664]{1,0:T(8,128)(2,1)S(1)}, bf16[96,1664]{1,0:T(8,128)(2,1)S(1)}, u32[]{:S(2)}, u32[]{:S(2)}) %collective-permute-start.2) | collective-permute-done | bytes 319520 | tf_op jit(solution)/shard_map/ppermute | solution.py:704
  60.8 1.4 collective-permute-done.3.rest_4_
  62.5 1.6 collective-permute-done.8.rest_9_
  64.1 1.1 fusion.7
  65.3 1.4 collective-permute-start.12
  66.6 1.5 collective-permute-start.13
  69.4 23.9 %forward_block.1 = (bf16[1024,2304]{1,0:T(8,128)(2,1)}, bf16[1024,768]{1,0:T(8,128)(2,1)}, f32[1024,768]{1,0:T(8,128)}, bf16[1024,768]{1,0:T(8,128)(2,1)}, bf16[...) custom-call(s32[2]{0:T(128)} %pad_add_fusion.1.where, ...), custom_call_target="tpu_custom_call" | custom-call | flops 6039797760 | bytes 23592960 | tf_op jit(solution)/shard_map/forward_block/pallas_call | solution.py:258
  93.4 1.2 collective-permute-done.14.rest_7_
  95.6 1.0 collective-permute-start.10
  97.0 1.8 collective-permute-start.11
  99.5 25.8 %mlp_part.2 = (bf16[1024,768]{1,0:T(8,128)(2,1)}, bf16[1024,768]{1,0:T(8,128)(2,1)}, bf16[768,1536]{1,0:T(8,128)(2,1)}, bf16[768,1536]{1,0:T(8,128)(2,1)}, f32[1,1536]{1,0:T(1,128)}) custom-call(s32[2]{0:T(128)} %pad_add_fusion.1.where, f32[1,3072]{1,0:T(1,128)} %get-tuple-element.124.bias, bf16[1024,768]{1,0:T(8,128)(2,1)} %get-tuple-element.136.rest_0_, ...), custom_call_target="tpu_custom_call" | custom-call | flops 14495514624 | bytes 6291456 | tf_op jit(solution)/shard_map/mlp_part/pallas_call | solution.py:384
  126.8 1.3 collective-permute-done.19.rest_8_
  130.6 26.0 %mlp_part.3 = (bf16[1024,768]{1,0:T(8,128)(2,1)}, bf16[1024,768]{1,0:T(8,128)(2,1)}, bf16[768,1536]{1,0:T(8,128)(2,1)}, bf16[768,1536]{1,0:T(8,128)(2,1)}, f32[1,1536]{1,0:T(1,128)}) custom-call(s32[2]{0:T(128)} %pad_add_fusion.1.where, f32[1,3072]{1,0:T(1,128)} %get-tuple-element.124.bias, bf16[1024,768]{1,0:T(8,128)(2,1)} %get-tuple-element.136.rest_0_, ...), custom_call_target="tpu_custom_call" | custom-call | flops 14495514624 | bytes 6291456 | tf_op jit(solution)/shard_map/mlp_part/pallas_call | solution.py:384
  156.8 3.5 %add_convert_fusion.8 = (bf16[192,1536]{1,0:T(8,128)(2,1)}, bf16[192,1536]{1,0:T(8,128)(2,1)}, bf16[192,1536]{1,0:T(8,128)(2,1)}) fusion(bf16[768,1536]{1,0:T(8,128)(2,1)} %collective-permute-done.24, s32[]{:T(128)S(6)} %select_n.52, bf16[768,1536]{1,0:T(8,128)(2,1)} %get-tuple-element.151, s32[]{:T(128)S(6)} %select_n.51, s32[]{:T(128)S(6)} %select_n.50), kind=kLoop, calls=%fused_computation.11 | loop fusion | flops 3538944 | bytes 5308428 | tf_op jit(solution)/shard_map/convert_element_type | solution.py:767
  160.4 1.3 collective-permute-start.25
  162.3 1.5 collective-permute-start.27
  163.9 2.0 add_convert_fusion
  165.9 4.5 %all-to-all-start.2 = ((bf16[4,192,1536]{2,1,0:T(8,128)(2,1)}), bf16[4,192,1536]{2,1,0:T(8,128)(2,1)}, u32[]{:S(2)}, u32[]{:S(2)}) async-start(bf16[4,192,1536]{2,1,0:T(8,128)(2,1)} %bitcast.22), calls=%async_computation.2 | async-start | bytes 4718592 | tf_op jit(solution)/shard_map/all_to_all | solution.py:741
  170.4 28.2 %backward_block.1 = (bf16[1024,2304]{1,0:T(8,128)(2,1)}, bf16[768,1024]{1,0:T(8,128)(2,1)}, f32[1024,768]{1,0:T(8,128)}, bf16[1024,768]{1,0:T(8,128)(2,1)}, f32[1,768]{1,0:T(1,128)}) custom-call(s32[2]{0:T(128)} %pad_add_fusion.1.where, s32[4]{0:T(128)} %copy-done.13, bf16[1024,768]{1,0:T(8,128)(2,1)} %get-tuple-element.107.sel, ...), custom_call_target="tpu_custom_call" | custom-call | flops 24159191040 | bytes 47185920 | tf_op jit(solution)/shard_map/backward_block/pallas_call | solution.py:508
  198.6 12.5 %project_grads.1 = (bf16[768,1664]{1,0:T(8,128)(2,1)}, bf16[768,1664]{1,0:T(8,128)(2,1)}) custom-call(s32[2]{0:T(128)} %pad_add_fusion.1.where, bf16[768,1024]{1,0:T(8,128)(2,1)} %get-tuple-element.154.n1t, bf16[768,1024]{1,0:T(8,128)(2,1)} %get-tuple-element.155.dattnt, bf16[1024,2304]{1,0:T(8,128)(2,1)} %get-tuple-element.156.dqkv, ...), custom_call_target="tpu_custom_call" | custom-call | flops 10468982784 | bytes 6291456 | tf_op jit(solution)/shard_map/project_grads/pallas_call | solution.py:576
  211.1 4.2 %all-to-all-done.2 = bf16[4,192,1536]{2,1,0:T(8,128)(2,1)} async-done(((bf16[4,192,1536]{2,1,0:T(8,128)(2,1)}), bf16[4,192,1536]{2,1,0:T(8,128)(2,1)}, u32[]{:S(2)}, u32[]{:S(2)}) %all-to-all-start.2) | async-done | bytes 2359328 | tf_op jit(solution)/shard_map/all_to_all | solution.py:741
  215.3 1.9 add_convert_fusion.6
  217.2 2.3 add_convert_fusion.7
  219.5 1.2 pad_maximum_fusion
  220.6 2.0 add_convert_fusion.2
  222.6 4.4 %all-to-all-start.3 = ((bf16[8,24,3072]{2,1,0:T(8,128)(2,1)}), bf16[8,24,3072]{2,1,0:T(8,128)(2,1)}, u32[]{:S(2)}, u32[]{:S(2)}) async-start(bf16[8,24,3072]{2,1,0:T(8,128)(2,1)} %bitcast.24), calls=%async_computation.3 | async-start | bytes 2359296 | tf_op jit(solution)/shard_map/all_to_all | solution.py:711
  227.6 1.2 collective-permute-start.30
  228.8 1.7 collective-permute-start.31
  230.5 13.5 %place_rows.1 = bf16[4,2048,768]{2,1,0:T(8,128)(2,1)} custom-call(s32[2,4]{1,0:T(2,128)} %pad_add_fusion.runs, bf16[1024,768]{1,0:T(8,128)(2,1)} %get-tuple-element.170.rows, s32[4,1,256]{2,1,0:T(1,128)} %broadcast_in_dim.36.target, bf16[4,2048,768]{2,1,0:T(8,128)(2,1)} %x.5), custom_call_target="tpu_custom_call" | custom-call | flops 3221225472 | bytes 25165824 | tf_op jit(solution)/shard_map/place_rows/pallas_call | solution.py:621
  244.0 14.4 %input_rows.2.rest_10_ = bf16[4,2048,768]{2,1,0:T(8,128)(2,1)} custom-call(s32[2]{0:T(128)} %pad_add_fusion.1.where, s32[2,4]{1,0:T(2,128)} %pad_add_fusion.runs, bf16[1024,768]{1,0:T(8,128)(2,1)} %get-tuple-element.107.sel, bf16[1024,768]{1,0:T(8,128)(2,1)} %get-tuple-element.108.grad, f32[8,768]{1,0:T(8,128)} %get-tuple-element.119.vec, ...), custom_call_target="tpu_custom_call" | custom-call | flops 1 | bytes 1 | tf_op jit(solution)/shard_map/input_rows/pallas_call | solution.py:667
  258.4 2.9 add_convert_fusion.1
  261.3 5.1 %all-to-all-start.4 = ((bf16[8,24,1664]{2,1,0:T(8,128)(2,1)}), bf16[8,24,1664]{2,1,0:T(8,128)(2,1)}, u32[]{:S(2)}, u32[]{:S(2)}) async-start(bf16[8,24,1664]{2,1,0:T(8,128)(2,1)} %bitcast.26), calls=%async_computation.4 | async-start | bytes 1277952 | tf_op jit(solution)/shard_map/all_to_all | solution.py:711
  266.4 2.3 convert_reduce_fusion
  268.7 14.4 %input_rows.3 = bf16[4,2048,768]{2,1,0:T(8,128)(2,1)} custom-call(s32[2]{0:T(128)} %pad_add_fusion.1.where, s32[2,4]{1,0:T(2,128)} %pad_add_fusion.runs, bf16[1024,768]{1,0:T(8,128)(2,1)} %get-tuple-element.107.sel, bf16[1024,768]{1,0:T(8,128)(2,1)} %get-tuple-element.108.grad, f32[8,768]{1,0:T(8,128)} %get-tuple-element.119.vec, ...), custom_call_target="tpu_custom_call", output_to_operand_aliasing={{}: (20, {})} | custom-call | flops 1 | bytes 1 | tf_op jit(solution)/shard_map/input_rows/pallas_call | solution.py:667
  283.1 1.2 slice_bitcast_fusion.3
  286.5 1.2 convert_reduce_fusion.1
  (127 shorter events, 20.7 us)
Async XLA Ops:
  4.8 7.4 %copy-start.14 = (s32[4]{0:T(128)S(1)}, s32[4]{0:T(128)}, u32[]{:S(2)}) copy-start(s32[4]{0:T(128)} %param.15) | copy-start | bytes 52
  4.8 7.4 %copy-start.12 = (s32[4,256]{1,0:T(4,128)S(1)}, s32[4,256]{1,0:T(4,128)}, u32[]{:S(2)}) copy-start(s32[4,256]{1,0:T(4,128)} %param.17) | copy-start | bytes 12292
  4.8 7.6 %copy-start.6 = (bf16[24,3072]{1,0:T(8,128)(2,1)S(1)}, bf16[24,3072]{1,0:T(8,128)(2,1)}, u32[]{:S(2)}) copy-start(bf16[24,3072]{1,0:T(8,128)(2,1)} %param.22) | copy-start | bytes 442372
  4.8 7.5 %copy-start.10 = (bf16[3072,24]{0,1:T(8,128)(2,1)S(1)}, bf16[3072,24]{0,1:T(8,128)(2,1)}, u32[]{:S(2)}) copy-start(bf16[3072,24]{0,1:T(8,128)(2,1)} %param.24) | copy-start | bytes 442372
  5.7 24.3 %all-to-all-start = ((bf16[8,24,1664]{2,1,0:T(8,128)(2,1)}), bf16[8,24,1664]{2,1,0:T(8,128)(2,1)}, u32[]{:S(2)}, u32[]{:S(2)}) async-start(bf16[8,24,1664]{2,1,0:T(8,128)(2,1)} %bitcast.11), calls=%async_computation | async-start | bytes 1277952 | tf_op jit(solution)/shard_map/all_to_all | solution.py:711
  12.8 2.8 copy-start.11
  30.1 34.1 %all-to-all-start.1 = ((bf16[8,24,3072]{2,1,0:T(8,128)(2,1)}), bf16[8,24,3072]{2,1,0:T(8,128)(2,1)S(1)}, u32[]{:S(2)}, u32[]{:S(2)}) async-start(bf16[8,24,3072]{2,1,0:T(8,128)(2,1)} %bitcast.94), calls=%async_computation.1 | async-start | bytes 2359296 | tf_op jit(solution)/shard_map/all_to_all | solution.py:711
  34.6 17.0 %collective-permute-start.1 = (bf16[192,1664]{1,0:T(8,128)(2,1)}, bf16[192,1664]{1,0:T(8,128)(2,1)S(1)}, u32[]{:S(2)}, u32[]{:S(2)}) collective-permute-start(bf16[192,1664]{1,0:T(8,128)(2,1)} %bitcast.12.rest_0_), channel_id=1, source_target_pairs={{0,4},{4,0},{8,12},{12,8},{16,20},{20,16},{24,28},{28,24},{1,5},{5... | collective-permute-start | bytes 1916936 | tf_op jit(solution)/shard_map/ppermute | solution.py:706
  36.1 17.1 %collective-permute-start = (bf16[192,1664]{1,0:T(8,128)(2,1)}, bf16[192,1664]{1,0:T(8,128)(2,1)S(1)}, u32[]{:S(2)}, u32[]{:S(2)}) collective-permute-start(bf16[192,1664]{1,0:T(8,128)(2,1)} %bitcast.12.rest_0_), channel_id=1, source_target_pairs={{0,2},{1,3},{2,0},{3,1},{4,6},{5,7},{6,4},{7,5},{8,10},{9,11},{10,... | collective-permute-start | bytes 1916936 | tf_op jit(solution)/shard_map/ppermute | solution.py:704
  37.6 24.6 %collective-permute-start.4 = (bf16[192,1664]{1,0:T(8,128)(2,1)}, bf16[192,1664]{1,0:T(8,128)(2,1)S(1)}, u32[]{:S(2)}, u32[]{:S(2)}) collective-permute-start(bf16[192,1664]{1,0:T(8,128)(2,1)} %bitcast.12.rest_0_), channel_id=1, source_target_pairs={{0,1},{1,0},{2,3},{3,2},{4,5},{5,4},{6,7},{7,6},{8,9},{9,8},{10,11... | collective-permute-start | bytes 1916936 | tf_op jit(solution)/shard_map/ppermute | solution.py:700
  51.6 13.7 %copy-start = (bf16[192,1664]{1,0:T(8,128)(2,1)}, bf16[192,1664]{1,0:T(8,128)(2,1)S(1)}, u32[]{:S(2)}) copy-start(bf16[192,1664]{1,0:T(8,128)(2,1)S(1)} %collective-permute-done.1.rest_2_) | copy-start | bytes 1916932
  51.6 9.2 %collective-permute-start.2 = (bf16[96,1664]{1,0:T(8,128)(2,1)S(1)}, bf16[96,1664]{1,0:T(8,128)(2,1)S(1)}, u32[]{:S(2)}, u32[]{:S(2)}) collective-permute-start(bf16[96,1664]{1,0:T(8,128)(2,1)S(1)} %slice.175), channel_id=1, source_target_pairs={{0,2},{1,3},{2,0},{3,1},{4,6},{5,7},{6,4},{7,5},{8,10},{9,11},{10,... | collective-permute-start | bytes 958472 | tf_op jit(solution)/shard_map/ppermute | solution.py:704
  53.1 12.1 %copy-start.1 = (bf16[192,1664]{1,0:T(8,128)(2,1)}, bf16[192,1664]{1,0:T(8,128)(2,1)S(1)}, u32[]{:S(2)}) copy-start(bf16[192,1664]{1,0:T(8,128)(2,1)S(1)} %collective-permute-done.rest_1_) | copy-start | bytes 1916932
  53.2 9.0 %collective-permute-start.3 = (bf16[96,1664]{1,0:T(8,128)(2,1)S(1)}, bf16[96,1664]{1,0:T(8,128)(2,1)}, u32[]{:S(2)}, u32[]{:S(2)}) collective-permute-start(bf16[96,1664]{1,0:T(8,128)(2,1)S(1)} %slice.176), channel_id=1, source_target_pairs={{0,4},{4,0},{8,12},{12,8},{16,20},{20,16},{24,28},{28,24},{1,5},{5... | collective-permute-start | bytes 958472 | tf_op jit(solution)/shard_map/ppermute | solution.py:706
  54.8 9.4 %collective-permute-start.5 = (bf16[192,1664]{1,0:T(8,128)(2,1)S(1)}, bf16[192,1664]{1,0:T(8,128)(2,1)}, u32[]{:S(2)}, u32[]{:S(2)}) collective-permute-start(bf16[192,1664]{1,0:T(8,128)(2,1)S(1)} %collective-permute-done.rest_1_), channel_id=1, source_target_pairs={{0,1},{1,0},{2,3},{3,2},{4,5},{5,4},{6,7},{7,6},{8,9},{9,8},{10,11... | collective-permute-start | bytes 1916936 | tf_op jit(solution)/shard_map/ppermute | solution.py:700
  54.8 9.4 %collective-permute-start.6 = (bf16[192,1664]{1,0:T(8,128)(2,1)S(1)}, bf16[192,1664]{1,0:T(8,128)(2,1)}, u32[]{:S(2)}, u32[]{:S(2)}) collective-permute-start(bf16[192,1664]{1,0:T(8,128)(2,1)S(1)} %collective-permute-done.1.rest_2_), channel_id=1, source_target_pairs={{0,1},{1,0},{2,3},{3,2},{4,5},{5,4},{6,7},{7,6},{8,9},{9,8},{10,11... | collective-permute-start | bytes 1916936 | tf_op jit(solution)/shard_map/ppermute | solution.py:700
  60.7 5.9 %copy-start.5 = (bf16[96,1664]{1,0:T(8,128)(2,1)}, bf16[96,1664]{1,0:T(8,128)(2,1)S(1)}, u32[]{:S(2)}) copy-start(bf16[96,1664]{1,0:T(8,128)(2,1)S(1)} %collective-permute-done.2.rest_3_) | copy-start | bytes 958468
  60.8 1.7 collective-permute-start.7
  62.2 2.0 collective-permute-start.8
  62.2 3.1 %copy-start.3 = (bf16[192,1664]{1,0:T(8,128)(2,1)}, bf16[192,1664]{1,0:T(8,128)(2,1)S(1)}, u32[]{:S(2)}) copy-start(bf16[192,1664]{1,0:T(8,128)(2,1)S(1)} %collective-permute-done.4.rest_5_) | copy-start | bytes 1916932
  65.3 28.1 %collective-permute-start.12 = (bf16[192,1536]{1,0:T(8,128)(2,1)}, bf16[192,1536]{1,0:T(8,128)(2,1)}, u32[]{:S(2)}, u32[]{:S(2)}) collective-permute-start(bf16[192,1536]{1,0:T(8,128)(2,1)} %get-tuple-element.130.rest_4_), channel_id=1, source_target_pairs={{0,2},{1,3},{2,0},{3,1},{4,6},{5,7},{6,4},{7,5},{8,10},{9,11},{10,... | collective-permute-start | bytes 1769480 | tf_op jit(solution)/shard_map/ppermute | solution.py:704
  66.6 26.7 %collective-permute-start.13 = (bf16[192,1536]{1,0:T(8,128)(2,1)}, bf16[192,1536]{1,0:T(8,128)(2,1)}, u32[]{:S(2)}, u32[]{:S(2)}) collective-permute-start(bf16[192,1536]{1,0:T(8,128)(2,1)} %get-tuple-element.130.rest_4_), channel_id=1, source_target_pairs={{0,4},{4,0},{8,12},{12,8},{16,20},{20,16},{24,28},{28,24},{1,5},{5... | collective-permute-start | bytes 1769480 | tf_op jit(solution)/shard_map/ppermute | solution.py:706
  68.2 26.5 %collective-permute-start.14 = (bf16[192,1536]{1,0:T(8,128)(2,1)}, bf16[192,1536]{1,0:T(8,128)(2,1)}, u32[]{:S(2)}, u32[]{:S(2)}) collective-permute-start(bf16[192,1536]{1,0:T(8,128)(2,1)} %get-tuple-element.130.rest_4_), channel_id=1, source_target_pairs={{0,6},{1,7},{2,4},{3,5},{4,2},{5,3},{6,0},{7,1},{8,14},{9,15},{10,... | collective-permute-start | bytes 1769480 | tf_op jit(solution)/shard_map/ppermute | solution.py:708
  94.6 2.3 collective-permute-start.15
  94.6 4.1 %collective-permute-start.16 = (bf16[192,1536]{1,0:T(8,128)(2,1)}, bf16[192,1536]{1,0:T(8,128)(2,1)}, u32[]{:S(2)}, u32[]{:S(2)}) collective-permute-start(bf16[192,1536]{1,0:T(8,128)(2,1)} %collective-permute-done.12.rest_5_), channel_id=1, source_target_pairs={{0,1},{1,0},{2,3},{3,2},{4,5},{5,4},{6,7},{7,6},{8,9},{9,8},{10,11... | collective-permute-start | bytes 1769480 | tf_op jit(solution)/shard_map/ppermute | solution.py:700
  95.1 4.3 %collective-permute-start.17 = (bf16[192,1536]{1,0:T(8,128)(2,1)}, bf16[192,1536]{1,0:T(8,128)(2,1)}, u32[]{:S(2)}, u32[]{:S(2)}) collective-permute-start(bf16[192,1536]{1,0:T(8,128)(2,1)} %collective-permute-done.13.rest_6_), channel_id=1, source_target_pairs={{0,1},{1,0},{2,3},{3,2},{4,5},{5,4},{6,7},{7,6},{8,9},{9,8},{10,11... | collective-permute-start | bytes 1769480 | tf_op jit(solution)/shard_map/ppermute | solution.py:700
  95.1 4.4 %collective-permute-start.18 = (bf16[192,1536]{1,0:T(8,128)(2,1)}, bf16[192,1536]{1,0:T(8,128)(2,1)}, u32[]{:S(2)}, u32[]{:S(2)}) collective-permute-start(bf16[192,1536]{1,0:T(8,128)(2,1)} %collective-permute-done.14.rest_7_), channel_id=1, source_target_pairs={{0,1},{1,0},{2,3},{3,2},{4,5},{5,4},{6,7},{7,6},{8,9},{9,8},{10,11... | collective-permute-start | bytes 1769480 | tf_op jit(solution)/shard_map/ppermute | solution.py:700
  95.6 29.7 %collective-permute-start.10 = (bf16[192,1536]{1,0:T(8,128)(2,1)}, bf16[192,1536]{1,0:T(8,128)(2,1)}, u32[]{:S(2)}, u32[]{:S(2)}) collective-permute-start(bf16[192,1536]{1,0:T(8,128)(2,1)} %get-tuple-element.137.rest_4_), channel_id=1, source_target_pairs={{0,4},{4,0},{8,12},{12,8},{16,20},{20,16},{24,28},{28,24},{1,5},{5... | collective-permute-start | bytes 1769480 | tf_op jit(solution)/shard_map/ppermute | solution.py:706
  97.0 28.3 %collective-permute-start.11 = (bf16[192,1536]{1,0:T(8,128)(2,1)}, bf16[192,1536]{1,0:T(8,128)(2,1)}, u32[]{:S(2)}, u32[]{:S(2)}) collective-permute-start(bf16[192,1536]{1,0:T(8,128)(2,1)} %get-tuple-element.137.rest_4_), channel_id=1, source_target_pairs={{0,6},{1,7},{2,4},{3,5},{4,2},{5,3},{6,0},{7,1},{8,14},{9,15},{10,... | collective-permute-start | bytes 1769480 | tf_op jit(solution)/shard_map/ppermute | solution.py:708
  98.7 27.0 %collective-permute-start.9 = (bf16[192,1536]{1,0:T(8,128)(2,1)}, bf16[192,1536]{1,0:T(8,128)(2,1)}, u32[]{:S(2)}, u32[]{:S(2)}) collective-permute-start(bf16[192,1536]{1,0:T(8,128)(2,1)} %get-tuple-element.137.rest_4_), channel_id=1, source_target_pairs={{0,2},{1,3},{2,0},{3,1},{4,6},{5,7},{6,4},{7,5},{8,10},{9,11},{10,... | collective-permute-start | bytes 1769480 | tf_op jit(solution)/shard_map/ppermute | solution.py:704
  125.8 2.3 collective-permute-start.19
  125.8 3.2 %collective-permute-start.20 = (bf16[192,1536]{1,0:T(8,128)(2,1)}, bf16[192,1536]{1,0:T(8,128)(2,1)}, u32[]{:S(2)}, u32[]{:S(2)}) collective-permute-start(bf16[192,1536]{1,0:T(8,128)(2,1)} %collective-permute-done.9.rest_5_), channel_id=1, source_target_pairs={{0,1},{1,0},{2,3},{3,2},{4,5},{5,4},{6,7},{7,6},{8,9},{9,8},{10,11... | collective-permute-start | bytes 1769480 | tf_op jit(solution)/shard_map/ppermute | solution.py:700
  126.3 3.5 %collective-permute-start.21 = (bf16[192,1536]{1,0:T(8,128)(2,1)}, bf16[192,1536]{1,0:T(8,128)(2,1)}, u32[]{:S(2)}, u32[]{:S(2)}) collective-permute-start(bf16[192,1536]{1,0:T(8,128)(2,1)} %collective-permute-done.10.rest_6_), channel_id=1, source_target_pairs={{0,1},{1,0},{2,3},{3,2},{4,5},{5,4},{6,7},{7,6},{8,9},{9,8},{10,11... | collective-permute-start | bytes 1769480 | tf_op jit(solution)/shard_map/ppermute | solution.py:700
  126.3 4.4 %collective-permute-start.22 = (bf16[192,1536]{1,0:T(8,128)(2,1)}, bf16[192,1536]{1,0:T(8,128)(2,1)}, u32[]{:S(2)}, u32[]{:S(2)}) collective-permute-start(bf16[192,1536]{1,0:T(8,128)(2,1)} %collective-permute-done.11.rest_7_), channel_id=1, source_target_pairs={{0,1},{1,0},{2,3},{3,2},{4,5},{5,4},{6,7},{7,6},{8,9},{9,8},{10,11... | collective-permute-start | bytes 1769480 | tf_op jit(solution)/shard_map/ppermute | solution.py:700
  126.8 30.1 %collective-permute-start.24 = (bf16[768,1536]{1,0:T(8,128)(2,1)}, bf16[768,1536]{1,0:T(8,128)(2,1)}, u32[]{:S(2)}, u32[]{:S(2)}) collective-permute-start(bf16[768,1536]{1,0:T(8,128)(2,1)} %get-tuple-element.143), channel_id=1, source_target_pairs={{0,1},{1,0},{2,3},{3,2},{4,5},{5,4},{6,7},{7,6},{8,9},{9,8},{10,11... | collective-permute-start | bytes 7077896 | tf_op jit(solution)/shard_map/ppermute | solution.py:700
  156.6 7.2 %collective-permute-start.23 = (bf16[768,1536]{1,0:T(8,128)(2,1)}, bf16[768,1536]{1,0:T(8,128)(2,1)S(1)}, u32[]{:S(2)}, u32[]{:S(2)}) collective-permute-start(bf16[768,1536]{1,0:T(8,128)(2,1)} %get-tuple-element.142), channel_id=1, source_target_pairs={{0,1},{1,0},{2,3},{3,2},{4,5},{5,4},{6,7},{7,6},{8,9},{9,8},{10,11... | collective-permute-start | bytes 7077896 | tf_op jit(solution)/shard_map/ppermute | solution.py:700
  156.8 7.0 %copy-start.4 = (bf16[768,1536]{1,0:T(8,128)(2,1)S(1)}, bf16[768,1536]{1,0:T(8,128)(2,1)}, u32[]{:S(2)}) copy-start(bf16[768,1536]{1,0:T(8,128)(2,1)} %get-tuple-element.141) | copy-start | bytes 7077892
  160.4 50.7 %collective-permute-start.25 = (bf16[192,1536]{1,0:T(8,128)(2,1)}, bf16[192,1536]{1,0:T(8,128)(2,1)}, u32[]{:S(2)}, u32[]{:S(2)}) collective-permute-start(bf16[192,1536]{1,0:T(8,128)(2,1)} %get-tuple-element.193), channel_id=1, source_target_pairs={{0,2},{1,3},{2,0},{3,1},{4,6},{5,7},{6,4},{7,5},{8,10},{9,11},{10,... | collective-permute-start | bytes 1769480 | tf_op jit(solution)/shard_map/ppermute | solution.py:704
  161.7 49.4 %collective-permute-start.26 = (bf16[192,1536]{1,0:T(8,128)(2,1)}, bf16[192,1536]{1,0:T(8,128)(2,1)}, u32[]{:S(2)}, u32[]{:S(2)}) collective-permute-start(bf16[192,1536]{1,0:T(8,128)(2,1)} %get-tuple-element.192), channel_id=1, source_target_pairs={{0,4},{4,0},{8,12},{12,8},{16,20},{20,16},{24,28},{28,24},{1,5},{5... | collective-permute-start | bytes 1769480 | tf_op jit(solution)/shard_map/ppermute | solution.py:706
  162.3 48.8 %collective-permute-start.27 = (bf16[192,1536]{1,0:T(8,128)(2,1)}, bf16[192,1536]{1,0:T(8,128)(2,1)}, u32[]{:S(2)}, u32[]{:S(2)}) collective-permute-start(bf16[192,1536]{1,0:T(8,128)(2,1)} %get-tuple-element.191), channel_id=1, source_target_pairs={{0,6},{1,7},{2,4},{3,5},{4,2},{5,3},{6,0},{7,1},{8,14},{9,15},{10,... | collective-permute-start | bytes 1769480 | tf_op jit(solution)/shard_map/ppermute | solution.py:708
  165.9 49.4 %all-to-all-start.2 = ((bf16[4,192,1536]{2,1,0:T(8,128)(2,1)}), bf16[4,192,1536]{2,1,0:T(8,128)(2,1)}, u32[]{:S(2)}, u32[]{:S(2)}) async-start(bf16[4,192,1536]{2,1,0:T(8,128)(2,1)} %bitcast.22), calls=%async_computation.2 | async-start | bytes 4718592 | tf_op jit(solution)/shard_map/all_to_all | solution.py:741
  215.3 5.4 %collective-permute-start.28 = (bf16[768,1664]{1,0:T(8,128)(2,1)}, bf16[768,1664]{1,0:T(8,128)(2,1)S(1)}, u32[]{:S(2)}, u32[]{:S(2)}) collective-permute-start(bf16[768,1664]{1,0:T(8,128)(2,1)} %get-tuple-element.168), channel_id=1, source_target_pairs={{0,1},{1,0},{2,3},{3,2},{4,5},{5,4},{6,7},{7,6},{8,9},{9,8},{10,11... | collective-permute-start | bytes 7667720 | tf_op jit(solution)/shard_map/ppermute | solution.py:700
  217.1 3.5 %copy-start.2 = (bf16[768,1664]{1,0:T(8,128)(2,1)S(1)}, bf16[768,1664]{1,0:T(8,128)(2,1)}, u32[]{:S(2)}) copy-start(bf16[768,1664]{1,0:T(8,128)(2,1)} %get-tuple-element.167) | copy-start | bytes 7667716
  222.6 38.7 %all-to-all-start.3 = ((bf16[8,24,3072]{2,1,0:T(8,128)(2,1)}), bf16[8,24,3072]{2,1,0:T(8,128)(2,1)}, u32[]{:S(2)}, u32[]{:S(2)}) async-start(bf16[8,24,3072]{2,1,0:T(8,128)(2,1)} %bitcast.24), calls=%async_computation.3 | async-start | bytes 2359296 | tf_op jit(solution)/shard_map/all_to_all | solution.py:711
  227.0 31.3 %collective-permute-start.29 = (bf16[192,1664]{1,0:T(8,128)(2,1)}, bf16[192,1664]{1,0:T(8,128)(2,1)}, u32[]{:S(2)}, u32[]{:S(2)}) collective-permute-start(bf16[192,1664]{1,0:T(8,128)(2,1)} %get-tuple-element.175), channel_id=1, source_target_pairs={{0,2},{1,3},{2,0},{3,1},{4,6},{5,7},{6,4},{7,5},{8,10},{9,11},{10,... | collective-permute-start | bytes 1916936 | tf_op jit(solution)/shard_map/ppermute | solution.py:704
  227.6 30.8 %collective-permute-start.30 = (bf16[192,1664]{1,0:T(8,128)(2,1)}, bf16[192,1664]{1,0:T(8,128)(2,1)}, u32[]{:S(2)}, u32[]{:S(2)}) collective-permute-start(bf16[192,1664]{1,0:T(8,128)(2,1)} %get-tuple-element.176), channel_id=1, source_target_pairs={{0,4},{4,0},{8,12},{12,8},{16,20},{20,16},{24,28},{28,24},{1,5},{5... | collective-permute-start | bytes 1916936 | tf_op jit(solution)/shard_map/ppermute | solution.py:706
  228.8 29.6 %collective-permute-start.31 = (bf16[192,1664]{1,0:T(8,128)(2,1)}, bf16[192,1664]{1,0:T(8,128)(2,1)}, u32[]{:S(2)}, u32[]{:S(2)}) collective-permute-start(bf16[192,1664]{1,0:T(8,128)(2,1)} %get-tuple-element.177), channel_id=1, source_target_pairs={{0,6},{1,7},{2,4},{3,5},{4,2},{5,3},{6,0},{7,1},{8,14},{9,15},{10,... | collective-permute-start | bytes 1916936 | tf_op jit(solution)/shard_map/ppermute | solution.py:708
  261.3 25.2 %all-to-all-start.4 = ((bf16[8,24,1664]{2,1,0:T(8,128)(2,1)}), bf16[8,24,1664]{2,1,0:T(8,128)(2,1)}, u32[]{:S(2)}, u32[]{:S(2)}) async-start(bf16[8,24,1664]{2,1,0:T(8,128)(2,1)} %bitcast.26), calls=%async_computation.4 | async-start | bytes 1277952 | tf_op jit(solution)/shard_map/all_to_all | solution.py:711
  (6 other events, 11.8 us)

commit v3 on v2

--- a/solution.py
+++ b/solution.py
@@ -885,12 +885,13 @@
     if fast:
         one_own, n2 = tie(one_own, n2)
         one_oth = paths.swap_all(one_own)
+        two_first, n2 = tie(paths.swap(two_own[0]), n2)
     mlp, dn2, d_one_own, d_one_oth, dbias_one = mlp_part(
         lay_two, where, 0, tile, n2, n2t, g, gt, one_own, one_oth, bias
     )
     if fast:
         two_own, mlp, n2 = tie(two_own, mlp, n2)
-        two_oth = paths.swap_all(two_own)
+        two_oth = [two_first] + paths.swap_all(two_own[1:])
         d_one_got = paths.swap(d_one_oth)
     mlp_two, dn2_two, d_two_own, d_two_oth, dbias_two = mlp_part(
         lay_two, where, 1, tile, n2, n2t, g, gt, two_own, two_oth, bias

time: 291 us -> 290 us (level)
  transfers between devices with their start and end apart: 37 -> 37, of which waited for: 15 -> 14; matrix products, arithmetic and copies ran while one was open for 8% -> 8% of each run, Pallas kernels for 59% -> 59%
where the time goes in v3:
time: 290 us; the launch traced here: 289 us
  Pallas kernels  171 us (59%)
  starting transfers between devices  47.8 us (16%)
  waiting for transfers between devices  32.8 us (11%)
  other arithmetic  25.4 us (9%)
  local copies, waits for them, and re-layouts  11.1 us (4%)
    pallas_call x2, Pallas kernels, mlp_part(): pl.pallas_call(partial(mlp_kernel, layout=layout, tile=tile), grid_spec=p...  51.8 us
    pallas_call x2, Pallas kernels, input_rows(): pl.pallas_call(partial(input_kernel, layout=layout, first=first), grid_sp...  28.7 us
    pallas_call x1, Pallas kernels, backward_block(): pl.pallas_call(partial(backward_kernel, layout=layout, half=3 * width //...  28.2 us
    pallas_call x1, Pallas kernels, forward_block(): pl.pallas_call(partial(forward_kernel, layout=layout, half=3 * width // 2...  23.9 us
    all_to_all x4, starting transfers between devices, along(): lax.all_to_all(value, AXES, 0, 0, axis_index_groups=self.lines, tiled=True)  20.5 us
    ppermute x6, waiting for transfers between devices, over(): return lax.ppermute(value, 'wide', [(i, i ^ 1) for i in range(self.wide)])  15.4 us
    pallas_call x1, Pallas kernels, place_rows(): pl.pallas_call(out_kernel, grid_spec=pltpu.PrefetchScalarGridSpec(num_sca...  13.5 us
    pallas_call x1, Pallas kernels, gather_rows(): pl.pallas_call(gather_kernel, grid=(seqs,), in_specs=[pl.BlockSpec((1, sl...  12.6 us
  transfers between devices with their start and end apart: 37, of which 14 were waited for; matrix products, arithmetic and copies ran while one was open for 8% of the time, Pallas kernels for 59%

profile of v3, /device:TPU:0, one launch (start us, length us, event | category | flops | bytes accessed | tf_op | source)
XLA Modules:
  0.0 289.5 jit_solution(237289409235208381)
XLA Ops:
  1.6 0.9 reshape.67
  4.8 0.9 broadcast_in_dim.32
  5.7 6.4 %all-to-all-start = ((bf16[8,24,1664]{2,1,0:T(8,128)(2,1)}), bf16[8,24,1664]{2,1,0:T(8,128)(2,1)}, u32[]{:S(2)}, u32[]{:S(2)}) async-start(bf16[8,24,1664]{2,1,0:T(8,128)(2,1)} %bitcast.11), calls=%async_computation | async-start | bytes 1277952 | tf_op jit(solution)/shard_map/all_to_all | solution.py:711
  12.8 1.1 broadcast_in_dim.33
  14.0 1.0 copy.29.target
  16.8 12.6 %gather_rows.1 = (bf16[1024,768]{1,0:T(8,128)(2,1)}, bf16[1024,768]{1,0:T(8,128)(2,1)}) custom-call(s32[4,256,1]{2,1,0:T(8,128)} %copy.29.target, bf16[4,2048,768]{2,1,0:T(8,128)(2,1)} %x.5, bf16[4,2048,768]{2,1,0:T(8,128)(2,1)} %x.7), custom_call_target="tpu_custom_call" | custom-call | flops 6442450944 | bytes 25165824 | tf_op jit(solution)/shard_map/gather_rows/pallas_call | solution.py:101
  30.1 4.5 %all-to-all-start.1 = ((bf16[8,24,3072]{2,1,0:T(8,128)(2,1)}), bf16[8,24,3072]{2,1,0:T(8,128)(2,1)S(1)}, u32[]{:S(2)}, u32[]{:S(2)}) async-start(bf16[8,24,3072]{2,1,0:T(8,128)(2,1)} %bitcast.94), calls=%async_computation.1 | async-start | bytes 2359296 | tf_op jit(solution)/shard_map/all_to_all | solution.py:711
  34.6 1.5 collective-permute-start.1
  36.1 1.5 collective-permute-start
  37.6 14.0 %collective-permute-done.1.rest_2_ = bf16[192,1664]{1,0:T(8,128)(2,1)S(1)} collective-permute-done((bf16[192,1664]{1,0:T(8,128)(2,1)}, bf16[192,1664]{1,0:T(8,128)(2,1)S(1)}, u32[]{:S(2)}, u32[]{:S(2)}) %collective-permute-start.1) | collective-permute-done | bytes 639008 | tf_op jit(solution)/shard_map/ppermute | solution.py:706
  51.6 1.5 collective-permute-start.2
  53.2 1.6 collective-permute-start.3
  55.3 5.5 %collective-permute-done.2.rest_3_ = bf16[96,1664]{1,0:T(8,128)(2,1)S(1)} collective-permute-done((bf16[96,1664]{1,0:T(8,128)(2,1)S(1)}, bf16[96,1664]{1,0:T(8,128)(2,1)S(1)}, u32[]{:S(2)}, u32[]{:S(2)}) %collective-permute-start.2) | collective-permute-done | bytes 319520 | tf_op jit(solution)/shard_map/ppermute | solution.py:704
  60.8 1.4 collective-permute-done.3.rest_4_
  62.5 1.6 collective-permute-done.8.rest_9_
  64.1 1.1 fusion.7
  65.3 1.4 collective-permute-start.13
  66.6 1.5 collective-permute-start.14
  69.4 23.9 %forward_block.1 = (bf16[1024,2304]{1,0:T(8,128)(2,1)}, bf16[1024,768]{1,0:T(8,128)(2,1)}, f32[1024,768]{1,0:T(8,128)}, bf16[1024,768]{1,0:T(8,128)(2,1)}, bf16[...) custom-call(s32[2]{0:T(128)} %pad_add_fusion.1.where, ...), custom_call_target="tpu_custom_call" | custom-call | flops 6039797760 | bytes 23592960 | tf_op jit(solution)/shard_map/forward_block/pallas_call | solution.py:258
  93.4 1.2 collective-permute-done.15.rest_7_
  95.7 1.0 collective-permute-start.10
  97.0 1.8 collective-permute-start.11
  99.5 25.8 %mlp_part.2 = (bf16[1024,768]{1,0:T(8,128)(2,1)}, bf16[1024,768]{1,0:T(8,128)(2,1)}, bf16[768,1536]{1,0:T(8,128)(2,1)}, bf16[768,1536]{1,0:T(8,128)(2,1)}, f32[1,1536]{1,0:T(1,128)}) custom-call(s32[2]{0:T(128)} %pad_add_fusion.1.where, f32[1,3072]{1,0:T(1,128)} %get-tuple-element.126.bias, bf16[1024,768]{1,0:T(8,128)(2,1)} %get-tuple-element.139.rest_0_, ...), custom_call_target="tpu_custom_call" | custom-call | flops 14495514624 | bytes 6291456 | tf_op jit(solution)/shard_map/mlp_part/pallas_call | solution.py:384
  126.8 1.3 collective-permute-done.20.rest_9_
  129.8 26.0 %mlp_part.3 = (bf16[1024,768]{1,0:T(8,128)(2,1)}, bf16[1024,768]{1,0:T(8,128)(2,1)}, bf16[768,1536]{1,0:T(8,128)(2,1)}, bf16[768,1536]{1,0:T(8,128)(2,1)}, f32[1,1536]{1,0:T(1,128)}) custom-call(s32[2]{0:T(128)} %pad_add_fusion.1.where, f32[1,3072]{1,0:T(1,128)} %get-tuple-element.126.bias, bf16[1024,768]{1,0:T(8,128)(2,1)} %get-tuple-element.139.rest_0_, ...), custom_call_target="tpu_custom_call" | custom-call | flops 14495514624 | bytes 6291456 | tf_op jit(solution)/shard_map/mlp_part/pallas_call | solution.py:384
  156.0 3.5 %add_convert_fusion.8 = (bf16[192,1536]{1,0:T(8,128)(2,1)}, bf16[192,1536]{1,0:T(8,128)(2,1)}, bf16[192,1536]{1,0:T(8,128)(2,1)}) fusion(bf16[768,1536]{1,0:T(8,128)(2,1)} %collective-permute-done.24, s32[]{:T(128)S(6)} %select_n.52, bf16[768,1536]{1,0:T(8,128)(2,1)} %get-tuple-element.155, s32[]{:T(128)S(6)} %select_n.51, s32[]{:T(128)S(6)} %select_n.50), kind=kLoop, calls=%fused_computation.11 | loop fusion | flops 3538944 | bytes 5308428 | tf_op jit(solution)/shard_map/convert_element_type | solution.py:767
  159.5 1.3 collective-permute-start.25
  161.5 1.5 collective-permute-start.27
  163.0 2.0 add_convert_fusion
  165.0 4.5 %all-to-all-start.2 = ((bf16[4,192,1536]{2,1,0:T(8,128)(2,1)}), bf16[4,192,1536]{2,1,0:T(8,128)(2,1)}, u32[]{:S(2)}, u32[]{:S(2)}) async-start(bf16[4,192,1536]{2,1,0:T(8,128)(2,1)} %bitcast.22), calls=%async_computation.2 | async-start | bytes 4718592 | tf_op jit(solution)/shard_map/all_to_all | solution.py:741
  169.5 28.2 %backward_block.1 = (bf16[1024,2304]{1,0:T(8,128)(2,1)}, bf16[768,1024]{1,0:T(8,128)(2,1)}, f32[1024,768]{1,0:T(8,128)}, bf16[1024,768]{1,0:T(8,128)(2,1)}, f32[1,768]{1,0:T(1,128)}) custom-call(s32[2]{0:T(128)} %pad_add_fusion.1.where, s32[4]{0:T(128)} %copy-done.13, bf16[1024,768]{1,0:T(8,128)(2,1)} %get-tuple-element.109.sel, ...), custom_call_target="tpu_custom_call" | custom-call | flops 24159191040 | bytes 47185920 | tf_op jit(solution)/shard_map/backward_block/pallas_call | solution.py:508
  197.8 12.5 %project_grads.1 = (bf16[768,1664]{1,0:T(8,128)(2,1)}, bf16[768,1664]{1,0:T(8,128)(2,1)}) custom-call(s32[2]{0:T(128)} %pad_add_fusion.1.where, bf16[768,1024]{1,0:T(8,128)(2,1)} %get-tuple-element.158.n1t, bf16[768,1024]{1,0:T(8,128)(2,1)} %get-tuple-element.159.dattnt, bf16[1024,2304]{1,0:T(8,128)(2,1)} %get-tuple-element.160.dqkv, ...), custom_call_target="tpu_custom_call" | custom-call | flops 10468982784 | bytes 6291456 | tf_op jit(solution)/shard_map/project_grads/pallas_call | solution.py:576
  210.2 4.2 %all-to-all-done.2 = bf16[4,192,1536]{2,1,0:T(8,128)(2,1)} async-done(((bf16[4,192,1536]{2,1,0:T(8,128)(2,1)}), bf16[4,192,1536]{2,1,0:T(8,128)(2,1)}, u32[]{:S(2)}, u32[]{:S(2)}) %all-to-all-start.2) | async-done | bytes 2359328 | tf_op jit(solution)/shard_map/all_to_all | solution.py:741
  214.4 1.9 add_convert_fusion.6
  216.3 2.3 add_convert_fusion.7
  218.6 1.2 pad_maximum_fusion
  219.8 2.0 add_convert_fusion.2
  221.8 4.4 %all-to-all-start.3 = ((bf16[8,24,3072]{2,1,0:T(8,128)(2,1)}), bf16[8,24,3072]{2,1,0:T(8,128)(2,1)}, u32[]{:S(2)}, u32[]{:S(2)}) async-start(bf16[8,24,3072]{2,1,0:T(8,128)(2,1)} %bitcast.24), calls=%async_computation.3 | async-start | bytes 2359296 | tf_op jit(solution)/shard_map/all_to_all | solution.py:711
  226.8 1.2 collective-permute-start.30
  228.0 1.7 collective-permute-start.31
  229.7 13.5 %place_rows.1 = bf16[4,2048,768]{2,1,0:T(8,128)(2,1)} custom-call(s32[2,4]{1,0:T(2,128)} %pad_add_fusion.runs, bf16[1024,768]{1,0:T(8,128)(2,1)} %get-tuple-element.174.rows, s32[4,1,256]{2,1,0:T(1,128)} %broadcast_in_dim.36.target, bf16[4,2048,768]{2,1,0:T(8,128)(2,1)} %x.5), custom_call_target="tpu_custom_call" | custom-call | flops 3221225472 | bytes 25165824 | tf_op jit(solution)/shard_map/place_rows/pallas_call | solution.py:621
  243.2 14.4 %input_rows.2.rest_10_ = bf16[4,2048,768]{2,1,0:T(8,128)(2,1)} custom-call(s32[2]{0:T(128)} %pad_add_fusion.1.where, s32[2,4]{1,0:T(2,128)} %pad_add_fusion.runs, bf16[1024,768]{1,0:T(8,128)(2,1)} %get-tuple-element.109.sel, bf16[1024,768]{1,0:T(8,128)(2,1)} %get-tuple-element.110.grad, f32[8,768]{1,0:T(8,128)} %get-tuple-element.121.vec, ...), custom_call_target="tpu_custom_call" | custom-call | flops 1 | bytes 1 | tf_op jit(solution)/shard_map/input_rows/pallas_call | solution.py:667
  257.6 2.9 add_convert_fusion.1
  260.4 5.1 %all-to-all-start.4 = ((bf16[8,24,1664]{2,1,0:T(8,128)(2,1)}), bf16[8,24,1664]{2,1,0:T(8,128)(2,1)}, u32[]{:S(2)}, u32[]{:S(2)}) async-start(bf16[8,24,1664]{2,1,0:T(8,128)(2,1)} %bitcast.26), calls=%async_computation.4 | async-start | bytes 1277952 | tf_op jit(solution)/shard_map/all_to_all | solution.py:711
  265.6 2.3 convert_reduce_fusion
  267.9 14.4 %input_rows.3 = bf16[4,2048,768]{2,1,0:T(8,128)(2,1)} custom-call(s32[2]{0:T(128)} %pad_add_fusion.1.where, s32[2,4]{1,0:T(2,128)} %pad_add_fusion.runs, bf16[1024,768]{1,0:T(8,128)(2,1)} %get-tuple-element.109.sel, bf16[1024,768]{1,0:T(8,128)(2,1)} %get-tuple-element.110.grad, f32[8,768]{1,0:T(8,128)} %get-tuple-element.121.vec, ...), custom_call_target="tpu_custom_call", output_to_operand_aliasing={{}: (20, {})} | custom-call | flops 1 | bytes 1 | tf_op jit(solution)/shard_map/input_rows/pallas_call | solution.py:667
  282.3 1.2 slice_bitcast_fusion.3
  285.6 1.2 convert_reduce_fusion.1
  (127 shorter events, 19.8 us)
Async XLA Ops:
  4.8 7.4 %copy-start.14 = (s32[4]{0:T(128)S(1)}, s32[4]{0:T(128)}, u32[]{:S(2)}) copy-start(s32[4]{0:T(128)} %param.15) | copy-start | bytes 52
  4.8 7.4 %copy-start.12 = (s32[4,256]{1,0:T(4,128)S(1)}, s32[4,256]{1,0:T(4,128)}, u32[]{:S(2)}) copy-start(s32[4,256]{1,0:T(4,128)} %param.17) | copy-start | bytes 12292
  4.8 7.6 %copy-start.6 = (bf16[24,3072]{1,0:T(8,128)(2,1)S(1)}, bf16[24,3072]{1,0:T(8,128)(2,1)}, u32[]{:S(2)}) copy-start(bf16[24,3072]{1,0:T(8,128)(2,1)} %param.22) | copy-start | bytes 442372
  4.8 7.5 %copy-start.10 = (bf16[3072,24]{0,1:T(8,128)(2,1)S(1)}, bf16[3072,24]{0,1:T(8,128)(2,1)}, u32[]{:S(2)}) copy-start(bf16[3072,24]{0,1:T(8,128)(2,1)} %param.24) | copy-start | bytes 442372
  5.7 24.3 %all-to-all-start = ((bf16[8,24,1664]{2,1,0:T(8,128)(2,1)}), bf16[8,24,1664]{2,1,0:T(8,128)(2,1)}, u32[]{:S(2)}, u32[]{:S(2)}) async-start(bf16[8,24,1664]{2,1,0:T(8,128)(2,1)} %bitcast.11), calls=%async_computation | async-start | bytes 1277952 | tf_op jit(solution)/shard_map/all_to_all | solution.py:711
  12.8 2.8 copy-start.11
  30.1 34.1 %all-to-all-start.1 = ((bf16[8,24,3072]{2,1,0:T(8,128)(2,1)}), bf16[8,24,3072]{2,1,0:T(8,128)(2,1)S(1)}, u32[]{:S(2)}, u32[]{:S(2)}) async-start(bf16[8,24,3072]{2,1,0:T(8,128)(2,1)} %bitcast.94), calls=%async_computation.1 | async-start | bytes 2359296 | tf_op jit(solution)/shard_map/all_to_all | solution.py:711
  34.6 17.0 %collective-permute-start.1 = (bf16[192,1664]{1,0:T(8,128)(2,1)}, bf16[192,1664]{1,0:T(8,128)(2,1)S(1)}, u32[]{:S(2)}, u32[]{:S(2)}) collective-permute-start(bf16[192,1664]{1,0:T(8,128)(2,1)} %bitcast.12.rest_0_), channel_id=1, source_target_pairs={{0,4},{4,0},{8,12},{12,8},{16,20},{20,16},{24,28},{28,24},{1,5},{5... | collective-permute-start | bytes 1916936 | tf_op jit(solution)/shard_map/ppermute | solution.py:706
  36.1 17.1 %collective-permute-start = (bf16[192,1664]{1,0:T(8,128)(2,1)}, bf16[192,1664]{1,0:T(8,128)(2,1)S(1)}, u32[]{:S(2)}, u32[]{:S(2)}) collective-permute-start(bf16[192,1664]{1,0:T(8,128)(2,1)} %bitcast.12.rest_0_), channel_id=1, source_target_pairs={{0,2},{1,3},{2,0},{3,1},{4,6},{5,7},{6,4},{7,5},{8,10},{9,11},{10,... | collective-permute-start | bytes 1916936 | tf_op jit(solution)/shard_map/ppermute | solution.py:704
  37.6 24.6 %collective-permute-start.4 = (bf16[192,1664]{1,0:T(8,128)(2,1)}, bf16[192,1664]{1,0:T(8,128)(2,1)S(1)}, u32[]{:S(2)}, u32[]{:S(2)}) collective-permute-start(bf16[192,1664]{1,0:T(8,128)(2,1)} %bitcast.12.rest_0_), channel_id=1, source_target_pairs={{0,1},{1,0},{2,3},{3,2},{4,5},{5,4},{6,7},{7,6},{8,9},{9,8},{10,11... | collective-permute-start | bytes 1916936 | tf_op jit(solution)/shard_map/ppermute | solution.py:700
  51.6 13.7 %copy-start = (bf16[192,1664]{1,0:T(8,128)(2,1)}, bf16[192,1664]{1,0:T(8,128)(2,1)S(1)}, u32[]{:S(2)}) copy-start(bf16[192,1664]{1,0:T(8,128)(2,1)S(1)} %collective-permute-done.1.rest_2_) | copy-start | bytes 1916932
  51.6 9.2 %collective-permute-start.2 = (bf16[96,1664]{1,0:T(8,128)(2,1)S(1)}, bf16[96,1664]{1,0:T(8,128)(2,1)S(1)}, u32[]{:S(2)}, u32[]{:S(2)}) collective-permute-start(bf16[96,1664]{1,0:T(8,128)(2,1)S(1)} %slice.175), channel_id=1, source_target_pairs={{0,2},{1,3},{2,0},{3,1},{4,6},{5,7},{6,4},{7,5},{8,10},{9,11},{10,... | collective-permute-start | bytes 958472 | tf_op jit(solution)/shard_map/ppermute | solution.py:704
  53.1 12.1 %copy-start.1 = (bf16[192,1664]{1,0:T(8,128)(2,1)}, bf16[192,1664]{1,0:T(8,128)(2,1)S(1)}, u32[]{:S(2)}) copy-start(bf16[192,1664]{1,0:T(8,128)(2,1)S(1)} %collective-permute-done.rest_1_) | copy-start | bytes 1916932
  53.2 9.0 %collective-permute-start.3 = (bf16[96,1664]{1,0:T(8,128)(2,1)S(1)}, bf16[96,1664]{1,0:T(8,128)(2,1)}, u32[]{:S(2)}, u32[]{:S(2)}) collective-permute-start(bf16[96,1664]{1,0:T(8,128)(2,1)S(1)} %slice.176), channel_id=1, source_target_pairs={{0,4},{4,0},{8,12},{12,8},{16,20},{20,16},{24,28},{28,24},{1,5},{5... | collective-permute-start | bytes 958472 | tf_op jit(solution)/shard_map/ppermute | solution.py:706
  54.8 9.4 %collective-permute-start.5 = (bf16[192,1664]{1,0:T(8,128)(2,1)S(1)}, bf16[192,1664]{1,0:T(8,128)(2,1)}, u32[]{:S(2)}, u32[]{:S(2)}) collective-permute-start(bf16[192,1664]{1,0:T(8,128)(2,1)S(1)} %collective-permute-done.rest_1_), channel_id=1, source_target_pairs={{0,1},{1,0},{2,3},{3,2},{4,5},{5,4},{6,7},{7,6},{8,9},{9,8},{10,11... | collective-permute-start | bytes 1916936 | tf_op jit(solution)/shard_map/ppermute | solution.py:700
  54.8 9.4 %collective-permute-start.6 = (bf16[192,1664]{1,0:T(8,128)(2,1)S(1)}, bf16[192,1664]{1,0:T(8,128)(2,1)}, u32[]{:S(2)}, u32[]{:S(2)}) collective-permute-start(bf16[192,1664]{1,0:T(8,128)(2,1)S(1)} %collective-permute-done.1.rest_2_), channel_id=1, source_target_pairs={{0,1},{1,0},{2,3},{3,2},{4,5},{5,4},{6,7},{7,6},{8,9},{9,8},{10,11... | collective-permute-start | bytes 1916936 | tf_op jit(solution)/shard_map/ppermute | solution.py:700
  60.7 5.9 %copy-start.5 = (bf16[96,1664]{1,0:T(8,128)(2,1)}, bf16[96,1664]{1,0:T(8,128)(2,1)S(1)}, u32[]{:S(2)}) copy-start(bf16[96,1664]{1,0:T(8,128)(2,1)S(1)} %collective-permute-done.2.rest_3_) | copy-start | bytes 958468
  60.8 1.7 collective-permute-start.7
  62.2 2.0 collective-permute-start.8
  62.2 3.1 %copy-start.3 = (bf16[192,1664]{1,0:T(8,128)(2,1)}, bf16[192,1664]{1,0:T(8,128)(2,1)S(1)}, u32[]{:S(2)}) copy-start(bf16[192,1664]{1,0:T(8,128)(2,1)S(1)} %collective-permute-done.4.rest_5_) | copy-start | bytes 1916932
  65.3 28.1 %collective-permute-start.13 = (bf16[192,1536]{1,0:T(8,128)(2,1)}, bf16[192,1536]{1,0:T(8,128)(2,1)}, u32[]{:S(2)}, u32[]{:S(2)}) collective-permute-start(bf16[192,1536]{1,0:T(8,128)(2,1)} %get-tuple-element.133.rest_4_), channel_id=1, source_target_pairs={{0,2},{1,3},{2,0},{3,1},{4,6},{5,7},{6,4},{7,5},{8,10},{9,11},{10,... | collective-permute-start | bytes 1769480 | tf_op jit(solution)/shard_map/ppermute | solution.py:704
  66.6 26.7 %collective-permute-start.14 = (bf16[192,1536]{1,0:T(8,128)(2,1)}, bf16[192,1536]{1,0:T(8,128)(2,1)}, u32[]{:S(2)}, u32[]{:S(2)}) collective-permute-start(bf16[192,1536]{1,0:T(8,128)(2,1)} %get-tuple-element.133.rest_4_), channel_id=1, source_target_pairs={{0,4},{4,0},{8,12},{12,8},{16,20},{20,16},{24,28},{28,24},{1,5},{5... | collective-permute-start | bytes 1769480 | tf_op jit(solution)/shard_map/ppermute | solution.py:706
  68.2 26.5 %collective-permute-start.15 = (bf16[192,1536]{1,0:T(8,128)(2,1)}, bf16[192,1536]{1,0:T(8,128)(2,1)}, u32[]{:S(2)}, u32[]{:S(2)}) collective-permute-start(bf16[192,1536]{1,0:T(8,128)(2,1)} %get-tuple-element.133.rest_4_), channel_id=1, source_target_pairs={{0,6},{1,7},{2,4},{3,5},{4,2},{5,3},{6,0},{7,1},{8,14},{9,15},{10,... | collective-permute-start | bytes 1769480 | tf_op jit(solution)/shard_map/ppermute | solution.py:708
  69.4 26.2 %collective-permute-start.12 = (bf16[192,1536]{1,0:T(8,128)(2,1)}, bf16[192,1536]{1,0:T(8,128)(2,1)}, u32[]{:S(2)}, u32[]{:S(2)}) collective-permute-start(bf16[192,1536]{1,0:T(8,128)(2,1)} %get-tuple-element.140.rest_4_), channel_id=1, source_target_pairs={{0,1},{1,0},{2,3},{3,2},{4,5},{5,4},{6,7},{7,6},{8,9},{9,8},{10,11... | collective-permute-start | bytes 1769480 | tf_op jit(solution)/shard_map/ppermute | solution.py:700
  94.6 2.3 collective-permute-start.16
  94.6 4.1 %collective-permute-start.17 = (bf16[192,1536]{1,0:T(8,128)(2,1)}, bf16[192,1536]{1,0:T(8,128)(2,1)}, u32[]{:S(2)}, u32[]{:S(2)}) collective-permute-start(bf16[192,1536]{1,0:T(8,128)(2,1)} %collective-permute-done.13.rest_5_), channel_id=1, source_target_pairs={{0,1},{1,0},{2,3},{3,2},{4,5},{5,4},{6,7},{7,6},{8,9},{9,8},{10,11... | collective-permute-start | bytes 1769480 | tf_op jit(solution)/shard_map/ppermute | solution.py:700
  95.1 4.3 %collective-permute-start.18 = (bf16[192,1536]{1,0:T(8,128)(2,1)}, bf16[192,1536]{1,0:T(8,128)(2,1)}, u32[]{:S(2)}, u32[]{:S(2)}) collective-permute-start(bf16[192,1536]{1,0:T(8,128)(2,1)} %collective-permute-done.14.rest_6_), channel_id=1, source_target_pairs={{0,1},{1,0},{2,3},{3,2},{4,5},{5,4},{6,7},{7,6},{8,9},{9,8},{10,11... | collective-permute-start | bytes 1769480 | tf_op jit(solution)/shard_map/ppermute | solution.py:700
  95.1 4.4 %collective-permute-start.19 = (bf16[192,1536]{1,0:T(8,128)(2,1)}, bf16[192,1536]{1,0:T(8,128)(2,1)}, u32[]{:S(2)}, u32[]{:S(2)}) collective-permute-start(bf16[192,1536]{1,0:T(8,128)(2,1)} %collective-permute-done.15.rest_7_), channel_id=1, source_target_pairs={{0,1},{1,0},{2,3},{3,2},{4,5},{5,4},{6,7},{7,6},{8,9},{9,8},{10,11... | collective-permute-start | bytes 1769480 | tf_op jit(solution)/shard_map/ppermute | solution.py:700
  95.7 29.7 %collective-permute-start.10 = (bf16[192,1536]{1,0:T(8,128)(2,1)}, bf16[192,1536]{1,0:T(8,128)(2,1)}, u32[]{:S(2)}, u32[]{:S(2)}) collective-permute-start(bf16[192,1536]{1,0:T(8,128)(2,1)} %get-tuple-element.140.rest_4_), channel_id=1, source_target_pairs={{0,4},{4,0},{8,12},{12,8},{16,20},{20,16},{24,28},{28,24},{1,5},{5... | collective-permute-start | bytes 1769480 | tf_op jit(solution)/shard_map/ppermute | solution.py:706
  97.0 28.3 %collective-permute-start.11 = (bf16[192,1536]{1,0:T(8,128)(2,1)}, bf16[192,1536]{1,0:T(8,128)(2,1)}, u32[]{:S(2)}, u32[]{:S(2)}) collective-permute-start(bf16[192,1536]{1,0:T(8,128)(2,1)} %get-tuple-element.140.rest_4_), channel_id=1, source_target_pairs={{0,6},{1,7},{2,4},{3,5},{4,2},{5,3},{6,0},{7,1},{8,14},{9,15},{10,... | collective-permute-start | bytes 1769480 | tf_op jit(solution)/shard_map/ppermute | solution.py:708
  98.7 27.0 %collective-permute-start.9 = (bf16[192,1536]{1,0:T(8,128)(2,1)}, bf16[192,1536]{1,0:T(8,128)(2,1)}, u32[]{:S(2)}, u32[]{:S(2)}) collective-permute-start(bf16[192,1536]{1,0:T(8,128)(2,1)} %get-tuple-element.140.rest_4_), channel_id=1, source_target_pairs={{0,2},{1,3},{2,0},{3,1},{4,6},{5,7},{6,4},{7,5},{8,10},{9,11},{10,... | collective-permute-start | bytes 1769480 | tf_op jit(solution)/shard_map/ppermute | solution.py:704
  125.8 2.3 collective-permute-start.20
  125.8 3.2 %collective-permute-start.21 = (bf16[192,1536]{1,0:T(8,128)(2,1)}, bf16[192,1536]{1,0:T(8,128)(2,1)}, u32[]{:S(2)}, u32[]{:S(2)}) collective-permute-start(bf16[192,1536]{1,0:T(8,128)(2,1)} %collective-permute-done.10.rest_6_), channel_id=1, source_target_pairs={{0,1},{1,0},{2,3},{3,2},{4,5},{5,4},{6,7},{7,6},{8,9},{9,8},{10,11... | collective-permute-start | bytes 1769480 | tf_op jit(solution)/shard_map/ppermute | solution.py:700
  126.3 3.5 %collective-permute-start.22 = (bf16[192,1536]{1,0:T(8,128)(2,1)}, bf16[192,1536]{1,0:T(8,128)(2,1)}, u32[]{:S(2)}, u32[]{:S(2)}) collective-permute-start(bf16[192,1536]{1,0:T(8,128)(2,1)} %collective-permute-done.11.rest_7_), channel_id=1, source_target_pairs={{0,1},{1,0},{2,3},{3,2},{4,5},{5,4},{6,7},{7,6},{8,9},{9,8},{10,11... | collective-permute-start | bytes 1769480 | tf_op jit(solution)/shard_map/ppermute | solution.py:700
  126.3 29.7 %collective-permute-start.24 = (bf16[768,1536]{1,0:T(8,128)(2,1)}, bf16[768,1536]{1,0:T(8,128)(2,1)}, u32[]{:S(2)}, u32[]{:S(2)}) collective-permute-start(bf16[768,1536]{1,0:T(8,128)(2,1)} %get-tuple-element.147), channel_id=1, source_target_pairs={{0,1},{1,0},{2,3},{3,2},{4,5},{5,4},{6,7},{7,6},{8,9},{9,8},{10,11... | collective-permute-start | bytes 7077896 | tf_op jit(solution)/shard_map/ppermute | solution.py:700
  155.8 7.2 %collective-permute-start.23 = (bf16[768,1536]{1,0:T(8,128)(2,1)}, bf16[768,1536]{1,0:T(8,128)(2,1)S(1)}, u32[]{:S(2)}, u32[]{:S(2)}) collective-permute-start(bf16[768,1536]{1,0:T(8,128)(2,1)} %get-tuple-element.146), channel_id=1, source_target_pairs={{0,1},{1,0},{2,3},{3,2},{4,5},{5,4},{6,7},{7,6},{8,9},{9,8},{10,11... | collective-permute-start | bytes 7077896 | tf_op jit(solution)/shard_map/ppermute | solution.py:700
  156.0 7.0 %copy-start.4 = (bf16[768,1536]{1,0:T(8,128)(2,1)S(1)}, bf16[768,1536]{1,0:T(8,128)(2,1)}, u32[]{:S(2)}) copy-start(bf16[768,1536]{1,0:T(8,128)(2,1)} %get-tuple-element.145) | copy-start | bytes 7077892
  159.5 50.7 %collective-permute-start.25 = (bf16[192,1536]{1,0:T(8,128)(2,1)}, bf16[192,1536]{1,0:T(8,128)(2,1)}, u32[]{:S(2)}, u32[]{:S(2)}) collective-permute-start(bf16[192,1536]{1,0:T(8,128)(2,1)} %get-tuple-element.197), channel_id=1, source_target_pairs={{0,2},{1,3},{2,0},{3,1},{4,6},{5,7},{6,4},{7,5},{8,10},{9,11},{10,... | collective-permute-start | bytes 1769480 | tf_op jit(solution)/shard_map/ppermute | solution.py:704
  160.9 49.4 %collective-permute-start.26 = (bf16[192,1536]{1,0:T(8,128)(2,1)}, bf16[192,1536]{1,0:T(8,128)(2,1)}, u32[]{:S(2)}, u32[]{:S(2)}) collective-permute-start(bf16[192,1536]{1,0:T(8,128)(2,1)} %get-tuple-element.196), channel_id=1, source_target_pairs={{0,4},{4,0},{8,12},{12,8},{16,20},{20,16},{24,28},{28,24},{1,5},{5... | collective-permute-start | bytes 1769480 | tf_op jit(solution)/shard_map/ppermute | solution.py:706
  161.5 48.8 %collective-permute-start.27 = (bf16[192,1536]{1,0:T(8,128)(2,1)}, bf16[192,1536]{1,0:T(8,128)(2,1)}, u32[]{:S(2)}, u32[]{:S(2)}) collective-permute-start(bf16[192,1536]{1,0:T(8,128)(2,1)} %get-tuple-element.195), channel_id=1, source_target_pairs={{0,6},{1,7},{2,4},{3,5},{4,2},{5,3},{6,0},{7,1},{8,14},{9,15},{10,... | collective-permute-start | bytes 1769480 | tf_op jit(solution)/shard_map/ppermute | solution.py:708
  165.0 49.4 %all-to-all-start.2 = ((bf16[4,192,1536]{2,1,0:T(8,128)(2,1)}), bf16[4,192,1536]{2,1,0:T(8,128)(2,1)}, u32[]{:S(2)}, u32[]{:S(2)}) async-start(bf16[4,192,1536]{2,1,0:T(8,128)(2,1)} %bitcast.22), calls=%async_computation.2 | async-start | bytes 4718592 | tf_op jit(solution)/shard_map/all_to_all | solution.py:741
  214.4 5.4 %collective-permute-start.28 = (bf16[768,1664]{1,0:T(8,128)(2,1)}, bf16[768,1664]{1,0:T(8,128)(2,1)S(1)}, u32[]{:S(2)}, u32[]{:S(2)}) collective-permute-start(bf16[768,1664]{1,0:T(8,128)(2,1)} %get-tuple-element.172), channel_id=1, source_target_pairs={{0,1},{1,0},{2,3},{3,2},{4,5},{5,4},{6,7},{7,6},{8,9},{9,8},{10,11... | collective-permute-start | bytes 7667720 | tf_op jit(solution)/shard_map/ppermute | solution.py:700
  216.3 3.5 %copy-start.2 = (bf16[768,1664]{1,0:T(8,128)(2,1)S(1)}, bf16[768,1664]{1,0:T(8,128)(2,1)}, u32[]{:S(2)}) copy-start(bf16[768,1664]{1,0:T(8,128)(2,1)} %get-tuple-element.171) | copy-start | bytes 7667716
  221.8 38.7 %all-to-all-start.3 = ((bf16[8,24,3072]{2,1,0:T(8,128)(2,1)}), bf16[8,24,3072]{2,1,0:T(8,128)(2,1)}, u32[]{:S(2)}, u32[]{:S(2)}) async-start(bf16[8,24,3072]{2,1,0:T(8,128)(2,1)} %bitcast.24), calls=%async_computation.3 | async-start | bytes 2359296 | tf_op jit(solution)/shard_map/all_to_all | solution.py:711
  226.2 31.3 %collective-permute-start.29 = (bf16[192,1664]{1,0:T(8,128)(2,1)}, bf16[192,1664]{1,0:T(8,128)(2,1)}, u32[]{:S(2)}, u32[]{:S(2)}) collective-permute-start(bf16[192,1664]{1,0:T(8,128)(2,1)} %get-tuple-element.179), channel_id=1, source_target_pairs={{0,2},{1,3},{2,0},{3,1},{4,6},{5,7},{6,4},{7,5},{8,10},{9,11},{10,... | collective-permute-start | bytes 1916936 | tf_op jit(solution)/shard_map/ppermute | solution.py:704
  226.8 30.8 %collective-permute-start.30 = (bf16[192,1664]{1,0:T(8,128)(2,1)}, bf16[192,1664]{1,0:T(8,128)(2,1)}, u32[]{:S(2)}, u32[]{:S(2)}) collective-permute-start(bf16[192,1664]{1,0:T(8,128)(2,1)} %get-tuple-element.180), channel_id=1, source_target_pairs={{0,4},{4,0},{8,12},{12,8},{16,20},{20,16},{24,28},{28,24},{1,5},{5... | collective-permute-start | bytes 1916936 | tf_op jit(solution)/shard_map/ppermute | solution.py:706
  228.0 29.6 %collective-permute-start.31 = (bf16[192,1664]{1,0:T(8,128)(2,1)}, bf16[192,1664]{1,0:T(8,128)(2,1)}, u32[]{:S(2)}, u32[]{:S(2)}) collective-permute-start(bf16[192,1664]{1,0:T(8,128)(2,1)} %get-tuple-element.181), channel_id=1, source_target_pairs={{0,6},{1,7},{2,4},{3,5},{4,2},{5,3},{6,0},{7,1},{8,14},{9,15},{10,... | collective-permute-start | bytes 1916936 | tf_op jit(solution)/shard_map/ppermute | solution.py:708
  260.4 25.2 %all-to-all-start.4 = ((bf16[8,24,1664]{2,1,0:T(8,128)(2,1)}), bf16[8,24,1664]{2,1,0:T(8,128)(2,1)}, u32[]{:S(2)}, u32[]{:S(2)}) async-start(bf16[8,24,1664]{2,1,0:T(8,128)(2,1)} %bitcast.26), calls=%async_computation.4 | async-start | bytes 1277952 | tf_op jit(solution)/shard_map/all_to_all | solution.py:711
  (6 other events, 11.8 us)
